TPU v7x, 32 devices: a whole 2x2x4 slice. The times are simulated.
32 devices in a mesh: clip: 4 (over y, core), sess: 8 (over z, x).
Axes of the slice: x: 2, y: 2, z: 4, core: 2. Of those that a mesh axis runs over, the one named last changes fastest.
Arguments:
- video: bfloat16 [32, 8, 2304], P('clip', 'sess'), may hold values from -6 to 6
- responses: bfloat16 [32, 8, 4096], P('clip', 'sess'), may hold values from 0 to 0.5
- assignment: int32 [32], P('clip'), may hold values from 0 to 7, as said below
- counts: int32 [8], P('sess'), may hold values from 1024 to 4096, as said below
- conv_weight: bfloat16 [64, 147], replicated, may hold values from -0.5 to 0.5
- conv_bias: float32 [64], replicated, may hold values from -3 to 3
- mix_weight: bfloat16 [64, 64], replicated, may hold values from -0.75 to 0.75
- mix_bias: float32 [64], replicated, may hold values from -3 to 3
- masks: bfloat16 [8, 4096, 576], P('sess'), may hold values from -0.25 to 0.25
- feat_w: bfloat16 [8, 4096, 64], P('sess'), may hold values from -0.75 to 0.75
- readout_bias: float32 [8, 4096], P('sess'), may hold values from -1 to 1
Outputs:
- loss: float32 [], replicated
- grad_conv_weight: float32 [64, 147], replicated
- grad_conv_bias: float32 [64], replicated
- grad_mix_weight: float32 [64, 64], replicated
- grad_mix_bias: float32 [64], replicated
- grad_masks: float32 [8, 4096, 576], P('sess', 'clip')
- grad_feat_w: float32 [8, 4096, 64], P('sess', 'clip')
- grad_readout_bias: float32 [8, 4096], P('sess', 'clip')
Inputs may be any that keep to these rules, and one draw needn't show every extreme that they name: `assignment`: in every aligned block of 8 clips, each of the 8 sessions is named by exactly one clip. `counts`: some session has exactly 4096 neurons.
All inputs are finite; a program needn't handle non-finite values.
Results may differ from a plain program's by a relative error of at most 0.0085.
Values may be sent and summed in bfloat16 or wider, within the bound.
No kernel may reach another device: no remote copies, remote signals or barrier semaphores. Data moves between devices by JAX's collectives and lax.ppermute only.
A program may use at most 192 MiB of HBM per device.

v0:
```python
import functools

import jax
import jax.numpy as jnp
import numpy as np
from jax import lax
from jax.experimental import pallas as pl
from jax.experimental.pallas import tpu as pltpu
from jax.sharding import PartitionSpec as P

HH = 36
WW = 64
KS = 7
KT = 3
DX = 8
PACK = 256
SEG = 64
BF = jnp.bfloat16
F32 = jnp.float32
NT = (((1,), (1,)), ((), ()))
TN = (((0,), (0,)), ((), ()))


def dot(a, b, dims=(((1,), (0,)), ((), ())), precision=None):
    return lax.dot_general(a, b, dims, precision=precision, preferred_element_type=F32)


def iota(shape, axis):
    return lax.broadcasted_iota(jnp.int32, shape, axis)


def tap_table(frames):
    table = np.zeros((PACK, KS, DX, frames), np.float32)
    for dt in range(KT):
        for dy in range(KS):
            for dx in range(KS):
                table[dt * KS * KS + dy * KS + dx, dy, dx, :] = 1.0
    table[KT * KS * KS, 0, KS, 0] = 1.0
    return table.reshape(PACK, -1).astype(jnp.bfloat16)


def pool_table():
    table = np.zeros((4, 2, WW // 2, 2, 4, WW // 2), np.float32)
    for pair in range(4):
        for col in range(WW // 2):
            table[pair, :, col, :, pair, col] = 0.25
    return table.reshape(8 * WW, 2 * WW).astype(jnp.bfloat16)


def pixel_chunks(pix):
    step = 8 * WW
    return [(p, min(step, pix - p)) for p in range(0, pix, step)]


def mix_blocks(mix, group):
    channels = mix.shape[0]
    size = channels * group
    wide = jnp.concatenate([mix.astype(F32)] * group, axis=1)
    tall = jnp.concatenate([wide] * group, axis=0)
    same = (iota((size, size), 0) // channels) == (iota((size, size), 1) // channels)
    return jnp.where(same, tall, 0.0).astype(BF)


def core_forward_kernel(recv, weight, cbias, mix, mbias, table, pool, pay, act1, slope1, slope2, xcol, pre, feats, wbig):
    frames = recv.shape[0]
    rows, pix = act1.shape
    channels = mix.shape[0]
    neurons = recv.shape[1] - pix
    group = max(1, 256 // channels)
    patch_cols = xcol.shape[0]
    video = recv[:, neurons:].astype(F32)
    lane = iota((frames, pix), 1)
    col = lane % WW
    row = lane // WW
    per_store = max(1, 16 // frames)
    for dx0 in range(0, DX, per_store):
        shifted = []
        for dx in range(dx0, dx0 + per_store):
            s = dx - KS // 2
            if dx == KS:
                shifted.append(None)
            elif s == 0:
                shifted.append(video)
            else:
                rolled = pltpu.roll(video, (-s) % pix, 1)
                shifted.append(jnp.where((col + s >= 0) & (col + s < WW), rolled, 0.0))
        for dy in range(KS):
            t = dy - KS // 2
            parts = []
            for item in shifted:
                if item is None:
                    parts.append(jnp.ones((frames, pix), F32))
                elif t == 0:
                    parts.append(item)
                else:
                    moved = pltpu.roll(item, (-t * WW) % pix, 1)
                    parts.append(jnp.where((row + t >= 0) & (row + t < HH), moved, 0.0))
            base = (dy * DX + dx0) * frames
            block = parts[0] if len(parts) == 1 else jnp.concatenate(parts, axis=0)
            xcol[base : base + per_store * frames, :] = block.astype(BF)
    taps = weight.shape[1]
    tap = iota((channels, taps), 1)
    weights = weight[...].astype(F32)
    split = [
        jnp.where((tap >= dt * KS * KS) & (tap < (dt + 1) * KS * KS), weights, 0.0).astype(BF)
        for dt in range(KT)
    ]
    spread = dot(jnp.concatenate(split, axis=0), table[0:taps, :])
    source = iota((channels, patch_cols), 1) % frames
    for f in range(frames):
        total = jnp.zeros((channels, patch_cols), F32)
        for dt in range(KT):
            total = total + jnp.where(source == f + dt - 1, spread[dt * channels : (dt + 1) * channels], 0.0)
        wbig[f * channels : (f + 1) * channels, :] = total.astype(BF)
    wide = wbig[...]
    for p, size in pixel_chunks(pix):
        pre[:, p : p + size] = dot(wide, xcol[:, p : p + size])

    per_frame = channels // 16

    def first(i, carry):
        r = pl.multiple_of(i * 16, 16)
        b = pl.multiple_of((i % per_frame) * 16, 16)
        x = pre[pl.ds(r, 16), :] + cbias[pl.ds(b, 16), :]
        e = jnp.exp(jnp.minimum(x, 0.0))
        act1[pl.ds(r, 16), :] = (jnp.maximum(x, 0.0) + (e - 1.0)).astype(BF)
        slope1[pl.ds(r, 16), :] = e.astype(BF)
        return carry

    lax.fori_loop(0, rows // 16, first, 0)
    blocks = mix_blocks(mix[...], group)
    span = channels * group
    for r in range(0, rows, span):
        for p, size in pixel_chunks(pix):
            pre[r : r + span, p : p + size] = dot(blocks, act1[r : r + span, p : p + size])

    def second(i, carry):
        r = pl.multiple_of(i * 16, 16)
        b = pl.multiple_of((i % per_frame) * 16, 16)
        x = pre[pl.ds(r, 16), :] + mbias[pl.ds(b, 16), :]
        e = jnp.exp(jnp.minimum(x, 0.0))
        feats[pl.ds(r, 16), :] = (jnp.maximum(x, 0.0) + (e - 1.0)).astype(BF)
        slope2[pl.ds(r, 16), :] = e.astype(BF)
        return carry

    lax.fori_loop(0, rows // 16, second, 0)
    half = 2 * WW
    chunks = pixel_chunks(pix)
    for p, size in chunks[:-1]:
        pay[:, p // 4 : p // 4 + half] = dot(feats[:, p : p + size], pool[...]).astype(BF)
    p, size = chunks[-1]
    tail = dot(feats[:, p : p + size], pool[0:size, :])
    pieces = []
    for t in range(neurons // half):
        tile = recv[:, t * half : (t + 1) * half].astype(F32)
        pieces += [pltpu.roll(tile, SEG, 1), tile]
    packed = jnp.concatenate(pieces, axis=0)
    pay[:, p // 4 : p // 4 + half] = jnp.where(iota((rows, half), 1) < SEG, tail, packed).astype(BF)


def drive_terms(projected, target, w, rbias, alive, scale, channels):
    frames = target.shape[0]
    sums = [
        jnp.sum(projected[f * channels : (f + 1) * channels] * w, axis=0, keepdims=True)
        for f in range(frames)
    ]
    drive = jnp.concatenate(sums, axis=0) + rbias
    e = jnp.exp(-jnp.abs(drive))
    rate = jnp.maximum(drive, 0.0) + jnp.log(1.0 + e) + 0.1
    sig = jnp.where(drive >= 0, 1.0, e) / (1.0 + e)
    grad = jnp.where(alive, (1.0 - target / rate) * sig, 0.0) * scale
    return rate, grad


def mixed_rows(grad, w):
    frames = grad.shape[0]
    return jnp.concatenate([grad[f : f + 1] * w for f in range(frames)], axis=0).astype(BF)


def readout_kernel(scale, count, recv, pay, mask, wt, rbias, pooled_grad, loss, acc, loss_acc):
    i = pl.program_id(0)
    block = mask.shape[1]
    pooled_n = mask.shape[2]
    channels = wt.shape[0]
    frames = recv.shape[0]

    @pl.when(i == 0)
    def _():
        acc[...] = jnp.zeros_like(acc)
        loss_acc[...] = jnp.zeros_like(loss_acc)

    w = wt[...].astype(F32)
    m = mask[0]
    projected = dot(pay[:, 0:pooled_n], m, NT)
    target = recv[...].astype(F32)
    alive = (i * block + iota((frames, block), 1)) < count[0]
    rate, grad = drive_terms(projected, target, w, rbias[...], alive, scale, channels)
    loss_acc[...] += jnp.where(alive, rate - target * jnp.log(rate), 0.0)
    acc[...] += dot(mixed_rows(grad, w), m)

    @pl.when(i == pl.num_programs(0) - 1)
    def _():
        pooled_grad[...] = acc[...].astype(BF)
        loss[...] = jnp.broadcast_to(jnp.sum(loss_acc[...], keepdims=True) * scale, loss.shape)


def core_backward_kernel(pooled_grad, loss, act1, slope1, slope2, xcol, mix, table, unpool, out, grad, g2, g1):
    rows, pix = act1.shape
    channels = mix.shape[0]
    frames = rows // channels
    group = max(1, 256 // channels)
    span = channels * group
    patch_cols = xcol.shape[0]
    per_frame = channels // 16
    for p, size in pixel_chunks(pix):
        grad[:, p : p + size] = dot(pooled_grad[:, p // 4 : (p + size) // 4], unpool[0 : size // 4, 0:size])

    sums = []
    for q in range(per_frame):

        def second(f, total):
            r = pl.multiple_of(f * channels + q * 16, 16)
            g = (grad[pl.ds(r, 16), :] * slope2[pl.ds(r, 16), :].astype(F32)).astype(BF)
            g2[pl.ds(r, 16), :] = g
            return total + jnp.sum(g.astype(F32), axis=1, keepdims=True)

        sums.append(lax.fori_loop(0, frames, second, jnp.zeros((16, 1), F32)))
    mix_bias_grad = jnp.concatenate(sums, axis=0)
    blocks = mix_blocks(mix[...], group)
    mix_grad = jnp.zeros((channels, span), F32)
    same = (iota((span, span), 0) // channels) == (iota((span, span), 1) // channels)
    for r in range(0, rows, span):
        full = jnp.where(same, dot(g2[r : r + span, :], act1[r : r + span, :], NT), 0.0)
        for a in range(group):
            mix_grad = mix_grad + full[a * channels : (a + 1) * channels]
        for p, size in pixel_chunks(pix):
            grad[r : r + span, p : p + size] = dot(blocks, g2[r : r + span, p : p + size], TN)
    half = 2 * channels
    folded = mix_grad[:, 0:half]
    for k in range(half, span, half):
        folded = folded + mix_grad[:, k : k + half]
    folded = folded + pltpu.roll(folded, channels, 1)

    def first(i, carry):
        r = pl.multiple_of(i * 16, 16)
        g1[pl.ds(r, 16), :] = (grad[pl.ds(r, 16), :] * slope1[pl.ds(r, 16), :].astype(F32)).astype(BF)
        return carry

    lax.fori_loop(0, rows // 16, first, 0)
    full = dot(g1[...], xcol[...], NT)
    source = iota((channels, patch_cols), 1) % frames
    parts = [jnp.zeros((channels, patch_cols), F32) for _ in range(KT + 1)]
    for f in range(frames):
        piece = full[f * channels : (f + 1) * channels]
        for dt in range(KT):
            parts[dt] = parts[dt] + jnp.where(source == f + dt - 1, piece, 0.0)
        parts[KT] = parts[KT] + piece
    taps = dot(
        jnp.concatenate(parts, axis=0), table[...].astype(F32), NT, precision=lax.Precision.HIGHEST
    )
    lane = iota((channels, PACK), 1)
    conv = jnp.zeros((channels, PACK), F32)
    for dt in range(KT + 1):
        inside = (lane >= dt * KS * KS) & (lane < (dt + 1) * KS * KS)
        conv = conv + jnp.where(inside, taps[dt * channels : (dt + 1) * channels], 0.0)
    used = KT * KS * KS + 1
    low = lane[:, 0:128]
    out[:, 0:128] = conv[:, 0:128]
    upper = jnp.where(low < used - 128, conv[:, 128:256], 0.0)
    upper = jnp.where(low == used - 128, mix_bias_grad, upper)
    upper = jnp.where((low == used - 127) & (iota((channels, 128), 0) == 0), loss[0:1, 0:1], upper)
    out[:, 128:256] = jnp.where(low >= channels, folded, upper)


def owned_rows_kernel(scale, where, count, *refs):
    clips = len(refs) - 6
    pays = refs[:clips]
    mask, wt, rbias, mask_grad, feat_grad, bias_grad = refs[clips:]
    i = pl.program_id(0)
    block = mask.shape[1]
    pooled_n = mask.shape[2]
    channels = wt.shape[0]
    frames = pays[0].shape[0] // channels
    first = (where[0] * pl.num_programs(0) + i) * block
    m = mask[0]
    w = wt[...].astype(F32)
    alive = (first + iota((frames, block), 1)) < count[0]
    total = None
    feat = jnp.zeros((channels, block), F32)
    bias = jnp.zeros((frames, block), F32)
    segs = block // SEG
    base = pl.multiple_of(first // SEG * frames, segs * frames)
    low = iota((frames, 128), 1) < SEG
    for pay in pays:
        pooled = pay[:, 0:pooled_n]
        held = pay[pl.ds(base, segs * frames), pooled_n - SEG : pooled_n + SEG].astype(F32)
        tiles = []
        for j in range(0, segs, 2):
            even = held[j * frames : (j + 1) * frames]
            odd = held[(j + 1) * frames : (j + 2) * frames]
            tiles.append(jnp.where(low, pltpu.roll(even, SEG, 1), odd))
        target = jnp.concatenate(tiles, axis=1)
        projected = dot(pooled, m, NT)
        _, grad = drive_terms(projected, target, w, rbias[...], alive, scale, channels)
        for f in range(frames):
            feat = feat + grad[f : f + 1] * projected[f * channels : (f + 1) * channels]
        bias = bias + grad
        part = dot(mixed_rows(grad, w), pooled, TN)
        total = part if total is None else total + part
    mask_grad[0] = total
    feat_grad[0] = feat.T
    bias_grad[...] = jnp.sum(bias, axis=0, keepdims=True)


def params(limit=48):
    return pltpu.CompilerParams(vmem_limit_bytes=limit << 20)


def xor_pairs(size, mask):
    return [(i, i ^ mask) for i in range(size)]


def per_device(
    video, responses, assignment, counts, conv_weight, conv_bias, mix_weight, mix_bias, masks, feat_w, readout_bias
):
    sess_total = lax.axis_size("sess")
    clip_total = lax.axis_size("clip")
    total = sess_total * clip_total
    clip_block, frame_block, pix = video.shape
    neurons = responses.shape[2]
    pooled_n = masks.shape[2]
    channels, taps = conv_weight.shape
    frames = frame_block * sess_total
    rows = frames * channels
    own = neurons // clip_total
    block = min(512, own)
    assert clip_block == sess_total and frame_block == 1 and masks.shape[0] == 1
    assert neurons == channels * SEG and pooled_n % 128 == SEG and pix == HH * WW
    scale = 1.0 / (clip_block * clip_total * frames)

    sessions = lax.broadcasted_iota(jnp.int32, (sess_total, clip_block), 0)
    pick = (sessions == assignment[None, :]).astype(BF)
    both = jnp.concatenate([responses[:, 0, :], video[:, 0, :]], axis=1)
    send = jnp.dot(pick, both, preferred_element_type=F32).astype(BF)
    recv = lax.all_to_all(send, "sess", split_axis=0, concat_axis=0, tiled=True)

    table = jnp.asarray(tap_table(frames))
    pool = jnp.asarray(pool_table())
    unpool = jnp.asarray(pool_table().T)
    wt = feat_w[0].T
    patch_cols = KS * DX * frames
    width = pooled_n + SEG
    pay, act1, slope1, slope2, xcol = pl.pallas_call(
        core_forward_kernel,
        out_shape=(
            jax.ShapeDtypeStruct((rows, width), BF),
            jax.ShapeDtypeStruct((rows, pix), BF),
            jax.ShapeDtypeStruct((rows, pix), BF),
            jax.ShapeDtypeStruct((rows, pix), BF),
            jax.ShapeDtypeStruct((patch_cols, pix), BF),
        ),
        scratch_shapes=[
            pltpu.VMEM((rows, pix), F32),
            pltpu.VMEM((rows, pix), BF),
            pltpu.VMEM((rows, patch_cols), BF),
        ],
        compiler_params=params(),
        name="core_forward",
    )(recv, conv_weight, conv_bias[:, None], mix_weight, mix_bias[:, None], table, pool)

    pays = [pay]
    for mask in range(1, clip_total):
        if mask % 2 == 0 or mask == 1:
            pays.append(lax.ppermute(pay, "clip", xor_pairs(clip_total, mask)))
        else:
            pays.append(lax.ppermute(pays[mask - 1], "clip", xor_pairs(clip_total, 1)))

    smem = pl.BlockSpec(memory_space=pltpu.SMEM)
    big = min(512, neurons)
    pooled_grad, loss = pl.pallas_call(
        functools.partial(readout_kernel, scale),
        grid=(neurons // big,),
        in_specs=[
            smem,
            pl.BlockSpec((frames, big), lambda i: (0, i)),
            pl.BlockSpec((rows, width), lambda i: (0, 0)),
            pl.BlockSpec((1, big, pooled_n), lambda i: (0, i, 0)),
            pl.BlockSpec((channels, big), lambda i: (0, i)),
            pl.BlockSpec((1, big), lambda i: (0, i)),
        ],
        out_specs=(
            pl.BlockSpec((rows, pooled_n), lambda i: (0, 0)),
            pl.BlockSpec((8, 128), lambda i: (0, 0)),
        ),
        out_shape=(jax.ShapeDtypeStruct((rows, pooled_n), BF), jax.ShapeDtypeStruct((8, 128), F32)),
        scratch_shapes=[pltpu.VMEM((rows, pooled_n), F32), pltpu.VMEM((frames, big), F32)],
        compiler_params=params(),
        name="readout",
    )(counts, recv, pay, masks, wt, readout_bias)

    core = pl.pallas_call(
        core_backward_kernel,
        out_shape=jax.ShapeDtypeStruct((channels, PACK), F32),
        scratch_shapes=[
            pltpu.VMEM((rows, pix), F32),
            pltpu.VMEM((rows, pix), BF),
            pltpu.VMEM((rows, pix), BF),
        ],
        compiler_params=params(),
        name="core_backward",
    )(pooled_grad, loss, act1, slope1, slope2, xcol, mix_weight, table, unpool)

    axes = ("clip", "sess")
    flat = core.reshape(total, -1)
    mine = jnp.sum(lax.all_to_all(flat, axes, split_axis=0, concat_axis=0, tiled=True), axis=0)
    copies = jnp.broadcast_to(mine[None], (total, mine.shape[0]))
    summed = lax.all_to_all(copies, axes, split_axis=0, concat_axis=0, tiled=True).reshape(channels, PACK)

    where = lax.axis_index("clip").astype(jnp.int32)[None]
    steps = own // block
    grad_masks, grad_feat, grad_rbias = pl.pallas_call(
        functools.partial(owned_rows_kernel, scale),
        grid_spec=pltpu.PrefetchScalarGridSpec(
            num_scalar_prefetch=1,
            grid=(steps,),
            in_specs=[smem]
            + [pl.BlockSpec((rows, width), lambda i, at: (0, 0)) for _ in pays]
            + [
                pl.BlockSpec((1, block, pooled_n), lambda i, at: (0, at[0] * steps + i, 0)),
                pl.BlockSpec((channels, block), lambda i, at: (0, at[0] * steps + i)),
                pl.BlockSpec((1, block), lambda i, at: (0, at[0] * steps + i)),
            ],
            out_specs=(
                pl.BlockSpec((1, block, pooled_n), lambda i, at: (0, i, 0)),
                pl.BlockSpec((1, block, channels), lambda i, at: (0, i, 0)),
                pl.BlockSpec((1, block), lambda i, at: (0, i)),
            ),
        ),
        out_shape=(
            jax.ShapeDtypeStruct((1, own, pooled_n), F32),
            jax.ShapeDtypeStruct((1, own, channels), F32),
            jax.ShapeDtypeStruct((1, own), F32),
        ),
        compiler_params=params(),
        name="owned_rows",
    )(where, counts, *pays, masks, wt, readout_bias)

    used = taps + 1
    return (
        summed[0, used + 1],
        summed[:, :taps],
        summed[:, taps],
        summed[:, PACK - channels :],
        summed[:, used],
        grad_masks,
        grad_feat,
        grad_rbias,
    )


def solution(mesh):
    return jax.shard_map(
        per_device,
        mesh=mesh,
        in_specs=(
            P("clip", "sess", None),
            P("clip", "sess", None),
            P("clip"),
            P("sess"),
            P(),
            P(),
            P(),
            P(),
            P("sess", None, None),
            P("sess", None, None),
            P("sess", None),
        ),
        out_specs=(
            P(),
            P(),
            P(),
            P(),
            P(),
            P("sess", "clip", None),
            P("sess", "clip", None),
            P("sess", "clip"),
        ),
        check_vma=False,
    )
```

profile of v0, /device:TPU:0, one launch (start us, length us, event | category | flops | bytes accessed | tf_op | source)
XLA Modules:
  0.0 122.5 jit_solution(4926919974629115022)
XLA Ops:
  0.6 1.0 fusion
  1.7 0.5 broadcast.7
  2.2 0.7 reduce.6
  2.9 0.7 reshape.37
  3.5 7.3 %all-to-all-start = ((bf16[8,2,3200]{2,1,0:T(2,128)(2,1)}), bf16[8,2,3200]{2,1,0:T(2,128)(2,1)S(1)}, u32[]{:S(2)}, u32[]{:S(2)}) async-start(bf16[8,2,3200]{2,1,0:T(2,128)(2,1)} %reshape.37), calls=%async_computation | async-start | bytes 204800 | tf_op jit(solution)/shard_map/all_to_all | solution.py:345
  10.8 0.7 copy.43.cbias
  11.6 0.7 copy.44.mbias
  12.3 5.7 %all-to-all-done = bf16[8,2,3200]{2,1,0:T(2,128)(2,1)S(1)} async-done(((bf16[8,2,3200]{2,1,0:T(2,128)(2,1)}), bf16[8,2,3200]{2,1,0:T(2,128)(2,1)S(1)}, u32[]{:S(2)}, u32[]{:S(2)}) %all-to-all-start) | async-done | bytes 102432 | tf_op jit(solution)/shard_map/all_to_all | solution.py:345
  18.0 0.1 reshape.38
  18.1 0.0 copy-start.5
  18.1 0.0 copy-start.3
  18.1 1.0 copy-done.3
  19.1 0.9 copy-done.9
  20.0 0.7 copy-done.11
  20.7 0.8 copy-done.13
  21.5 12.4 %core_forward.1 = (bf16[512,640]{1,0:T(8,128)(2,1)S(1)}, bf16[512,2304]{1,0:T(8,128)(2,1)S(1)}, bf16[512,2304]{1,0:T(8,128)(2,1)}, bf16[512,2304]{1,0:T(8,128)(2,1)}, bf16[448,2304]{1,0:T(8,128)(2,1)S(1)}) custom-call(bf16[8,6400]{1,0:T(8,128)(2,1)S(1)} %bitcast.17, bf16[64,147]{1,0:T(8,128)(2,1)S(1)} %copy-done.13, f32[64,1]{1,0:T(8,128)S(1)} %copy.43.cbias, ...), custom_call_target="tpu_custom_call" | custom-call | tf_op jit(solution)/shard_map/core_forward/pallas_call | solution.py:353
  33.8 1.4 %copy-done.1 = bf16[448,2304]{1,0:T(8,128)(2,1)} copy-done((bf16[448,2304]{1,0:T(8,128)(2,1)}, bf16[448,2304]{1,0:T(8,128)(2,1)S(1)}, u32[]{:S(2)}) %copy-start.1) | copy-done | bytes 2064408
  35.3 1.5 %collective-permute-start.1 = (bf16[512,640]{1,0:T(8,128)(2,1)S(1)}, bf16[512,640]{1,0:T(8,128)(2,1)}, u32[]{:S(2)}, u32[]{:S(2)}) collective-permute-start(bf16[512,640]{1,0:T(8,128)(2,1)S(1)} %get-tuple-element.18.pay.refs_0_), channel_id=1, source_target_pairs={{0,16},{8,24},{16,0},{24,8},{1,17},{9,25},{17,1},{25,9},{2,18},{10... | collective-permute-start | bytes 1966088 | tf_op jit(solution)/shard_map/ppermute | solution.py:374
  36.8 0.0 collective-permute-start
  36.8 13.7 %collective-permute-done.1.refs_2_ = bf16[512,640]{1,0:T(8,128)(2,1)} collective-permute-done((bf16[512,640]{1,0:T(8,128)(2,1)S(1)}, bf16[512,640]{1,0:T(8,128)(2,1)}, u32[]{:S(2)}, u32[]{:S(2)}) %collective-permute-start.1) | collective-permute-done | bytes 655392 | tf_op jit(solution)/shard_map/ppermute | solution.py:374
  50.5 0.0 copy-done.5
  50.5 0.0 collective-permute-start.2
  50.5 7.6 %copy.45.mask.refs_4_ = bf16[1,4096,576]{2,1,0:T(8,128)(2,1)} copy(bf16[1,4096,576]{1,2,0:T(8,128)(2,1)} %param.22) | data formatting | bytes 9437184 | tf_op args[8]
  58.8 0.0 copy-done
  58.8 0.0 copy-done.10
  58.8 0.0 copy-start.6
  58.8 0.9 copy-done.6
  59.7 11.3 %readout.1 = (bf16[512,576]{1,0:T(8,128)(2,1)S(1)}, f32[8,128]{1,0:T(8,128)S(1)}) custom-call(s32[1]{0:T(128)S(6)} %copy.54.count, bf16[8,6400]{1,0:T(8,128)(2,1)S(1)} %bitcast.18, bf16[512,640]{1,0:T(8,128)(2,1)S(1)} %get-tuple-element.18.pay.refs_0_, bf16[1,4096,576]{2,1,0:T(8,128)(2,1)} %copy.45.mask.refs_4_, bf16[64,4096]{1,0:T(8,128)(2,1)S(1)} %bitcast.15, ...), custom_call_target="tpu_custom_call" | custom-call | tf_op jit(solution)/shard_map/readout/pallas_call | solution.py:380
  71.0 0.0 copy-done.2
  71.0 11.4 %core_backward.1 = f32[64,256]{1,0:T(8,128)S(1)} custom-call(bf16[512,576]{1,0:T(8,128)(2,1)S(1)} %get-tuple-element.19.pooled_grad, f32[8,128]{1,0:T(8,128)S(1)} %get-tuple-element.20.loss, bf16[512,2304]{1,0:T(8,128)(2,1)S(1)} %get-tuple-element.21.act1, bf16[512,2304]{1,0:T(8,128)(2,1)} %get-tuple-element.22.slope1, ...), custom_call_target="tpu_custom_call" | custom-call | tf_op jit(solution)/shard_map/core_backward/pallas_call | solution.py:401
  82.4 0.0 copy-start.7
  82.4 0.6 copy-done.7
  83.1 0.9 all_to_all.23
  84.0 9.6 %all_to_all.27 = f32[32,1,512]{2,1,0:T(1,128)S(1)} all-to-all(f32[32,1,512]{2,1,0:T(1,128)S(1)} %all_to_all.23), channel_id=1, replica_groups=mesh['clip'=4,'sess'=8] {'clip','sess'}, dimensions={0} | all-to-all | bytes 131072 | tf_op jit(solution)/shard_map/all_to_all | solution.py:415
  93.5 0.1 reduce_sum.9
  93.6 0.7 broadcast_in_dim.18
  94.3 2.8 %all-to-all-start.2 = ((f32[32,1,512]{2,1,0:T(1,128)}), f32[32,1,512]{2,1,0:T(1,128)S(1)}, u32[]{:S(2)}, u32[]{:S(2)}) async-start(f32[32,1,512]{2,1,0:T(1,128)} %broadcast_in_dim.18), calls=%async_computation.2 | async-start | bytes 131072 | tf_op jit(solution)/shard_map/all_to_all | solution.py:417
  97.0 7.1 %all-to-all-done.2 = f32[32,1,512]{2,1,0:T(1,128)S(1)} async-done(((f32[32,1,512]{2,1,0:T(1,128)}), f32[32,1,512]{2,1,0:T(1,128)S(1)}, u32[]{:S(2)}, u32[]{:S(2)}) %all-to-all-start.2) | async-done | bytes 65568 | tf_op jit(solution)/shard_map/all_to_all | solution.py:417
  104.1 0.2 reduce.1
  104.3 0.0 copy-start.14
  104.3 0.7 slice.23
  105.0 0.6 slice.20
  105.6 0.7 slice_reduce_fusion
  106.3 0.0 collective-permute-done.refs_1_
  106.3 0.0 collective-permute-done.2.refs_3_
  106.3 12.2 %owned_rows.1 = (f32[1,1024,576]{2,1,0:T(8,128)}, f32[1,1024,64]{2,1,0:T(8,128)S(1)}, f32[1,1024]{1,0:T(1,128)}) custom-call(s32[1]{0:T(128)} %bitcast.8.where, s32[1]{0:T(128)S(6)} %copy.54.count, bf16[512,640]{1,0:T(8,128)(2,1)S(1)} %get-tuple-element.18.pay.refs_0_, bf16[512,640]{1,0:T(8,128)(2,1)} %collective-permute-done.refs_1_, ...), custom_call_target="tpu_custom_call" | custom-call | tf_op jit(solution)/shard_map/owned_rows/pallas_call | solution.py:421
  118.5 3.1 %copy.48 = f32[1,1024,576]{1,2,0:T(8,128)} copy(f32[1,1024,576]{2,1,0:T(8,128)} %get-tuple-element.57) | data formatting | bytes 4718592
  121.6 0.9 copy.49
  (16 shorter events, 0.1 us)
Async XLA Ops:
  3.5 14.4 %all-to-all-start = ((bf16[8,2,3200]{2,1,0:T(2,128)(2,1)}), bf16[8,2,3200]{2,1,0:T(2,128)(2,1)S(1)}, u32[]{:S(2)}, u32[]{:S(2)}) async-start(bf16[8,2,3200]{2,1,0:T(2,128)(2,1)} %reshape.37), calls=%async_computation | async-start | bytes 204800 | tf_op jit(solution)/shard_map/all_to_all | solution.py:345
  18.1 32.4 %copy-start.5 = (bf16[8,1,6400]{2,0,1:T(8,128)(2,1)}, bf16[8,1,6400]{2,0,1:T(8,128)(2,1)S(1)}, u32[]{:S(2)}) copy-start(bf16[8,1,6400]{2,0,1:T(8,128)(2,1)S(1)} %copy.52) | copy-start | bytes 307204
  18.1 1.0 copy-start.3
  19.1 0.9 copy-start.9
  20.0 0.7 copy-start.11
  20.7 0.8 copy-start.13
  33.8 1.4 %copy-start.1 = (bf16[448,2304]{1,0:T(8,128)(2,1)}, bf16[448,2304]{1,0:T(8,128)(2,1)S(1)}, u32[]{:S(2)}) copy-start(bf16[448,2304]{1,0:T(8,128)(2,1)S(1)} %get-tuple-element.24.xcol) | copy-start | bytes 6193156
  35.3 23.5 %copy-start = (bf16[1,4096,64]{1,2,0:T(8,128)(2,1)S(1)}, bf16[1,4096,64]{1,2,0:T(8,128)(2,1)}, u32[]{:S(2)}) copy-start(bf16[1,4096,64]{1,2,0:T(8,128)(2,1)} %param.23) | copy-start | bytes 1572868
  35.3 23.6 %copy-start.10 = (f32[1,4096]{1,0:T(1,128)S(1)}, f32[1,4096]{1,0:T(1,128)}, u32[]{:S(2)}) copy-start(f32[1,4096]{1,0:T(1,128)} %refs_6_.1) | copy-start | bytes 49156
  35.3 15.2 %collective-permute-start.1 = (bf16[512,640]{1,0:T(8,128)(2,1)S(1)}, bf16[512,640]{1,0:T(8,128)(2,1)}, u32[]{:S(2)}, u32[]{:S(2)}) collective-permute-start(bf16[512,640]{1,0:T(8,128)(2,1)S(1)} %get-tuple-element.18.pay.refs_0_), channel_id=1, source_target_pairs={{0,16},{8,24},{16,0},{24,8},{1,17},{9,25},{17,1},{25,9},{2,18},{10... | collective-permute-start | bytes 1966088 | tf_op jit(solution)/shard_map/ppermute | solution.py:374
  36.8 69.5 %collective-permute-start = (bf16[512,640]{1,0:T(8,128)(2,1)S(1)}, bf16[512,640]{1,0:T(8,128)(2,1)}, u32[]{:S(2)}, u32[]{:S(2)}) collective-permute-start(bf16[512,640]{1,0:T(8,128)(2,1)S(1)} %get-tuple-element.18.pay.refs_0_), channel_id=1, source_target_pairs={{0,8},{8,0},{16,24},{24,16},{1,9},{9,1},{17,25},{25,17},{2,10},{10... | collective-permute-start | bytes 1966088 | tf_op jit(solution)/shard_map/ppermute | solution.py:374
  50.5 55.8 %collective-permute-start.2 = (bf16[512,640]{1,0:T(8,128)(2,1)}, bf16[512,640]{1,0:T(8,128)(2,1)}, u32[]{:S(2)}, u32[]{:S(2)}) collective-permute-start(bf16[512,640]{1,0:T(8,128)(2,1)} %collective-permute-done.1.refs_2_), channel_id=1, source_target_pairs={{0,8},{8,0},{16,24},{24,16},{1,9},{9,1},{17,25},{25,17},{2,10},{10... | collective-permute-start | bytes 1966088 | tf_op jit(solution)/shard_map/ppermute | solution.py:376
  58.8 0.9 copy-start.6
  59.7 11.3 %copy-start.2 = (bf16[448,2304]{1,0:T(8,128)(2,1)S(1)}, bf16[448,2304]{1,0:T(8,128)(2,1)}, u32[]{:S(2)}) copy-start(bf16[448,2304]{1,0:T(8,128)(2,1)} %copy-done.1) | copy-start | bytes 6193156
  59.7 11.3 %copy-start.4 = (bf16[256,448]{1,0:T(8,128)(2,1)S(1)}, bf16[256,448]{1,0:T(8,128)(2,1)}, u32[]{:S(2)}) copy-start(bf16[256,448]{1,0:T(8,128)(2,1)} %constant.13.clone.table) | copy-start | bytes 688132
  59.7 11.3 %copy-start.8 = (bf16[128,512]{1,0:T(8,128)(2,1)S(1)}, bf16[128,512]{1,0:T(8,128)(2,1)}, u32[]{:S(2)}) copy-start(bf16[128,512]{1,0:T(8,128)(2,1)} %constant.15.clone.unpool) | copy-start | bytes 393220
  59.7 11.3 %copy-start.12 = (bf16[64,64]{1,0:T(8,128)(2,1)S(1)}, bf16[64,64]{1,0:T(8,128)(2,1)}, u32[]{:S(2)}) copy-start(bf16[64,64]{1,0:T(8,128)(2,1)} %mix.3) | copy-start | bytes 24580
  82.4 0.6 copy-start.7
  94.3 9.9 %all-to-all-start.2 = ((f32[32,1,512]{2,1,0:T(1,128)}), f32[32,1,512]{2,1,0:T(1,128)S(1)}, u32[]{:S(2)}, u32[]{:S(2)}) async-start(f32[32,1,512]{2,1,0:T(1,128)} %broadcast_in_dim.18), calls=%async_computation.2 | async-start | bytes 131072 | tf_op jit(solution)/shard_map/all_to_all | solution.py:417
  104.3 14.2 %copy-start.14 = (f32[64,256]{1,0:T(8,128)}, f32[64,256]{1,0:T(8,128)S(1)}, u32[]{:S(2)}) copy-start(f32[64,256]{1,0:T(8,128)S(1)} %reshape.33) | copy-start | bytes 196612
where the time goes:
time: 123 us
  Pallas kernels  47.2 us (38%)
  waiting for transfers between devices  26.5 us (22%)
  local copies, waits for them, and re-layouts  24.3 us (20%)
  starting transfers between devices  11.6 us (9%)
  blocking collectives  9.57 us (8%)
  between operations  1.47 us (1%)
    unnamed x36, local copies, waits for them, and re-layouts  18.7 us
    ppermute x2, waiting for transfers between devices, per_device(): pays.append(lax.ppermute(pay, 'clip', xor_pairs(clip_total, mask)))  13.7 us
    pallas_call x1, Pallas kernels, per_device(): pl.pallas_call(core_forward_kernel, out_shape=(jax.ShapeDtypeStruct((rows...  12.4 us
    pallas_call x1, Pallas kernels, per_device(): pl.pallas_call(functools.partial(owned_rows_kernel, scale), grid_spec=plt...  12.2 us
    pallas_call x1, Pallas kernels, per_device(): pl.pallas_call(core_backward_kernel, out_shape=jax.ShapeDtypeStruct((chan...  11.4 us
    pallas_call x1, Pallas kernels, per_device(): pl.pallas_call(functools.partial(readout_kernel, scale), grid=(neurons //...  11.3 us
    all_to_all x1, blocking collectives, per_device(): lax.all_to_all(flat, axes, split_axis=0, concat_axis=0, tiled=True)  9.57 us
    all_to_all x1, starting transfers between devices, per_device(): recv = lax.all_to_all(send, 'sess', split_axis=0, concat_axis=0, tiled=True)  7.28 us
  transfers between devices with their start and end apart: 5, of which 3 were waited for; matrix products, arithmetic and copies ran while one was open for 10% of the time, Pallas kernels for 18%

commit v1 on v0

v1 whole, which is shorter than its diff:
```python
import functools

import jax
import jax.numpy as jnp
from jax import lax
from jax.experimental import pallas as pl
from jax.experimental.pallas import tpu as pltpu
from jax.sharding import PartitionSpec as P

HH = 36
WW = 64
KS = 7
KT = 3
DX = 8
PACK = 256
SEG = 64
BF = jnp.bfloat16
F32 = jnp.float32
NT = (((1,), (1,)), ((), ()))
TN = (((0,), (0,)), ((), ()))


def dot(a, b, dims=(((1,), (0,)), ((), ())), precision=None):
    return lax.dot_general(a, b, dims, precision=precision, preferred_element_type=F32)


def iota(shape, axis):
    return lax.broadcasted_iota(jnp.int32, shape, axis)


def pixel_chunks(pix):
    step = 8 * WW
    return [(p, min(step, pix - p)) for p in range(0, pix, step)]


def bias_column(row):
    size = row.shape[1]
    return jnp.sum(jnp.where(iota((size, size), 0) == iota((size, size), 1), row, 0.0), axis=1, keepdims=True)


def select_kernel(assign, video, responses, out):
    owners, lines, width = out.shape
    clips, pix = video.shape
    neurons = responses.shape[1]
    pick = (iota((owners, clips), 0) == assign[...]).astype(BF)
    first = dot(pick, responses[...])
    second = dot(pick, video[...])
    rows = [first[:, p : p + width] for p in range(0, neurons, width)]
    for p in range(0, pix, width):
        piece = second[:, p : p + width]
        if piece.shape[1] < width:
            piece = jnp.concatenate([piece, jnp.zeros((owners, width - piece.shape[1]), F32)], axis=1)
        rows.append(piece)
    while len(rows) < lines:
        rows.append(jnp.zeros((owners, width), F32))
    out[...] = jnp.stack(rows, axis=1).astype(BF)


def prep_kernel(frames, weight, cbias, mix, mbias, wbig, blocks, blocks_t, bias, table, pool, unpool):
    channels, taps = weight.shape
    patch_cols = wbig.shape[1]
    group = blocks.shape[0] // channels
    t = iota(table.shape, 0)
    l = iota(table.shape, 1)
    dy = l // (DX * frames)
    dx = (l // frames) % DX
    place = dy * KS + dx
    hit = (t == place) | (t == place + KS * KS) | (t == place + 2 * KS * KS)
    last = (t == KT * KS * KS) & (l == KS * frames)
    table[...] = jnp.where(((dx < KS) & hit & (t < KT * KS * KS)) | last, 1.0, 0.0).astype(BF)
    r = iota(pool.shape, 0)
    c = iota(pool.shape, 1)
    target = (r // (2 * WW)) * (WW // 2) + (r % WW) // 2
    pool[...] = jnp.where(target == c, 0.25, 0.0).astype(BF)
    r = iota(unpool.shape, 1)
    c = iota(unpool.shape, 0)
    target = (r // (2 * WW)) * (WW // 2) + (r % WW) // 2
    unpool[...] = jnp.where(target == c, 0.25, 0.0).astype(BF)
    size = channels * group
    same = (iota((size, size), 0) // channels) == (iota((size, size), 1) // channels)
    square = mix[...].astype(F32)
    for ref, base in ((blocks, square), (blocks_t, square.T)):
        wide = jnp.concatenate([base] * group, axis=1)
        ref[...] = jnp.where(same, jnp.concatenate([wide] * group, axis=0), 0.0).astype(BF)
    lane = iota(bias.shape, 1)
    bias[...] = jnp.where(lane == 0, bias_column(cbias[...]), bias_column(mbias[...]))
    tap = iota((channels, taps), 1)
    weights = weight[...].astype(F32)
    split = [
        jnp.where((tap >= dt * KS * KS) & (tap < (dt + 1) * KS * KS), weights, 0.0).astype(BF)
        for dt in range(KT)
    ]
    spread = dot(jnp.concatenate(split, axis=0), table[0:taps, :])
    source = iota((channels, patch_cols), 1) % frames
    for f in range(frames):
        total = jnp.zeros((channels, patch_cols), F32)
        for dt in range(KT):
            total = total + jnp.where(source == f + dt - 1, spread[dt * channels : (dt + 1) * channels], 0.0)
        wbig[f * channels : (f + 1) * channels, :] = total.astype(BF)


def core_forward_kernel(recv, wbig, blocks, bias, pool, pay, target, act1, slope1, slope2, xcol, pre, feats):
    frames, _, width = recv.shape
    rows, pix = act1.shape
    channels = bias.shape[0]
    neurons = target.shape[1]
    span = blocks.shape[0]
    packet = recv[...].astype(F32)
    lines = [packet[:, j, :] for j in range((neurons + pix + width - 1) // width)]
    held = neurons // width
    for j in range(held):
        target[:, j * width : (j + 1) * width] = lines[j]
    video = jnp.concatenate(lines[held:], axis=1)[:, 0:pix]
    lane = iota((frames, pix), 1)
    col = lane % WW
    row = lane // WW
    per_store = max(1, 16 // frames)
    for dx0 in range(0, DX, per_store):
        shifted = []
        for dx in range(dx0, dx0 + per_store):
            s = dx - KS // 2
            if dx == KS:
                shifted.append(None)
            elif s == 0:
                shifted.append(video)
            else:
                rolled = pltpu.roll(video, (-s) % pix, 1)
                shifted.append(jnp.where((col + s >= 0) & (col + s < WW), rolled, 0.0))
        for dy in range(KS):
            t = dy - KS // 2
            parts = []
            for item in shifted:
                if item is None:
                    parts.append(jnp.ones((frames, pix), F32))
                elif t == 0:
                    parts.append(item)
                else:
                    moved = pltpu.roll(item, (-t * WW) % pix, 1)
                    parts.append(jnp.where((row + t >= 0) & (row + t < HH), moved, 0.0))
            base = (dy * DX + dx0) * frames
            block = parts[0] if len(parts) == 1 else jnp.concatenate(parts, axis=0)
            xcol[base : base + per_store * frames, :] = block.astype(BF)
    wide = wbig[...]
    for p, size in pixel_chunks(pix):
        pre[:, p : p + size] = dot(wide, xcol[:, p : p + size])

    per_frame = channels // 16

    def first(i, carry):
        r = pl.multiple_of(i * 16, 16)
        b = pl.multiple_of((i % per_frame) * 16, 16)
        x = pre[pl.ds(r, 16), :] + bias[pl.ds(b, 16), 0:1]
        e = jnp.exp(jnp.minimum(x, 0.0))
        act1[pl.ds(r, 16), :] = (jnp.maximum(x, 0.0) + (e - 1.0)).astype(BF)
        slope1[pl.ds(r, 16), :] = e.astype(BF)
        return carry

    lax.fori_loop(0, rows // 16, first, 0)
    for r in range(0, rows, span):
        for p, size in pixel_chunks(pix):
            pre[r : r + span, p : p + size] = dot(blocks[...], act1[r : r + span, p : p + size])

    def second(i, carry):
        r = pl.multiple_of(i * 16, 16)
        b = pl.multiple_of((i % per_frame) * 16, 16)
        x = pre[pl.ds(r, 16), :] + bias[pl.ds(b, 16), 1:2]
        e = jnp.exp(jnp.minimum(x, 0.0))
        feats[pl.ds(r, 16), :] = (jnp.maximum(x, 0.0) + (e - 1.0)).astype(BF)
        slope2[pl.ds(r, 16), :] = e.astype(BF)
        return carry

    lax.fori_loop(0, rows // 16, second, 0)
    half = 2 * WW
    chunks = pixel_chunks(pix)
    for p, size in chunks[:-1]:
        pay[:, p // 4 : p // 4 + half] = dot(feats[:, p : p + size], pool[...]).astype(BF)
    p, size = chunks[-1]
    tail = dot(feats[:, p : p + size], pool[0:size, :])
    pieces = []
    for t in range(neurons // half):
        at = t * half
        tile = lines[at // width][:, at % width : at % width + half]
        pieces += [pltpu.roll(tile, SEG, 1), tile]
    packed = jnp.concatenate(pieces, axis=0)
    pay[:, p // 4 : p // 4 + half] = jnp.where(iota((rows, half), 1) < SEG, tail, packed).astype(BF)


def drive_terms(projected, target, w, rbias, alive, scale, channels):
    frames = target.shape[0]
    sums = [
        jnp.sum(projected[f * channels : (f + 1) * channels] * w, axis=0, keepdims=True)
        for f in range(frames)
    ]
    drive = jnp.concatenate(sums, axis=0) + rbias
    e = jnp.exp(-jnp.abs(drive))
    rate = jnp.maximum(drive, 0.0) + jnp.log(1.0 + e) + 0.1
    sig = jnp.where(drive >= 0, 1.0, e) / (1.0 + e)
    grad = jnp.where(alive, (1.0 - target / rate) * sig, 0.0) * scale
    return rate, grad


def mixed_rows(grad, w):
    frames = grad.shape[0]
    return jnp.concatenate([grad[f : f + 1] * w for f in range(frames)], axis=0).astype(BF)


def readout_kernel(scale, count, target, pay, mask, wt, rbias, pooled_grad, loss, acc, loss_acc):
    i = pl.program_id(0)
    pooled_n, block = mask.shape
    channels = wt.shape[0]
    frames = target.shape[0]

    @pl.when(i == 0)
    def _():
        acc[...] = jnp.zeros_like(acc)
        loss_acc[...] = jnp.zeros_like(loss_acc)

    w = wt[...].astype(F32)
    m = mask[...]
    projected = dot(pay[:, 0:pooled_n], m)
    alive = (i * block + iota((frames, block), 1)) < count[0]
    rate, grad = drive_terms(projected, target[...], w, rbias[...], alive, scale, channels)
    loss_acc[...] += jnp.where(alive, rate - target[...] * jnp.log(rate), 0.0)
    acc[...] += dot(mixed_rows(grad, w), m, NT)

    @pl.when(i == pl.num_programs(0) - 1)
    def _():
        pooled_grad[...] = acc[...].astype(BF)
        loss[...] = jnp.broadcast_to(jnp.sum(loss_acc[...], keepdims=True) * scale, loss.shape)


def core_backward_kernel(
    channels, pooled_grad, loss, act1, slope1, slope2, xcol, blocks_t, table, unpool, out, grad, g2, g1
):
    rows, pix = act1.shape
    frames = rows // channels
    span = blocks_t.shape[0]
    group = span // channels
    patch_cols = xcol.shape[0]
    per_frame = channels // 16
    for p, size in pixel_chunks(pix):
        grad[:, p : p + size] = dot(pooled_grad[:, p // 4 : (p + size) // 4], unpool[0 : size // 4, 0:size])

    sums = []
    for q in range(per_frame):

        def second(f, total):
            r = pl.multiple_of(f * channels + q * 16, 16)
            g = (grad[pl.ds(r, 16), :] * slope2[pl.ds(r, 16), :].astype(F32)).astype(BF)
            g2[pl.ds(r, 16), :] = g
            return total + jnp.sum(g.astype(F32), axis=1, keepdims=True)

        sums.append(lax.fori_loop(0, frames, second, jnp.zeros((16, 1), F32)))
    mix_bias_grad = jnp.concatenate(sums, axis=0)
    mix_grad = jnp.zeros((channels, span), F32)
    same = (iota((span, span), 0) // channels) == (iota((span, span), 1) // channels)
    for r in range(0, rows, span):
        full = jnp.where(same, dot(g2[r : r + span, :], act1[r : r + span, :], NT), 0.0)
        for a in range(group):
            mix_grad = mix_grad + full[a * channels : (a + 1) * channels]
        for p, size in pixel_chunks(pix):
            grad[r : r + span, p : p + size] = dot(blocks_t[...], g2[r : r + span, p : p + size])
    half = 2 * channels
    folded = mix_grad[:, 0:half]
    for k in range(half, span, half):
        folded = folded + mix_grad[:, k : k + half]
    folded = folded + pltpu.roll(folded, channels, 1)

    def first(i, carry):
        r = pl.multiple_of(i * 16, 16)
        g1[pl.ds(r, 16), :] = (grad[pl.ds(r, 16), :] * slope1[pl.ds(r, 16), :].astype(F32)).astype(BF)
        return carry

    lax.fori_loop(0, rows // 16, first, 0)
    full = dot(g1[...], xcol[...], NT)
    source = iota((channels, patch_cols), 1) % frames
    parts = [jnp.zeros((channels, patch_cols), F32) for _ in range(KT + 1)]
    for f in range(frames):
        piece = full[f * channels : (f + 1) * channels]
        for dt in range(KT):
            parts[dt] = parts[dt] + jnp.where(source == f + dt - 1, piece, 0.0)
        parts[KT] = parts[KT] + piece
    taps = dot(
        jnp.concatenate(parts, axis=0), table[...].astype(F32), NT, precision=lax.Precision.HIGHEST
    )
    lane = iota((channels, PACK), 1)
    conv = jnp.zeros((channels, PACK), F32)
    for dt in range(KT + 1):
        inside = (lane >= dt * KS * KS) & (lane < (dt + 1) * KS * KS)
        conv = conv + jnp.where(inside, taps[dt * channels : (dt + 1) * channels], 0.0)
    used = KT * KS * KS + 1
    low = lane[:, 0:128]
    upper = jnp.where(low < used - 128, conv[:, 128:256], 0.0)
    upper = jnp.where(low == used - 128, mix_bias_grad, upper)
    upper = jnp.where((low == used - 127) & (iota((channels, 128), 0) == 0), loss[0:1, 0:1], upper)
    upper = jnp.where(low >= channels, folded, upper)
    tiles = channels // 8
    out[...] = jnp.zeros_like(out)
    for i in range(tiles):
        out[i] = conv[8 * i : 8 * i + 8, 0:128]
        out[tiles + i] = upper[8 * i : 8 * i + 8, :]


def share_kernel(total, parts, out):
    each = parts.shape[0] // total
    for k in range(each):
        tile = parts[k]
        for d in range(1, total):
            tile = tile + parts[d * each + k]
        for d in range(total):
            out[d * each + k] = tile


def unpack_kernel(parts, conv, conv_bias, mix, mix_bias, loss):
    channels, taps = conv.shape
    tiles = channels // 8
    low = jnp.concatenate([parts[i] for i in range(tiles)], axis=0)
    high = jnp.concatenate([parts[tiles + i] for i in range(tiles)], axis=0)
    rest = taps - 128
    conv[...] = jnp.concatenate([low, high], axis=1)[:, 0:taps]
    mix[...] = pltpu.roll(high, 128 - channels, 1)[:, 0:channels]
    same = iota((channels, channels), 0) == iota((channels, channels), 1)
    conv_bias[...] = jnp.sum(jnp.where(same, high[:, rest : rest + 1], 0.0), axis=0, keepdims=True)
    mix_bias[...] = jnp.sum(jnp.where(same, high[:, rest + 1 : rest + 2], 0.0), axis=0, keepdims=True)
    loss[...] = high[0:1, rest + 2 : rest + 3]


def owned_rows_kernel(scale, where, count, *refs):
    clips = len(refs) - 6
    pays = refs[:clips]
    mask, wt, rbias, mask_grad, feat_grad, bias_grad = refs[clips:]
    i = pl.program_id(0)
    pooled_n, block = mask.shape
    channels = wt.shape[0]
    frames = pays[0].shape[0] // channels
    first = (where[0] * pl.num_programs(0) + i) * block
    m = mask[...]
    w = wt[...].astype(F32)
    alive = (first + iota((frames, block), 1)) < count[0]
    total = None
    feat = jnp.zeros((channels, block), F32)
    bias = jnp.zeros((frames, block), F32)
    segs = block // SEG
    base = pl.multiple_of(first // SEG * frames, segs * frames)
    low = iota((frames, 128), 1) < SEG
    for pay in pays:
        pooled = pay[:, 0:pooled_n]
        held = pay[pl.ds(base, segs * frames), pooled_n - SEG : pooled_n + SEG].astype(F32)
        tiles = []
        for j in range(0, segs, 2):
            even = held[j * frames : (j + 1) * frames]
            odd = held[(j + 1) * frames : (j + 2) * frames]
            tiles.append(jnp.where(low, pltpu.roll(even, SEG, 1), odd))
        target = jnp.concatenate(tiles, axis=1)
        projected = dot(pooled, m)
        _, grad = drive_terms(projected, target, w, rbias[...], alive, scale, channels)
        for f in range(frames):
            feat = feat + grad[f : f + 1] * projected[f * channels : (f + 1) * channels]
        bias = bias + grad
        part = dot(pooled, mixed_rows(grad, w), TN)
        total = part if total is None else total + part
    mask_grad[...] = total
    feat_grad[...] = feat
    bias_grad[...] = jnp.sum(bias, axis=0, keepdims=True)


def params(limit=40):
    return pltpu.CompilerParams(vmem_limit_bytes=limit << 20)


def cost(flops, moved=1 << 20):
    return pl.CostEstimate(flops=int(flops), transcendentals=0, bytes_accessed=int(moved))


def in_hbm(*arrays):
    return [pltpu.with_memory_space_constraint(a, pltpu.HBM) for a in arrays]


def xor_pairs(size, mask):
    return [(i, i ^ mask) for i in range(size)]


def per_device(
    video, responses, assignment, counts, conv_weight, conv_bias, mix_weight, mix_bias, masks, feat_w, readout_bias
):
    sess_total = lax.axis_size("sess")
    clip_total = lax.axis_size("clip")
    total = sess_total * clip_total
    clip_block, frame_block, pix = video.shape
    neurons = responses.shape[2]
    pooled_n = masks.shape[2]
    channels, taps = conv_weight.shape
    frames = frame_block * sess_total
    rows = frames * channels
    own = neurons // clip_total
    block = min(512, own)
    assert clip_block == sess_total and frame_block == 1 and masks.shape[0] == 1
    assert neurons == channels * SEG and pooled_n % 128 == SEG and pix == HH * WW
    scale = 1.0 / (clip_block * clip_total * frames)

    group = max(1, 256 // channels)
    lines = 16
    packet = 512
    assert neurons + pix <= lines * packet
    send = pl.pallas_call(
        select_kernel,
        out_shape=jax.ShapeDtypeStruct((sess_total, lines, packet), BF),
        compiler_params=params(),
        name="select",
    )(*in_hbm(assignment[None, :], video.reshape(clip_block, pix), responses.reshape(clip_block, neurons)))
    recv = lax.all_to_all(send, "sess", split_axis=0, concat_axis=0, tiled=True)

    patch_cols = KS * DX * frames
    span = channels * group
    half = 2 * WW
    wbig, blocks, blocks_t, bias, table, pool, unpool = pl.pallas_call(
        functools.partial(prep_kernel, frames),
        out_shape=(
            jax.ShapeDtypeStruct((rows, patch_cols), BF),
            jax.ShapeDtypeStruct((span, span), BF),
            jax.ShapeDtypeStruct((span, span), BF),
            jax.ShapeDtypeStruct((channels, 128), F32),
            jax.ShapeDtypeStruct((PACK, patch_cols), BF),
            jax.ShapeDtypeStruct((4 * half, half), BF),
            jax.ShapeDtypeStruct((half, 4 * half), BF),
        ),
        compiler_params=params(),
        cost_estimate=cost(1 << 27),
        name="prep",
    )(*in_hbm(conv_weight, conv_bias[None, :], mix_weight, mix_bias[None, :]))

    wt = jnp.swapaxes(feat_w, 1, 2).reshape(channels, neurons)
    mask_t = jnp.swapaxes(masks, 1, 2).reshape(pooled_n, neurons)
    mask_t, wt, rbias = in_hbm(mask_t, wt, readout_bias)
    width = pooled_n + SEG
    pay, target, act1, slope1, slope2, xcol = pl.pallas_call(
        core_forward_kernel,
        out_shape=(
            jax.ShapeDtypeStruct((rows, width), BF),
            jax.ShapeDtypeStruct((frames, neurons), F32),
            jax.ShapeDtypeStruct((rows, pix), BF),
            jax.ShapeDtypeStruct((rows, pix), BF),
            jax.ShapeDtypeStruct((rows, pix), BF),
            jax.ShapeDtypeStruct((patch_cols, pix), BF),
        ),
        scratch_shapes=[pltpu.VMEM((rows, pix), F32), pltpu.VMEM((rows, pix), BF)],
        compiler_params=params(),
        cost_estimate=cost(2 * rows * pix * patch_cols, 8 * rows * pix),
        name="core_forward",
    )(recv, wbig, blocks, bias, pool)

    near = {0: pay}
    for mask in range(1, clip_total):
        if mask % 2 == 0 or mask == 1:
            near[mask] = lax.ppermute(pay, "clip", xor_pairs(clip_total, mask))

    smem = pl.BlockSpec(memory_space=pltpu.SMEM)
    big = min(512, neurons)
    work = 2 * rows * neurons * pooled_n
    pooled_grad, loss = pl.pallas_call(
        functools.partial(readout_kernel, scale),
        grid=(neurons // big,),
        in_specs=[
            smem,
            pl.BlockSpec((frames, big), lambda i: (0, i)),
            pl.BlockSpec((rows, width), lambda i: (0, 0)),
            pl.BlockSpec((pooled_n, big), lambda i: (0, i)),
            pl.BlockSpec((channels, big), lambda i: (0, i)),
            pl.BlockSpec((1, big), lambda i: (0, i)),
        ],
        out_specs=(
            pl.BlockSpec((rows, pooled_n), lambda i: (0, 0)),
            pl.BlockSpec((8, 128), lambda i: (0, 0)),
        ),
        out_shape=(jax.ShapeDtypeStruct((rows, pooled_n), BF), jax.ShapeDtypeStruct((8, 128), F32)),
        scratch_shapes=[pltpu.VMEM((rows, pooled_n), F32), pltpu.VMEM((frames, big), F32)],
        compiler_params=params(),
        cost_estimate=cost(2 * work, 2 * neurons * pooled_n),
        name="readout",
    )(counts, target, pay, mask_t, wt, rbias)

    pieces = total * max(1, (2 * channels // 8) // total)
    core = pl.pallas_call(
        functools.partial(core_backward_kernel, channels),
        out_shape=jax.ShapeDtypeStruct((pieces, 8, 128), F32),
        scratch_shapes=[
            pltpu.VMEM((rows, pix), F32),
            pltpu.VMEM((rows, pix), BF),
            pltpu.VMEM((rows, pix), BF),
        ],
        compiler_params=params(),
        cost_estimate=cost(2 * work, 8 * rows * pix),
        name="core_backward",
    )(pooled_grad, loss, act1, slope1, slope2, xcol, blocks_t, table, unpool)

    far = [mask for mask in near if mask > 1]
    held, core = lax.optimization_barrier(([near[mask] for mask in far], core))
    pays = [near[0], near[1]]
    for mask, value in zip(far, held):
        pays += [value, lax.ppermute(value, "clip", xor_pairs(clip_total, 1))]

    axes = ("clip", "sess")
    parts = lax.all_to_all(core, axes, split_axis=0, concat_axis=0, tiled=True)

    where = lax.axis_index("clip").astype(jnp.int32)[None]
    steps = own // block
    mask_grad, feat_grad, grad_rbias = pl.pallas_call(
        functools.partial(owned_rows_kernel, scale),
        grid_spec=pltpu.PrefetchScalarGridSpec(
            num_scalar_prefetch=1,
            grid=(steps,),
            in_specs=[smem]
            + [pl.BlockSpec((rows, width), lambda i, at: (0, 0)) for _ in pays]
            + [
                pl.BlockSpec((pooled_n, block), lambda i, at: (0, at[0] * steps + i)),
                pl.BlockSpec((channels, block), lambda i, at: (0, at[0] * steps + i)),
                pl.BlockSpec((1, block), lambda i, at: (0, at[0] * steps + i)),
            ],
            out_specs=(
                pl.BlockSpec((pooled_n, block), lambda i, at: (0, i)),
                pl.BlockSpec((channels, block), lambda i, at: (0, i)),
                pl.BlockSpec((1, block), lambda i, at: (0, i)),
            ),
        ),
        out_shape=(
            jax.ShapeDtypeStruct((pooled_n, own), F32),
            jax.ShapeDtypeStruct((channels, own), F32),
            jax.ShapeDtypeStruct((1, own), F32),
        ),
        compiler_params=params(),
        cost_estimate=cost(2 * work, 4 * own * pooled_n),
        name="owned_rows",
    )(where, counts, *pays, mask_t, wt, rbias)

    parts, mask_grad, feat_grad, grad_rbias = lax.optimization_barrier((parts, mask_grad, feat_grad, grad_rbias))
    copies = pl.pallas_call(
        functools.partial(share_kernel, total),
        out_shape=jax.ShapeDtypeStruct((pieces, 8, 128), F32),
        compiler_params=params(),
        name="share",
    )(parts)
    summed = lax.all_to_all(copies, axes, split_axis=0, concat_axis=0, tiled=True)
    grad_conv, grad_cb, grad_mix, grad_mb, loss = pl.pallas_call(
        unpack_kernel,
        out_shape=(
            jax.ShapeDtypeStruct((channels, taps), F32),
            jax.ShapeDtypeStruct((1, channels), F32),
            jax.ShapeDtypeStruct((channels, channels), F32),
            jax.ShapeDtypeStruct((1, channels), F32),
            jax.ShapeDtypeStruct((1, 1), F32),
        ),
        compiler_params=params(),
        name="unpack",
    )(summed)
    return (
        loss.reshape(()),
        grad_conv,
        grad_cb.reshape(channels),
        grad_mix,
        grad_mb.reshape(channels),
        jnp.swapaxes(mask_grad[None], 1, 2),
        jnp.swapaxes(feat_grad[None], 1, 2),
        grad_rbias,
    )


def solution(mesh):
    return jax.shard_map(
        per_device,
        mesh=mesh,
        in_specs=(
            P("clip", "sess", None),
            P("clip", "sess", None),
            P("clip"),
            P("sess"),
            P(),
            P(),
            P(),
            P(),
            P("sess", None, None),
            P("sess", None, None),
            P("sess", None),
        ),
        out_specs=(
            P(),
            P(),
            P(),
            P(),
            P(),
            P("sess", "clip", None),
            P("sess", "clip", None),
            P("sess", "clip"),
        ),
        check_vma=False,
    )
```

time: 123 us -> 77.8 us (0.63)
  local copies, waits for them, and re-layouts: 24.3 us -> 0 us
  waiting for transfers between devices: 26.5 us -> 5.32 us
  blocking collectives: 9.57 us -> 13.3 us
  Pallas kernels: 47.2 us -> 45.3 us
    unnamed x36 -> x0, local copies, waits for them, and re-layouts: 18.7 us -> none
    ppermute x3, waiting for transfers between devices: 13.7 us -> 0.01 us  [the longest x2 0.01 us: per_device(): near[mask] = lax.ppermute(pay, 'clip', xor_pairs(clip_total, mask))]
    all_to_all x1, waiting for transfers between devices: 7.09 us -> 0.01 us  [per_device(): parts = lax.all_to_all(core, axes, split_axis=0, concat_axis=0, tiled=True)]
    all_to_all x1, blocking collectives: 9.57 us -> 13.3 us  [per_device(): lax.all_to_all(copies, axes, split_axis=0, concat_axis=0, tiled=True)]
    pallas_call x1, Pallas kernels: 12.2 us -> 9.87 us  [per_device(): pl.pallas_call(functools.partial(owned_rows_kernel, scale), grid_spec=plt...]
    pallas_call x1 -> x5, Pallas kernels: 11.4 us -> 13.6 us  [the longest x1 9.66 us: per_device(): pl.pallas_call(functools.partial(core_backward_kernel, channels), out_sha...]
    broadcast_in_dim x3 -> x0, local copies, waits for them, and re-layouts: 2.15 us -> none  [the longest x1 0.74 us: per_device(): conv_bias[:, None]]
    slice x3 -> x0, local copies, waits for them, and re-layouts: 1.97 us -> none  [the longest x1 0.7 us: per_device(): summed[:, used]]
  transfers between devices with their start and end apart: 5 -> 5, of which waited for: 3 -> 1; matrix products, arithmetic and copies ran while one was open for 10% -> 0% of each run, Pallas kernels for 18% -> 41%
where the time goes in v1:
time: 77.8 us; the launch traced here: 77.4 us
  Pallas kernels  45.3 us (58%)
  blocking collectives  13.3 us (17%)
  starting transfers between devices  12.1 us (16%)
  waiting for transfers between devices  5.32 us (7%)
  between operations  1.34 us (2%)
    all_to_all x1, blocking collectives, per_device(): lax.all_to_all(copies, axes, split_axis=0, concat_axis=0, tiled=True)  13.3 us
    pallas_call x1, Pallas kernels, per_device(): pl.pallas_call(core_forward_kernel, out_shape=(jax.ShapeDtypeStruct((rows...  10.9 us
    pallas_call x1, Pallas kernels, per_device(): pl.pallas_call(functools.partial(readout_kernel, scale), grid=(neurons //...  10.9 us
    pallas_call x1, Pallas kernels, per_device(): pl.pallas_call(functools.partial(owned_rows_kernel, scale), grid_spec=plt...  9.87 us
    pallas_call x1, Pallas kernels, per_device(): pl.pallas_call(functools.partial(core_backward_kernel, channels), out_sha...  9.66 us
    all_to_all x1, starting transfers between devices, per_device(): recv = lax.all_to_all(send, 'sess', split_axis=0, concat_axis=0, tiled=True)  7.28 us
    all_to_all x1, waiting for transfers between devices, per_device(): recv = lax.all_to_all(send, 'sess', split_axis=0, concat_axis=0, tiled=True)  5.31 us
    all_to_all x1, starting transfers between devices, per_device(): parts = lax.all_to_all(core, axes, split_axis=0, concat_axis=0, tiled=True)  2.74 us
  transfers between devices with their start and end apart: 5, of which 1 were waited for; matrix products, arithmetic and copies ran while one was open for 0% of the time, Pallas kernels for 41%

profile of v1, /device:TPU:0, one launch (start us, length us, event | category | flops | bytes accessed | tf_op | source)
XLA Modules:
  0.0 77.4 jit_solution(6824302553748880559)
XLA Ops:
  0.6 1.8 %select.1 = bf16[8,16,512]{2,1,0:T(8,128)(2,1)} custom-call(s32[1,8]{1,0:T(1,128)} %bitcast.23, bf16[8,2304]{1,0:T(8,128)(2,1)} %bitcast.22, bf16[8,4096]{1,0:T(8,128)(2,1)} %bitcast.21), custom_call_target="tpu_custom_call" | custom-call | tf_op jit(solution)/shard_map/select/pallas_call | solution.py:405
  2.5 7.3 %all-to-all-start = ((bf16[8,16,512]{2,1,0:T(8,128)(2,1)}), bf16[8,16,512]{2,1,0:T(8,128)(2,1)S(1)}, u32[]{:S(2)}, u32[]{:S(2)}) async-start(bf16[8,16,512]{2,1,0:T(8,128)(2,1)} %select.1), calls=%async_computation | async-start | bytes 262144 | tf_op jit(solution)/shard_map/all_to_all | solution.py:411
  10.4 1.4 %prep.1 = (bf16[512,448]{1,0:T(8,128)(2,1)S(1)}, bf16[256,256]{1,0:T(8,128)(2,1)S(1)}, bf16[256,256]{1,0:T(8,128)(2,1)S(1)}, f32[64,128]{1,0:T(8,128)S(1)}, bf16...) custom-call(bf16[64,147]{1,0:T(8,128)(2,1)} %weight.1, f32[1,64]{1,0:T(1,128)} %bitcast.28, ...), custom_call_target="tpu_custom_call" | custom-call | flops 134217728 | bytes 1048576 | tf_op jit(solution)/shard_map/prep/pallas_call | solution.py:416
  11.8 5.3 %all-to-all-done.recv = bf16[8,16,512]{2,1,0:T(8,128)(2,1)S(1)} async-done(((bf16[8,16,512]{2,1,0:T(8,128)(2,1)}), bf16[8,16,512]{2,1,0:T(8,128)(2,1)S(1)}, u32[]{:S(2)}, u32[]{:S(2)}) %all-to-all-start) | async-done | bytes 131104 | tf_op jit(solution)/shard_map/all_to_all | solution.py:411
  17.1 10.9 %core_forward.1 = (bf16[512,640]{1,0:T(8,128)(2,1)S(1)}, f32[8,4096]{1,0:T(8,128)S(1)}, bf16[512,2304]{1,0:T(8,128)(2,1)S(1)}, bf16[512,2304]{1,0:T(8,128)(2,1)S...) custom-call(bf16[8,16,512]{2,1,0:T(8,128)(2,1)S(1)} %all-to-all-done.recv, ...), custom_call_target="tpu_custom_call" | custom-call | flops 1056964608 | bytes 9437184 | tf_op jit(solution)/shard_map/core_forward/pallas_call | solution.py:436
  28.0 1.6 %collective-permute-start = (bf16[512,640]{1,0:T(8,128)(2,1)S(1)}, bf16[512,640]{1,0:T(8,128)(2,1)S(1)}, u32[]{:S(2)}, u32[]{:S(2)}) collective-permute-start(bf16[512,640]{1,0:T(8,128)(2,1)S(1)} %get-tuple-element.41.pay.refs_0_), channel_id=1, source_target_pairs={{0,16},{8,24},{16,0},{24,8},{1,17},{9,25},{17,1},{25,9},{2,18},{10... | collective-permute-start | bytes 1966088 | tf_op jit(solution)/shard_map/ppermute | solution.py:455
  29.6 0.0 collective-permute-start.1
  29.6 10.9 %readout.1 = (bf16[512,576]{1,0:T(8,128)(2,1)S(1)}, f32[8,128]{1,0:T(8,128)S(1)}) custom-call(s32[1]{0:T(128)S(6)} %copy.19.count, f32[8,4096]{1,0:T(8,128)S(1)} %get-tuple-element.42.target, bf16[512,640]{1,0:T(8,128)(2,1)S(1)} %get-tuple-element.41.pay.refs_0_, bf16[576,4096]{1,0:T(8,128)(2,1)} %bitcast.24, bf16[64,4096]{1,0:T(8,128)(2,1)} %bitcast.26, ...), custom_call_target="tpu_custom_call" | custom-call | flops 4831838208 | bytes 4718592 | tf_op jit(solution)/shard_map/readout/pallas_call | solution.py:460
  40.5 9.7 %core_backward.1 = f32[32,8,128]{2,1,0:T(8,128)} custom-call(bf16[512,576]{1,0:T(8,128)(2,1)S(1)} %get-tuple-element.43.pooled_grad, f32[8,128]{1,0:T(8,128)S(1)} %get-tuple-element.44.loss, bf16[512,2304]{1,0:T(8,128)(2,1)S(1)} %get-tuple-element.45.act1, bf16[512,2304]{1,0:T(8,128)(2,1)S(1)} %get-tuple-element.46.slope1, ...), custom_call_target="tpu_custom_call" | custom-call | flops 4831838208 | bytes 9437184 | tf_op jit(solution)/shard_map/core_backward/pallas_call | solution.py:483
  50.2 0.0 collective-permute-done.refs_2_
  50.2 0.5 collective-permute-start.2
  50.7 2.7 %all-to-all-start.1 = ((f32[32,8,128]{2,1,0:T(8,128)}), f32[32,8,128]{2,1,0:T(8,128)S(1)}, u32[]{:S(2)}, u32[]{:S(2)}) async-start(f32[32,8,128]{2,1,0:T(8,128)} %core_backward.1), calls=%async_computation.1 | async-start | bytes 262144 | tf_op jit(solution)/shard_map/all_to_all | solution.py:503
  53.4 0.0 collective-permute-done.1.refs_1_
  53.4 0.0 collective-permute-done.2.refs_3_
  53.4 9.9 %owned_rows.1 = (f32[576,1024]{1,0:T(8,128)}, f32[64,1024]{1,0:T(8,128)}, f32[1,1024]{1,0:T(1,128)}) custom-call(s32[1]{0:T(128)} %bitcast.9.where, s32[1]{0:T(128)S(6)} %copy.19.count, bf16[512,640]{1,0:T(8,128)(2,1)S(1)} %get-tuple-element.41.pay.refs_0_, bf16[512,640]{1,0:T(8,128)(2,1)S(1)} %collective-permute-done.1.refs_1_, ...), custom_call_target="tpu_custom_call" | custom-call | flops 4831838208 | bytes 2359296 | tf_op jit(solution)/shard_map/owned_rows/pallas_call | solution.py:507
  63.3 0.0 all-to-all-done.1.parts
  63.4 13.3 %all_to_all.15.parts = f32[32,8,128]{2,1,0:T(8,128)S(1)} all-to-all(f32[32,8,128]{2,1,0:T(8,128)S(1)} %share.1), channel_id=1, replica_groups=mesh['clip'=4,'sess'=8] {'clip','sess'}, dimensions={0} | all-to-all | bytes 262144 | tf_op jit(solution)/shard_map/all_to_all | solution.py:542
  76.6 0.7 unpack.1
  (1 shorter events, 0.0 us)
Async XLA Ops:
  2.5 14.6 %all-to-all-start = ((bf16[8,16,512]{2,1,0:T(8,128)(2,1)}), bf16[8,16,512]{2,1,0:T(8,128)(2,1)S(1)}, u32[]{:S(2)}, u32[]{:S(2)}) async-start(bf16[8,16,512]{2,1,0:T(8,128)(2,1)} %select.1), calls=%async_computation | async-start | bytes 262144 | tf_op jit(solution)/shard_map/all_to_all | solution.py:411
  28.0 22.1 %collective-permute-start = (bf16[512,640]{1,0:T(8,128)(2,1)S(1)}, bf16[512,640]{1,0:T(8,128)(2,1)S(1)}, u32[]{:S(2)}, u32[]{:S(2)}) collective-permute-start(bf16[512,640]{1,0:T(8,128)(2,1)S(1)} %get-tuple-element.41.pay.refs_0_), channel_id=1, source_target_pairs={{0,16},{8,24},{16,0},{24,8},{1,17},{9,25},{17,1},{25,9},{2,18},{10... | collective-permute-start | bytes 1966088 | tf_op jit(solution)/shard_map/ppermute | solution.py:455
  29.6 23.8 %collective-permute-start.1 = (bf16[512,640]{1,0:T(8,128)(2,1)S(1)}, bf16[512,640]{1,0:T(8,128)(2,1)S(1)}, u32[]{:S(2)}, u32[]{:S(2)}) collective-permute-start(bf16[512,640]{1,0:T(8,128)(2,1)S(1)} %get-tuple-element.41.pay.refs_0_), channel_id=1, source_target_pairs={{0,8},{8,0},{16,24},{24,16},{1,9},{9,1},{17,25},{25,17},{2,10},{10... | collective-permute-start | bytes 1966088 | tf_op jit(solution)/shard_map/ppermute | solution.py:455
  50.2 3.3 %collective-permute-start.2 = (bf16[512,640]{1,0:T(8,128)(2,1)S(1)}, bf16[512,640]{1,0:T(8,128)(2,1)S(1)}, u32[]{:S(2)}, u32[]{:S(2)}) collective-permute-start(bf16[512,640]{1,0:T(8,128)(2,1)S(1)} %collective-permute-done.refs_2_), channel_id=1, source_target_pairs={{0,8},{8,0},{16,24},{24,16},{1,9},{9,1},{17,25},{25,17},{2,10},{10... | collective-permute-start | bytes 1966088 | tf_op jit(solution)/shard_map/ppermute | solution.py:500
  50.7 12.6 %all-to-all-start.1 = ((f32[32,8,128]{2,1,0:T(8,128)}), f32[32,8,128]{2,1,0:T(8,128)S(1)}, u32[]{:S(2)}, u32[]{:S(2)}) async-start(f32[32,8,128]{2,1,0:T(8,128)} %core_backward.1), calls=%async_computation.1 | async-start | bytes 262144 | tf_op jit(solution)/shard_map/all_to_all | solution.py:503

commit v2 on v1

--- a/solution.py
+++ b/solution.py
@@ -14,6 +14,7 @@
 DX = 8
 PACK = 256
 SEG = 64
+CHUNK = 4 * WW
 BF = jnp.bfloat16
 F32 = jnp.float32
 NT = (((1,), (1,)), ((), ()))
@@ -26,11 +27,6 @@
 
 def iota(shape, axis):
     return lax.broadcasted_iota(jnp.int32, shape, axis)
-
-
-def pixel_chunks(pix):
-    step = 8 * WW
-    return [(p, min(step, pix - p)) for p in range(0, pix, step)]
 
 
 def bias_column(row):
@@ -82,8 +78,8 @@
     for ref, base in ((blocks, square), (blocks_t, square.T)):
         wide = jnp.concatenate([base] * group, axis=1)
         ref[...] = jnp.where(same, jnp.concatenate([wide] * group, axis=0), 0.0).astype(BF)
-    lane = iota(bias.shape, 1)
-    bias[...] = jnp.where(lane == 0, bias_column(cbias[...]), bias_column(mbias[...]))
+    bias[0] = jnp.broadcast_to(bias_column(cbias[...]), bias.shape[1:])
+    bias[1] = jnp.broadcast_to(bias_column(mbias[...]), bias.shape[1:])
     tap = iota((channels, taps), 1)
     weights = weight[...].astype(F32)
     split = [
@@ -99,10 +95,12 @@
         wbig[f * channels : (f + 1) * channels, :] = total.astype(BF)
 
 
-def core_forward_kernel(recv, wbig, blocks, bias, pool, pay, target, act1, slope1, slope2, xcol, pre, feats):
+def core_forward_kernel(
+    recv, wbig, blocks, bias, pool, pay, target, act1, slope1, slope2, xcol, pre0, pre1, mid0, mid1, feats
+):
     frames, _, width = recv.shape
     rows, pix = act1.shape
-    channels = bias.shape[0]
+    channels = bias.shape[1]
     neurons = target.shape[1]
     span = blocks.shape[0]
     packet = recv[...].astype(F32)
@@ -140,42 +138,37 @@
             base = (dy * DX + dx0) * frames
             block = parts[0] if len(parts) == 1 else jnp.concatenate(parts, axis=0)
             xcol[base : base + per_store * frames, :] = block.astype(BF)
+    half = 2 * WW
+    pre = (pre0, pre1)
+    mid = (mid0, mid1)
+    count = pix // CHUNK
     wide = wbig[...]
-    for p, size in pixel_chunks(pix):
-        pre[:, p : p + size] = dot(wide, xcol[:, p : p + size])
-
-    per_frame = channels // 16
-
-    def first(i, carry):
-        r = pl.multiple_of(i * 16, 16)
-        b = pl.multiple_of((i % per_frame) * 16, 16)
-        x = pre[pl.ds(r, 16), :] + bias[pl.ds(b, 16), 0:1]
-        e = jnp.exp(jnp.minimum(x, 0.0))
-        act1[pl.ds(r, 16), :] = (jnp.maximum(x, 0.0) + (e - 1.0)).astype(BF)
-        slope1[pl.ds(r, 16), :] = e.astype(BF)
-        return carry
-
-    lax.fori_loop(0, rows // 16, first, 0)
-    for r in range(0, rows, span):
-        for p, size in pixel_chunks(pix):
-            pre[r : r + span, p : p + size] = dot(blocks[...], act1[r : r + span, p : p + size])
-
-    def second(i, carry):
-        r = pl.multiple_of(i * 16, 16)
-        b = pl.multiple_of((i % per_frame) * 16, 16)
-        x = pre[pl.ds(r, 16), :] + bias[pl.ds(b, 16), 1:2]
-        e = jnp.exp(jnp.minimum(x, 0.0))
-        feats[pl.ds(r, 16), :] = (jnp.maximum(x, 0.0) + (e - 1.0)).astype(BF)
-        slope2[pl.ds(r, 16), :] = e.astype(BF)
-        return carry
-
-    lax.fori_loop(0, rows // 16, second, 0)
-    half = 2 * WW
-    chunks = pixel_chunks(pix)
-    for p, size in chunks[:-1]:
-        pay[:, p // 4 : p // 4 + half] = dot(feats[:, p : p + size], pool[...]).astype(BF)
-    p, size = chunks[-1]
-    tail = dot(feats[:, p : p + size], pool[0:size, :])
+
+    def activate(source, which, act, slope, at):
+        add = jnp.concatenate([bias[which]] * (CHUNK // 128), axis=1)
+        for r in range(0, rows, channels):
+            x = source[r : r + channels, :] + add
+            e = jnp.exp(jnp.minimum(x, 0.0))
+            act[r : r + channels, at] = (jnp.maximum(x, 0.0) + (e - 1.0)).astype(BF)
+            slope[r : r + channels, at] = e.astype(BF)
+
+    for t in range(count + 2):
+        if t < count:
+            pre[t % 2][...] = dot(wide, xcol[:, t * CHUNK : (t + 1) * CHUNK])
+        if 1 <= t <= count:
+            at = slice((t - 1) * CHUNK, t * CHUNK)
+            activate(pre[(t - 1) % 2], 0, act1, slope1, at)
+            for r in range(0, rows, span):
+                mid[(t - 1) % 2][r : r + span, :] = dot(blocks[...], act1[r : r + span, at])
+        if t >= 2:
+            at = slice((t - 2) * CHUNK, (t - 1) * CHUNK)
+            activate(mid[t % 2], 1, feats, slope2, at)
+            if t % 2 == 1:
+                first = (t - 3) * CHUNK
+                pooled = dot(feats[:, first : first + 2 * CHUNK], pool[...])
+                pay[:, first // 4 : first // 4 + half] = pooled.astype(BF)
+    p = pix - CHUNK
+    tail = dot(feats[:, p:pix], pool[0:CHUNK, :])
     pieces = []
     for t in range(neurons // half):
         at = t * half
@@ -221,57 +214,60 @@
     alive = (i * block + iota((frames, block), 1)) < count[0]
     rate, grad = drive_terms(projected, target[...], w, rbias[...], alive, scale, channels)
     loss_acc[...] += jnp.where(alive, rate - target[...] * jnp.log(rate), 0.0)
-    acc[...] += dot(mixed_rows(grad, w), m, NT)
+    acc[...] += dot(m, mixed_rows(grad, w), NT)
 
     @pl.when(i == pl.num_programs(0) - 1)
     def _():
-        pooled_grad[...] = acc[...].astype(BF)
+        pooled_grad[...] = acc[...].T.astype(BF)
         loss[...] = jnp.broadcast_to(jnp.sum(loss_acc[...], keepdims=True) * scale, loss.shape)
 
 
 def core_backward_kernel(
-    channels, pooled_grad, loss, act1, slope1, slope2, xcol, blocks_t, table, unpool, out, grad, g2, g1
+    channels, pooled_grad, loss, act1, slope1, slope2, xcol, blocks_t, table, unpool, out, up0, up1, down0, down1, g2, g1
 ):
     rows, pix = act1.shape
     frames = rows // channels
     span = blocks_t.shape[0]
     group = span // channels
     patch_cols = xcol.shape[0]
-    per_frame = channels // 16
-    for p, size in pixel_chunks(pix):
-        grad[:, p : p + size] = dot(pooled_grad[:, p // 4 : (p + size) // 4], unpool[0 : size // 4, 0:size])
-
-    sums = []
-    for q in range(per_frame):
-
-        def second(f, total):
-            r = pl.multiple_of(f * channels + q * 16, 16)
-            g = (grad[pl.ds(r, 16), :] * slope2[pl.ds(r, 16), :].astype(F32)).astype(BF)
-            g2[pl.ds(r, 16), :] = g
-            return total + jnp.sum(g.astype(F32), axis=1, keepdims=True)
-
-        sums.append(lax.fori_loop(0, frames, second, jnp.zeros((16, 1), F32)))
-    mix_bias_grad = jnp.concatenate(sums, axis=0)
+    up = (up0, up1)
+    down = (down0, down1)
+    count = pix // CHUNK
+    half = 2 * WW
+    bias_sum = jnp.zeros((channels, 128), F32)
+    for t in range(count + 2):
+        if t < count:
+            first = (t // 2) * half
+            wide = min(half, pooled_grad.shape[1] - first)
+            side = (t % 2) * CHUNK
+            up[t % 2][...] = dot(pooled_grad[:, first : first + wide], unpool[0:wide, side : side + CHUNK])
+        if 1 <= t <= count:
+            at = slice((t - 1) * CHUNK, t * CHUNK)
+            for r in range(0, rows, channels):
+                g = (up[(t - 1) % 2][r : r + channels, :] * slope2[r : r + channels, at].astype(F32)).astype(BF)
+                g2[r : r + channels, at] = g
+                g = g.astype(F32)
+                for c in range(0, CHUNK, 128):
+                    bias_sum = bias_sum + g[:, c : c + 128]
+            for r in range(0, rows, span):
+                down[(t - 1) % 2][r : r + span, :] = dot(blocks_t[...], g2[r : r + span, at])
+        if t >= 2:
+            at = slice((t - 2) * CHUNK, (t - 1) * CHUNK)
+            for r in range(0, rows, channels):
+                g = down[t % 2][r : r + channels, :] * slope1[r : r + channels, at].astype(F32)
+                g1[r : r + channels, at] = g.astype(BF)
+    mix_bias_grad = jnp.sum(bias_sum, axis=1, keepdims=True)
     mix_grad = jnp.zeros((channels, span), F32)
     same = (iota((span, span), 0) // channels) == (iota((span, span), 1) // channels)
     for r in range(0, rows, span):
         full = jnp.where(same, dot(g2[r : r + span, :], act1[r : r + span, :], NT), 0.0)
         for a in range(group):
             mix_grad = mix_grad + full[a * channels : (a + 1) * channels]
-        for p, size in pixel_chunks(pix):
-            grad[r : r + span, p : p + size] = dot(blocks_t[...], g2[r : r + span, p : p + size])
-    half = 2 * channels
-    folded = mix_grad[:, 0:half]
-    for k in range(half, span, half):
-        folded = folded + mix_grad[:, k : k + half]
+    fold = 2 * channels
+    folded = mix_grad[:, 0:fold]
+    for k in range(fold, span, fold):
+        folded = folded + mix_grad[:, k : k + fold]
     folded = folded + pltpu.roll(folded, channels, 1)
-
-    def first(i, carry):
-        r = pl.multiple_of(i * 16, 16)
-        g1[pl.ds(r, 16), :] = (grad[pl.ds(r, 16), :] * slope1[pl.ds(r, 16), :].astype(F32)).astype(BF)
-        return carry
-
-    lax.fori_loop(0, rows // 16, first, 0)
     full = dot(g1[...], xcol[...], NT)
     source = iota((channels, patch_cols), 1) % frames
     parts = [jnp.zeros((channels, patch_cols), F32) for _ in range(KT + 1)]
@@ -280,9 +276,12 @@
         for dt in range(KT):
             parts[dt] = parts[dt] + jnp.where(source == f + dt - 1, piece, 0.0)
         parts[KT] = parts[KT] + piece
-    taps = dot(
-        jnp.concatenate(parts, axis=0), table[...].astype(F32), NT, precision=lax.Precision.HIGHEST
-    )
+    left = jnp.concatenate(parts, axis=0)
+    taps = jnp.zeros((left.shape[0], PACK), F32)
+    for _ in range(3):
+        term = left.astype(BF)
+        left = left - term.astype(F32)
+        taps = taps + dot(term, table[...], NT)
     lane = iota((channels, PACK), 1)
     conv = jnp.zeros((channels, PACK), F32)
     for dt in range(KT + 1):
@@ -325,15 +324,15 @@
     loss[...] = high[0:1, rest + 2 : rest + 3]
 
 
-def owned_rows_kernel(scale, where, count, *refs):
-    clips = len(refs) - 6
+def owned_rows_kernel(scale, clips, steps, begin, where, count, *refs):
     pays = refs[:clips]
-    mask, wt, rbias, mask_grad, feat_grad, bias_grad = refs[clips:]
-    i = pl.program_id(0)
+    mask, wt, rbias = refs[clips : clips + 3]
+    mask_grad, feat_grad, bias_grad = refs[-3:]
+    i = begin + pl.program_id(0)
     pooled_n, block = mask.shape
     channels = wt.shape[0]
     frames = pays[0].shape[0] // channels
-    first = (where[0] * pl.num_programs(0) + i) * block
+    first = (where[0] * steps + i) * block
     m = mask[...]
     w = wt[...].astype(F32)
     alive = (first + iota((frames, block), 1)) < count[0]
@@ -419,7 +418,7 @@
             jax.ShapeDtypeStruct((rows, patch_cols), BF),
             jax.ShapeDtypeStruct((span, span), BF),
             jax.ShapeDtypeStruct((span, span), BF),
-            jax.ShapeDtypeStruct((channels, 128), F32),
+            jax.ShapeDtypeStruct((2, channels, 128), F32),
             jax.ShapeDtypeStruct((PACK, patch_cols), BF),
             jax.ShapeDtypeStruct((4 * half, half), BF),
             jax.ShapeDtypeStruct((half, 4 * half), BF),
@@ -443,7 +442,7 @@
             jax.ShapeDtypeStruct((rows, pix), BF),
             jax.ShapeDtypeStruct((patch_cols, pix), BF),
         ),
-        scratch_shapes=[pltpu.VMEM((rows, pix), F32), pltpu.VMEM((rows, pix), BF)],
+        scratch_shapes=[pltpu.VMEM((rows, CHUNK), F32)] * 4 + [pltpu.VMEM((rows, pix), BF)],
         compiler_params=params(),
         cost_estimate=cost(2 * rows * pix * patch_cols, 8 * rows * pix),
         name="core_forward",
@@ -473,7 +472,7 @@
             pl.BlockSpec((8, 128), lambda i: (0, 0)),
         ),
         out_shape=(jax.ShapeDtypeStruct((rows, pooled_n), BF), jax.ShapeDtypeStruct((8, 128), F32)),
-        scratch_shapes=[pltpu.VMEM((rows, pooled_n), F32), pltpu.VMEM((frames, big), F32)],
+        scratch_shapes=[pltpu.VMEM((pooled_n, rows), F32), pltpu.VMEM((frames, big), F32)],
         compiler_params=params(),
         cost_estimate=cost(2 * work, 2 * neurons * pooled_n),
         name="readout",
@@ -483,11 +482,7 @@
     core = pl.pallas_call(
         functools.partial(core_backward_kernel, channels),
         out_shape=jax.ShapeDtypeStruct((pieces, 8, 128), F32),
-        scratch_shapes=[
-            pltpu.VMEM((rows, pix), F32),
-            pltpu.VMEM((rows, pix), BF),
-            pltpu.VMEM((rows, pix), BF),
-        ],
+        scratch_shapes=[pltpu.VMEM((rows, CHUNK), F32)] * 4 + [pltpu.VMEM((rows, pix), BF)] * 2,
         compiler_params=params(),
         cost_estimate=cost(2 * work, 8 * rows * pix),
         name="core_backward",
@@ -504,35 +499,42 @@
 
     where = lax.axis_index("clip").astype(jnp.int32)[None]
     steps = own // block
-    mask_grad, feat_grad, grad_rbias = pl.pallas_call(
-        functools.partial(owned_rows_kernel, scale),
-        grid_spec=pltpu.PrefetchScalarGridSpec(
-            num_scalar_prefetch=1,
-            grid=(steps,),
-            in_specs=[smem]
-            + [pl.BlockSpec((rows, width), lambda i, at: (0, 0)) for _ in pays]
-            + [
-                pl.BlockSpec((pooled_n, block), lambda i, at: (0, at[0] * steps + i)),
-                pl.BlockSpec((channels, block), lambda i, at: (0, at[0] * steps + i)),
-                pl.BlockSpec((1, block), lambda i, at: (0, at[0] * steps + i)),
-            ],
-            out_specs=(
-                pl.BlockSpec((pooled_n, block), lambda i, at: (0, i)),
-                pl.BlockSpec((channels, block), lambda i, at: (0, i)),
-                pl.BlockSpec((1, block), lambda i, at: (0, i)),
+
+    def owned_rows(begin, number, held):
+        whole = [pl.BlockSpec(memory_space=pl.ANY) for _ in held]
+        return pl.pallas_call(
+            functools.partial(owned_rows_kernel, scale, clip_total, steps, begin),
+            grid_spec=pltpu.PrefetchScalarGridSpec(
+                num_scalar_prefetch=1,
+                grid=(number,),
+                in_specs=[smem]
+                + [pl.BlockSpec((rows, width), lambda i, at: (0, 0)) for _ in pays]
+                + [
+                    pl.BlockSpec((pooled_n, block), lambda i, at: (0, at[0] * steps + begin + i)),
+                    pl.BlockSpec((channels, block), lambda i, at: (0, at[0] * steps + begin + i)),
+                    pl.BlockSpec((1, block), lambda i, at: (0, at[0] * steps + begin + i)),
+                ]
+                + whole,
+                out_specs=(
+                    pl.BlockSpec((pooled_n, block), lambda i, at: (0, begin + i)),
+                    pl.BlockSpec((channels, block), lambda i, at: (0, begin + i)),
+                    pl.BlockSpec((1, block), lambda i, at: (0, begin + i)),
+                ),
             ),
-        ),
-        out_shape=(
-            jax.ShapeDtypeStruct((pooled_n, own), F32),
-            jax.ShapeDtypeStruct((channels, own), F32),
-            jax.ShapeDtypeStruct((1, own), F32),
-        ),
-        compiler_params=params(),
-        cost_estimate=cost(2 * work, 4 * own * pooled_n),
-        name="owned_rows",
-    )(where, counts, *pays, mask_t, wt, rbias)
-
-    parts, mask_grad, feat_grad, grad_rbias = lax.optimization_barrier((parts, mask_grad, feat_grad, grad_rbias))
+            out_shape=(
+                jax.ShapeDtypeStruct((pooled_n, own), F32),
+                jax.ShapeDtypeStruct((channels, own), F32),
+                jax.ShapeDtypeStruct((1, own), F32),
+            ),
+            input_output_aliases={5 + clip_total + k: k for k in range(len(held))},
+            compiler_params=params(),
+            cost_estimate=cost(2 * work * number // steps, 4 * own * pooled_n),
+            name="owned_rows",
+        )(where, counts, *pays, mask_t, wt, rbias, *held)
+
+    early = max(1, steps // 2)
+    readout_grads = owned_rows(0, early, ())
+    parts, readout_grads = lax.optimization_barrier((parts, readout_grads))
     copies = pl.pallas_call(
         functools.partial(share_kernel, total),
         out_shape=jax.ShapeDtypeStruct((pieces, 8, 128), F32),
@@ -540,6 +542,10 @@
         name="share",
     )(parts)
     summed = lax.all_to_all(copies, axes, split_axis=0, concat_axis=0, tiled=True)
+    if early < steps:
+        readout_grads = owned_rows(early, steps - early, readout_grads)
+        summed, readout_grads = lax.optimization_barrier((summed, readout_grads))
+    mask_grad, feat_grad, grad_rbias = readout_grads
     grad_conv, grad_cb, grad_mix, grad_mb, loss = pl.pallas_call(
         unpack_kernel,
         out_shape=(

time: 77.8 us -> 62.3 us (0.80)
  blocking collectives: 13.3 us -> 0 us
  Pallas kernels: 45.3 us -> 35.5 us
  starting transfers between devices: 12.1 us -> 16.1 us
  waiting for transfers between devices: 5.32 us -> 8.8 us
    all_to_all x1 -> x0, blocking collectives: 13.3 us -> none  [per_device(): lax.all_to_all(copies, axes, split_axis=0, concat_axis=0, tiled=True)]
    pallas_call x1, Pallas kernels: 10.9 us -> 3.72 us  [per_device(): pl.pallas_call(core_forward_kernel, out_shape=(jax.ShapeDtypeStruct((rows...]
    pallas_call x1, Pallas kernels: 9.66 us -> 4.57 us  [per_device(): pl.pallas_call(functools.partial(core_backward_kernel, channels), out_sha...]
    all_to_all x0 -> x1, starting transfers between devices: none -> 4.03 us  [per_device(): lax.all_to_all(copies, axes, split_axis=0, concat_axis=0, tiled=True)]
    pallas_call x1 -> x2, Pallas kernels: 9.87 us -> 11.9 us  [owned_rows(): pl.pallas_call(functools.partial(owned_rows_kernel, scale, clip_total, st...]
    all_to_all x0 -> x1, waiting for transfers between devices: none -> 1.84 us  [per_device(): lax.all_to_all(copies, axes, split_axis=0, concat_axis=0, tiled=True)]
    all_to_all x1, waiting for transfers between devices: 0.01 us -> 1.64 us  [per_device(): parts = lax.all_to_all(core, axes, split_axis=0, concat_axis=0, tiled=True)]
  transfers between devices with their start and end apart: 5 -> 6, of which waited for: 1 -> 3; matrix products, arithmetic and copies ran while one was open for 0% -> 0% of each run, Pallas kernels for 41% -> 46%
where the time goes in v2:
time: 62.3 us; the launch traced here: 61.8 us
  Pallas kernels  35.5 us (57%)
  starting transfers between devices  16.1 us (26%)
  waiting for transfers between devices  8.8 us (14%)
  between operations  1.35 us (2%)
    pallas_call x2, Pallas kernels, owned_rows(): pl.pallas_call(functools.partial(owned_rows_kernel, scale, clip_total, st...  11.9 us
    pallas_call x1, Pallas kernels, per_device(): pl.pallas_call(functools.partial(readout_kernel, scale), grid=(neurons //...  10.7 us
    all_to_all x1, starting transfers between devices, per_device(): recv = lax.all_to_all(send, 'sess', split_axis=0, concat_axis=0, tiled=True)  7.28 us
    all_to_all x1, waiting for transfers between devices, per_device(): recv = lax.all_to_all(send, 'sess', split_axis=0, concat_axis=0, tiled=True)  5.31 us
    pallas_call x1, Pallas kernels, per_device(): pl.pallas_call(functools.partial(core_backward_kernel, channels), out_sha...  4.57 us
    all_to_all x1, starting transfers between devices, per_device(): lax.all_to_all(copies, axes, split_axis=0, concat_axis=0, tiled=True)  4.03 us
    pallas_call x1, Pallas kernels, per_device(): pl.pallas_call(core_forward_kernel, out_shape=(jax.ShapeDtypeStruct((rows...  3.72 us
    all_to_all x1, starting transfers between devices, per_device(): parts = lax.all_to_all(core, axes, split_axis=0, concat_axis=0, tiled=True)  2.75 us
  transfers between devices with their start and end apart: 6, of which 3 were waited for; matrix products, arithmetic and copies ran while one was open for 0% of the time, Pallas kernels for 46%

profile of v2, /device:TPU:0, one launch (start us, length us, event | category | flops | bytes accessed | tf_op | source)
XLA Modules:
  0.0 61.8 jit_solution(12969270974532060773)
XLA Ops:
  0.6 1.8 %select.1 = bf16[8,16,512]{2,1,0:T(8,128)(2,1)} custom-call(s32[1,8]{1,0:T(1,128)} %bitcast.31, bf16[8,2304]{1,0:T(8,128)(2,1)} %bitcast.30, bf16[8,4096]{1,0:T(8,128)(2,1)} %bitcast.29), custom_call_target="tpu_custom_call" | custom-call | tf_op jit(solution)/shard_map/select/pallas_call | solution.py:404
  2.5 7.3 %all-to-all-start = ((bf16[8,16,512]{2,1,0:T(8,128)(2,1)}), bf16[8,16,512]{2,1,0:T(8,128)(2,1)S(1)}, u32[]{:S(2)}, u32[]{:S(2)}) async-start(bf16[8,16,512]{2,1,0:T(8,128)(2,1)} %select.1), calls=%async_computation | async-start | bytes 262144 | tf_op jit(solution)/shard_map/all_to_all | solution.py:410
  10.4 1.4 %prep.1 = (bf16[512,448]{1,0:T(8,128)(2,1)S(1)}, bf16[256,256]{1,0:T(8,128)(2,1)S(1)}, bf16[256,256]{1,0:T(8,128)(2,1)S(1)}, f32[2,64,128]{2,1,0:T(8,128)S(1)}, ...) custom-call(bf16[64,147]{1,0:T(8,128)(2,1)} %weight.1, f32[1,64]{1,0:T(1,128)} %bitcast.32, ...), custom_call_target="tpu_custom_call" | custom-call | flops 134217728 | bytes 1048576 | tf_op jit(solution)/shard_map/prep/pallas_call | solution.py:415
  11.8 5.3 %all-to-all-done.recv = bf16[8,16,512]{2,1,0:T(8,128)(2,1)S(1)} async-done(((bf16[8,16,512]{2,1,0:T(8,128)(2,1)}), bf16[8,16,512]{2,1,0:T(8,128)(2,1)S(1)}, u32[]{:S(2)}, u32[]{:S(2)}) %all-to-all-start) | async-done | bytes 131104 | tf_op jit(solution)/shard_map/all_to_all | solution.py:410
  17.1 3.7 %core_forward.1 = (bf16[512,640]{1,0:T(8,128)(2,1)S(1)}, f32[8,4096]{1,0:T(8,128)S(1)}, bf16[512,2304]{1,0:T(8,128)(2,1)S(1)}, bf16[512,2304]{1,0:T(8,128)(2,1)S...) custom-call(bf16[8,16,512]{2,1,0:T(8,128)(2,1)S(1)} %all-to-all-done.recv, ...), custom_call_target="tpu_custom_call" | custom-call | flops 1056964608 | bytes 9437184 | tf_op jit(solution)/shard_map/core_forward/pallas_call | solution.py:435
  20.8 1.6 %collective-permute-start = (bf16[512,640]{1,0:T(8,128)(2,1)S(1)}, bf16[512,640]{1,0:T(8,128)(2,1)S(1)}, u32[]{:S(2)}, u32[]{:S(2)}) collective-permute-start(bf16[512,640]{1,0:T(8,128)(2,1)S(1)} %get-tuple-element.48.pay.refs_0_), channel_id=1, source_target_pairs={{0,16},{8,24},{16,0},{24,8},{1,17},{9,25},{17,1},{25,9},{2,18},{10... | collective-permute-start | bytes 1966088 | tf_op jit(solution)/shard_map/ppermute | solution.py:454
  22.4 0.0 collective-permute-start.1
  22.4 10.7 %readout.1 = (bf16[512,576]{1,0:T(8,128)(2,1)S(1)}, f32[8,128]{1,0:T(8,128)S(1)}) custom-call(s32[1]{0:T(128)S(6)} %copy.25.count, f32[8,4096]{1,0:T(8,128)S(1)} %get-tuple-element.49.target, bf16[512,640]{1,0:T(8,128)(2,1)S(1)} %get-tuple-element.48.pay.refs_0_, bf16[576,4096]{1,0:T(8,128)(2,1)} %bitcast.21, bf16[64,4096]{1,0:T(8,128)(2,1)} %bitcast.25, ...), custom_call_target="tpu_custom_call" | custom-call | flops 4831838208 | bytes 4718592 | tf_op jit(solution)/shard_map/readout/pallas_call | solution.py:459
  33.1 4.6 %core_backward.1 = f32[32,8,128]{2,1,0:T(8,128)} custom-call(bf16[512,576]{1,0:T(8,128)(2,1)S(1)} %get-tuple-element.50.pooled_grad, f32[8,128]{1,0:T(8,128)S(1)} %get-tuple-element.51.loss, bf16[512,2304]{1,0:T(8,128)(2,1)S(1)} %get-tuple-element.52.act1, bf16[512,2304]{1,0:T(8,128)(2,1)S(1)} %get-tuple-element.53.slope1, ...), custom_call_target="tpu_custom_call" | custom-call | flops 4831838208 | bytes 9437184 | tf_op jit(solution)/shard_map/core_backward/pallas_call | solution.py:482
  37.7 0.0 collective-permute-done.refs_2_
  37.7 0.4 collective-permute-start.2
  38.1 2.7 %all-to-all-start.1 = ((f32[32,8,128]{2,1,0:T(8,128)}), f32[32,8,128]{2,1,0:T(8,128)S(1)}, u32[]{:S(2)}, u32[]{:S(2)}) async-start(f32[32,8,128]{2,1,0:T(8,128)} %core_backward.1), calls=%async_computation.1 | async-start | bytes 262144 | tf_op jit(solution)/shard_map/all_to_all | solution.py:498
  40.9 0.0 collective-permute-done.1.refs_1_
  40.9 0.0 collective-permute-done.2.refs_3_
  40.9 6.0 %owned_rows.2 = (f32[576,1024]{1,0:T(8,128)}, f32[64,1024]{1,0:T(8,128)}, f32[1,1024]{1,0:T(1,128)}) custom-call(s32[1]{0:T(128)} %bitcast.9.where, s32[1]{0:T(128)S(6)} %copy.25.count, bf16[512,640]{1,0:T(8,128)(2,1)S(1)} %get-tuple-element.48.pay.refs_0_, bf16[512,640]{1,0:T(8,128)(2,1)S(1)} %collective-permute-done.1.refs_1_, ...), custom_call_target="tpu_custom_call" | custom-call | flops 2415919104 | bytes 2359296 | tf_op jit(solution)/shard_map/owned_rows/pallas_call | solution.py:505
  46.9 1.6 %all-to-all-done.1.parts = f32[32,8,128]{2,1,0:T(8,128)S(1)} async-done(((f32[32,8,128]{2,1,0:T(8,128)}), f32[32,8,128]{2,1,0:T(8,128)S(1)}, u32[]{:S(2)}, u32[]{:S(2)}) %all-to-all-start.1) | async-done | bytes 131104 | tf_op jit(solution)/shard_map/all_to_all | solution.py:498
  48.5 0.7 %share.1 = f32[32,8,128]{2,1,0:T(8,128)} custom-call(f32[32,8,128]{2,1,0:T(8,128)S(1)} %all-to-all-done.1.parts), custom_call_target="tpu_custom_call" | custom-call | tf_op jit(solution)/shard_map/share/pallas_call | solution.py:538
  49.2 4.0 %all-to-all-start.2 = ((f32[32,8,128]{2,1,0:T(8,128)}), f32[32,8,128]{2,1,0:T(8,128)S(1)}, u32[]{:S(2)}, u32[]{:S(2)}) async-start(f32[32,8,128]{2,1,0:T(8,128)} %share.1), calls=%async_computation.2 | async-start | bytes 262144 | tf_op jit(solution)/shard_map/all_to_all | solution.py:544
  53.2 6.0 %owned_rows.3 = (f32[576,1024]{1,0:T(8,128)}, f32[64,1024]{1,0:T(8,128)}, f32[1,1024]{1,0:T(1,128)}) custom-call(s32[1]{0:T(128)} %bitcast.9.where, s32[1]{0:T(128)S(6)} %copy.25.count, bf16[512,640]{1,0:T(8,128)(2,1)S(1)} %get-tuple-element.48.pay.refs_0_, ...), custom_call_target="tpu_custom_call", output_to_operand_aliasing={{0}: (9, {}), {1}: (10, {}), {2}: (11, {})} | custom-call | flops 2415919104 | bytes 2359296 | tf_op jit(solution)/shard_map/owned_rows/pallas_call | solution.py:505
  59.2 1.8 %all-to-all-done.2.parts = f32[32,8,128]{2,1,0:T(8,128)S(1)} async-done(((f32[32,8,128]{2,1,0:T(8,128)}), f32[32,8,128]{2,1,0:T(8,128)S(1)}, u32[]{:S(2)}, u32[]{:S(2)}) %all-to-all-start.2) | async-done | bytes 131104 | tf_op jit(solution)/shard_map/all_to_all | solution.py:544
  61.1 0.7 %unpack.1 = (f32[64,147]{1,0:T(8,128)}, f32[1,64]{1,0:T(1,128)}, f32[64,64]{1,0:T(8,128)}, f32[1,64]{1,0:T(1,128)}, f32[1,1]{1,0:T(1,128)}) custom-call(f32[32,8,128]{2,1,0:T(8,128)S(1)} %all-to-all-done.2.parts), custom_call_target="tpu_custom_call" | custom-call | tf_op jit(solution)/shard_map/unpack/pallas_call | solution.py:549
Async XLA Ops:
  2.5 14.6 %all-to-all-start = ((bf16[8,16,512]{2,1,0:T(8,128)(2,1)}), bf16[8,16,512]{2,1,0:T(8,128)(2,1)S(1)}, u32[]{:S(2)}, u32[]{:S(2)}) async-start(bf16[8,16,512]{2,1,0:T(8,128)(2,1)} %select.1), calls=%async_computation | async-start | bytes 262144 | tf_op jit(solution)/shard_map/all_to_all | solution.py:410
  20.8 16.9 %collective-permute-start = (bf16[512,640]{1,0:T(8,128)(2,1)S(1)}, bf16[512,640]{1,0:T(8,128)(2,1)S(1)}, u32[]{:S(2)}, u32[]{:S(2)}) collective-permute-start(bf16[512,640]{1,0:T(8,128)(2,1)S(1)} %get-tuple-element.48.pay.refs_0_), channel_id=1, source_target_pairs={{0,16},{8,24},{16,0},{24,8},{1,17},{9,25},{17,1},{25,9},{2,18},{10... | collective-permute-start | bytes 1966088 | tf_op jit(solution)/shard_map/ppermute | solution.py:454
  22.4 18.5 %collective-permute-start.1 = (bf16[512,640]{1,0:T(8,128)(2,1)S(1)}, bf16[512,640]{1,0:T(8,128)(2,1)S(1)}, u32[]{:S(2)}, u32[]{:S(2)}) collective-permute-start(bf16[512,640]{1,0:T(8,128)(2,1)S(1)} %get-tuple-element.48.pay.refs_0_), channel_id=1, source_target_pairs={{0,8},{8,0},{16,24},{24,16},{1,9},{9,1},{17,25},{25,17},{2,10},{10... | collective-permute-start | bytes 1966088 | tf_op jit(solution)/shard_map/ppermute | solution.py:454
  37.7 3.2 %collective-permute-start.2 = (bf16[512,640]{1,0:T(8,128)(2,1)S(1)}, bf16[512,640]{1,0:T(8,128)(2,1)S(1)}, u32[]{:S(2)}, u32[]{:S(2)}) collective-permute-start(bf16[512,640]{1,0:T(8,128)(2,1)S(1)} %collective-permute-done.refs_2_), channel_id=1, source_target_pairs={{0,8},{8,0},{16,24},{24,16},{1,9},{9,1},{17,25},{25,17},{2,10},{10... | collective-permute-start | bytes 1966088 | tf_op jit(solution)/shard_map/ppermute | solution.py:495
  38.1 10.4 %all-to-all-start.1 = ((f32[32,8,128]{2,1,0:T(8,128)}), f32[32,8,128]{2,1,0:T(8,128)S(1)}, u32[]{:S(2)}, u32[]{:S(2)}) async-start(f32[32,8,128]{2,1,0:T(8,128)} %core_backward.1), calls=%async_computation.1 | async-start | bytes 262144 | tf_op jit(solution)/shard_map/all_to_all | solution.py:498
  49.2 11.8 %all-to-all-start.2 = ((f32[32,8,128]{2,1,0:T(8,128)}), f32[32,8,128]{2,1,0:T(8,128)S(1)}, u32[]{:S(2)}, u32[]{:S(2)}) async-start(f32[32,8,128]{2,1,0:T(8,128)} %share.1), calls=%async_computation.2 | async-start | bytes 262144 | tf_op jit(solution)/shard_map/all_to_all | solution.py:544

commit v3 on v2

--- a/solution.py
+++ b/solution.py
@@ -96,8 +96,31 @@
 
 
 def core_forward_kernel(
-    recv, wbig, blocks, bias, pool, pay, target, act1, slope1, slope2, xcol, pre0, pre1, mid0, mid1, feats
+    recv,
+    wbig,
+    blocks,
+    bias,
+    pool,
+    mask_in,
+    wt_in,
+    pay,
+    target,
+    act1,
+    slope1,
+    slope2,
+    xcol,
+    mask,
+    wt,
+    pre0,
+    pre1,
+    mid0,
+    mid1,
+    feats,
+    sems,
 ):
+    copies = [pltpu.make_async_copy(mask_in, mask, sems.at[0]), pltpu.make_async_copy(wt_in, wt, sems.at[1])]
+    for copy in copies:
+        copy.start()
     frames, _, width = recv.shape
     rows, pix = act1.shape
     channels = bias.shape[1]
@@ -176,12 +199,14 @@
         pieces += [pltpu.roll(tile, SEG, 1), tile]
     packed = jnp.concatenate(pieces, axis=0)
     pay[:, p // 4 : p // 4 + half] = jnp.where(iota((rows, half), 1) < SEG, tail, packed).astype(BF)
+    for copy in copies:
+        copy.wait()
 
 
 def drive_terms(projected, target, w, rbias, alive, scale, channels):
     frames = target.shape[0]
     sums = [
-        jnp.sum(projected[f * channels : (f + 1) * channels] * w, axis=0, keepdims=True)
+        jnp.sum(projected[f * channels : (f + 1) * channels, :] * w, axis=0, keepdims=True)
         for f in range(frames)
     ]
     drive = jnp.concatenate(sums, axis=0) + rbias
@@ -197,29 +222,38 @@
     return jnp.concatenate([grad[f : f + 1] * w for f in range(frames)], axis=0).astype(BF)
 
 
-def readout_kernel(scale, count, target, pay, mask, wt, rbias, pooled_grad, loss, acc, loss_acc):
-    i = pl.program_id(0)
-    pooled_n, block = mask.shape
+def readout_kernel(
+    scale, count, target, pay, mask, wt, rbias, pooled_grad, loss, proj0, proj1, mixed, acc
+):
+    pooled_n, neurons = mask.shape
     channels = wt.shape[0]
     frames = target.shape[0]
-
-    @pl.when(i == 0)
-    def _():
-        acc[...] = jnp.zeros_like(acc)
-        loss_acc[...] = jnp.zeros_like(loss_acc)
-
-    w = wt[...].astype(F32)
-    m = mask[...]
-    projected = dot(pay[:, 0:pooled_n], m)
-    alive = (i * block + iota((frames, block), 1)) < count[0]
-    rate, grad = drive_terms(projected, target[...], w, rbias[...], alive, scale, channels)
-    loss_acc[...] += jnp.where(alive, rate - target[...] * jnp.log(rate), 0.0)
-    acc[...] += dot(m, mixed_rows(grad, w), NT)
-
-    @pl.when(i == pl.num_programs(0) - 1)
-    def _():
-        pooled_grad[...] = acc[...].T.astype(BF)
-        loss[...] = jnp.broadcast_to(jnp.sum(loss_acc[...], keepdims=True) * scale, loss.shape)
+    proj = (proj0, proj1)
+    block = proj0.shape[1]
+    steps = neurons // block
+    pooled = pay[:, 0:pooled_n]
+    loss_sum = jnp.zeros((frames, block), F32)
+    begun = False
+    for t in range(steps + 2):
+        if t < steps:
+            proj[t % 2][...] = dot(pooled, mask[:, t * block : (t + 1) * block])
+        if 1 <= t <= steps:
+            at = slice((t - 1) * block, t * block)
+            w = wt[:, at].astype(F32)
+            goal = target[:, at]
+            alive = ((t - 1) * block + iota((frames, block), 1)) < count[0]
+            rate, grad = drive_terms(proj[(t - 1) % 2], goal, w, rbias[:, at], alive, scale, channels)
+            loss_sum = loss_sum + jnp.where(alive, rate - goal * jnp.log(rate), 0.0)
+            for f in range(frames):
+                mixed[f * channels : (f + 1) * channels, at] = (grad[f : f + 1] * w).astype(BF)
+        if t >= 2 and (t % 2 == 1 or t == steps + 1):
+            low = ((t - 2) // 2) * 2 * block
+            at = slice(low, (t - 1) * block)
+            part = dot(mask[:, at], mixed[:, at], NT)
+            acc[...] = acc[...] + part if begun else part
+            begun = True
+    pooled_grad[...] = acc[...].T.astype(BF)
+    loss[...] = jnp.broadcast_to(jnp.sum(loss_sum, keepdims=True) * scale, loss.shape)
 
 
 def core_backward_kernel(
@@ -293,28 +327,26 @@
     upper = jnp.where(low == used - 128, mix_bias_grad, upper)
     upper = jnp.where((low == used - 127) & (iota((channels, 128), 0) == 0), loss[0:1, 0:1], upper)
     upper = jnp.where(low >= channels, folded, upper)
-    tiles = channels // 8
-    out[...] = jnp.zeros_like(out)
-    for i in range(tiles):
-        out[i] = conv[8 * i : 8 * i + 8, 0:128]
-        out[tiles + i] = upper[8 * i : 8 * i + 8, :]
-
-
-def share_kernel(total, parts, out):
-    each = parts.shape[0] // total
-    for k in range(each):
-        tile = parts[k]
-        for d in range(1, total):
-            tile = tile + parts[d * each + k]
-        for d in range(total):
-            out[d * each + k] = tile
+    pieces, lines, _ = out.shape
+    both = jnp.concatenate([conv[:, 0:128], upper], axis=0)
+    for k in range(pieces):
+        out[k] = both[k * lines : (k + 1) * lines, :]
+
+
+def share_kernel(parts, out):
+    total = parts.shape[0]
+    tile = parts[0]
+    for d in range(1, total):
+        tile = tile + parts[d]
+    for d in range(total):
+        out[d] = tile
 
 
 def unpack_kernel(parts, conv, conv_bias, mix, mix_bias, loss):
     channels, taps = conv.shape
-    tiles = channels // 8
-    low = jnp.concatenate([parts[i] for i in range(tiles)], axis=0)
-    high = jnp.concatenate([parts[tiles + i] for i in range(tiles)], axis=0)
+    both = jnp.concatenate([parts[k] for k in range(parts.shape[0])], axis=0)
+    low = both[0:channels]
+    high = both[channels:]
     rest = taps - 128
     conv[...] = jnp.concatenate([low, high], axis=1)[:, 0:taps]
     mix[...] = pltpu.roll(high, 128 - channels, 1)[:, 0:channels]
@@ -324,17 +356,20 @@
     loss[...] = high[0:1, rest + 2 : rest + 3]
 
 
-def owned_rows_kernel(scale, clips, steps, begin, where, count, *refs):
+def owned_rows_kernel(scale, clips, begin, own, where, count, *refs):
     pays = refs[:clips]
-    mask, wt, rbias = refs[clips : clips + 3]
-    mask_grad, feat_grad, bias_grad = refs[-3:]
-    i = begin + pl.program_id(0)
-    pooled_n, block = mask.shape
+    wt, rbias, mask = refs[clips : clips + 3]
+    outs = refs[-8:-5]
+    stage = refs[-5:-2]
+    mask_part, sems = refs[-2:]
+    pooled_n, block = stage[0].shape
     channels = wt.shape[0]
     frames = pays[0].shape[0] // channels
-    first = (where[0] * steps + i) * block
-    m = mask[...]
-    w = wt[...].astype(F32)
+    first = pl.multiple_of(where[0] * own + begin, block)
+    fetch = pltpu.make_async_copy(mask.at[:, pl.ds(first, block)], mask_part, sems.at[3])
+    fetch.start()
+    w = wt[:, pl.ds(first, block)].astype(F32)
+    add = rbias[:, pl.ds(first, block)]
     alive = (first + iota((frames, block), 1)) < count[0]
     total = None
     feat = jnp.zeros((channels, block), F32)
@@ -342,6 +377,8 @@
     segs = block // SEG
     base = pl.multiple_of(first // SEG * frames, segs * frames)
     low = iota((frames, 128), 1) < SEG
+    fetch.wait()
+    m = mask_part[...]
     for pay in pays:
         pooled = pay[:, 0:pooled_n]
         held = pay[pl.ds(base, segs * frames), pooled_n - SEG : pooled_n + SEG].astype(F32)
@@ -352,18 +389,26 @@
             tiles.append(jnp.where(low, pltpu.roll(even, SEG, 1), odd))
         target = jnp.concatenate(tiles, axis=1)
         projected = dot(pooled, m)
-        _, grad = drive_terms(projected, target, w, rbias[...], alive, scale, channels)
+        _, grad = drive_terms(projected, target, w, add, alive, scale, channels)
         for f in range(frames):
             feat = feat + grad[f : f + 1] * projected[f * channels : (f + 1) * channels]
         bias = bias + grad
         part = dot(pooled, mixed_rows(grad, w), TN)
         total = part if total is None else total + part
-    mask_grad[...] = total
-    feat_grad[...] = feat
-    bias_grad[...] = jnp.sum(bias, axis=0, keepdims=True)
-
-
-def params(limit=40):
+    stage[0][...] = total
+    stage[1][...] = feat
+    stage[2][...] = jnp.sum(bias, axis=0, keepdims=True)
+    copies = [
+        pltpu.make_async_copy(src, dst.at[:, begin : begin + block], sems.at[k])
+        for k, (src, dst) in enumerate(zip(stage, outs))
+    ]
+    for copy in copies:
+        copy.start()
+    for copy in copies:
+        copy.wait()
+
+
+def params(limit=20):
     return pltpu.CompilerParams(vmem_limit_bytes=limit << 20)
 
 
@@ -432,7 +477,10 @@
     mask_t = jnp.swapaxes(masks, 1, 2).reshape(pooled_n, neurons)
     mask_t, wt, rbias = in_hbm(mask_t, wt, readout_bias)
     width = pooled_n + SEG
-    pay, target, act1, slope1, slope2, xcol = pl.pallas_call(
+    vmem = pl.BlockSpec(memory_space=pltpu.VMEM)
+    anywhere = pl.BlockSpec(memory_space=pl.ANY)
+    smem = pl.BlockSpec(memory_space=pltpu.SMEM)
+    pay, target, act1, slope1, slope2, xcol, mask_v, wt_v = pl.pallas_call(
         core_forward_kernel,
         out_shape=(
             jax.ShapeDtypeStruct((rows, width), BF),
@@ -441,47 +489,41 @@
             jax.ShapeDtypeStruct((rows, pix), BF),
             jax.ShapeDtypeStruct((rows, pix), BF),
             jax.ShapeDtypeStruct((patch_cols, pix), BF),
+            jax.ShapeDtypeStruct((pooled_n, neurons), BF),
+            jax.ShapeDtypeStruct((channels, neurons), BF),
         ),
-        scratch_shapes=[pltpu.VMEM((rows, CHUNK), F32)] * 4 + [pltpu.VMEM((rows, pix), BF)],
+        in_specs=[vmem] * 5 + [anywhere] * 2,
+        scratch_shapes=[pltpu.VMEM((rows, CHUNK), F32)] * 4
+        + [pltpu.VMEM((rows, pix), BF), pltpu.SemaphoreType.DMA((2,))],
         compiler_params=params(),
         cost_estimate=cost(2 * rows * pix * patch_cols, 8 * rows * pix),
         name="core_forward",
-    )(recv, wbig, blocks, bias, pool)
+    )(recv, wbig, blocks, bias, pool, mask_t, wt)
 
     near = {0: pay}
     for mask in range(1, clip_total):
         if mask % 2 == 0 or mask == 1:
             near[mask] = lax.ppermute(pay, "clip", xor_pairs(clip_total, mask))
 
-    smem = pl.BlockSpec(memory_space=pltpu.SMEM)
     big = min(512, neurons)
     work = 2 * rows * neurons * pooled_n
+    where = lax.axis_index("clip").astype(jnp.int32)[None]
     pooled_grad, loss = pl.pallas_call(
         functools.partial(readout_kernel, scale),
-        grid=(neurons // big,),
-        in_specs=[
-            smem,
-            pl.BlockSpec((frames, big), lambda i: (0, i)),
-            pl.BlockSpec((rows, width), lambda i: (0, 0)),
-            pl.BlockSpec((pooled_n, big), lambda i: (0, i)),
-            pl.BlockSpec((channels, big), lambda i: (0, i)),
-            pl.BlockSpec((1, big), lambda i: (0, i)),
-        ],
-        out_specs=(
-            pl.BlockSpec((rows, pooled_n), lambda i: (0, 0)),
-            pl.BlockSpec((8, 128), lambda i: (0, 0)),
-        ),
+        in_specs=[smem] + [vmem] * 5,
         out_shape=(jax.ShapeDtypeStruct((rows, pooled_n), BF), jax.ShapeDtypeStruct((8, 128), F32)),
-        scratch_shapes=[pltpu.VMEM((pooled_n, rows), F32), pltpu.VMEM((frames, big), F32)],
+        scratch_shapes=[pltpu.VMEM((rows, big), F32)] * 2
+        + [pltpu.VMEM((rows, neurons), BF), pltpu.VMEM((pooled_n, rows), F32)],
         compiler_params=params(),
         cost_estimate=cost(2 * work, 2 * neurons * pooled_n),
         name="readout",
-    )(counts, target, pay, mask_t, wt, rbias)
-
-    pieces = total * max(1, (2 * channels // 8) // total)
+    )(counts, target, pay, mask_v, wt_v, rbias)
+
+    assert 2 * channels % total == 0
+    pieces = (total, 2 * channels // total, 128)
     core = pl.pallas_call(
         functools.partial(core_backward_kernel, channels),
-        out_shape=jax.ShapeDtypeStruct((pieces, 8, 128), F32),
+        out_shape=jax.ShapeDtypeStruct(pieces, F32),
         scratch_shapes=[pltpu.VMEM((rows, CHUNK), F32)] * 4 + [pltpu.VMEM((rows, pix), BF)] * 2,
         compiler_params=params(),
         cost_estimate=cost(2 * work, 8 * rows * pix),
@@ -497,53 +539,44 @@
     axes = ("clip", "sess")
     parts = lax.all_to_all(core, axes, split_axis=0, concat_axis=0, tiled=True)
 
-    where = lax.axis_index("clip").astype(jnp.int32)[None]
-    steps = own // block
-
-    def owned_rows(begin, number, held):
-        whole = [pl.BlockSpec(memory_space=pl.ANY) for _ in held]
+    def owned_rows(begin, held):
         return pl.pallas_call(
-            functools.partial(owned_rows_kernel, scale, clip_total, steps, begin),
-            grid_spec=pltpu.PrefetchScalarGridSpec(
-                num_scalar_prefetch=1,
-                grid=(number,),
-                in_specs=[smem]
-                + [pl.BlockSpec((rows, width), lambda i, at: (0, 0)) for _ in pays]
-                + [
-                    pl.BlockSpec((pooled_n, block), lambda i, at: (0, at[0] * steps + begin + i)),
-                    pl.BlockSpec((channels, block), lambda i, at: (0, at[0] * steps + begin + i)),
-                    pl.BlockSpec((1, block), lambda i, at: (0, at[0] * steps + begin + i)),
-                ]
-                + whole,
-                out_specs=(
-                    pl.BlockSpec((pooled_n, block), lambda i, at: (0, begin + i)),
-                    pl.BlockSpec((channels, block), lambda i, at: (0, begin + i)),
-                    pl.BlockSpec((1, block), lambda i, at: (0, begin + i)),
-                ),
-            ),
-            out_shape=(
+            functools.partial(owned_rows_kernel, scale, clip_total, begin, own),
+            in_specs=[smem, smem] + [vmem] * (clip_total + 2) + [anywhere] * (1 + len(held)),
+            out_specs=[anywhere] * 3,
+            out_shape=[
                 jax.ShapeDtypeStruct((pooled_n, own), F32),
                 jax.ShapeDtypeStruct((channels, own), F32),
                 jax.ShapeDtypeStruct((1, own), F32),
-            ),
+            ],
             input_output_aliases={5 + clip_total + k: k for k in range(len(held))},
+            scratch_shapes=[
+                pltpu.VMEM((pooled_n, block), F32),
+                pltpu.VMEM((channels, block), F32),
+                pltpu.VMEM((1, block), F32),
+                pltpu.VMEM((pooled_n, block), BF),
+                pltpu.SemaphoreType.DMA((4,)),
+            ],
             compiler_params=params(),
-            cost_estimate=cost(2 * work * number // steps, 4 * own * pooled_n),
+            cost_estimate=cost(2 * work * block // own, 4 * block * pooled_n),
             name="owned_rows",
-        )(where, counts, *pays, mask_t, wt, rbias, *held)
-
-    early = max(1, steps // 2)
-    readout_grads = owned_rows(0, early, ())
+        )(where, counts, *pays, wt_v, rbias, mask_t, *held)
+
+    readout_grads = ()
+    early = max(block, own // 2)
+    for begin in range(0, early, block):
+        readout_grads = owned_rows(begin, readout_grads)
     parts, readout_grads = lax.optimization_barrier((parts, readout_grads))
     copies = pl.pallas_call(
-        functools.partial(share_kernel, total),
-        out_shape=jax.ShapeDtypeStruct((pieces, 8, 128), F32),
+        share_kernel,
+        out_shape=jax.ShapeDtypeStruct(pieces, F32),
         compiler_params=params(),
         name="share",
     )(parts)
     summed = lax.all_to_all(copies, axes, split_axis=0, concat_axis=0, tiled=True)
-    if early < steps:
-        readout_grads = owned_rows(early, steps - early, readout_grads)
+    if early < own:
+        for begin in range(early, own, block):
+            readout_grads = owned_rows(begin, readout_grads)
         summed, readout_grads = lax.optimization_barrier((summed, readout_grads))
     mask_grad, feat_grad, grad_rbias = readout_grads
     grad_conv, grad_cb, grad_mix, grad_mb, loss = pl.pallas_call(

time: 62.3 us -> 63 us (1.011)
  starting transfers between devices: 16.1 us -> 17 us
    pallas_call x4, Pallas kernels: 23.3 us -> 20.8 us  [the longest x2 13.4 us: owned_rows(): pl.pallas_call(functools.partial(owned_rows_kernel, scale, clip_total, be...]
    pallas_call x1, Pallas kernels: 3.72 us -> 6.1 us  [per_device(): pl.pallas_call(core_forward_kernel, out_shape=(jax.ShapeDtypeStruct((rows...]
    ppermute x2, waiting for transfers between devices: 0.01 us -> 1.97 us  [per_device(): near[mask] = lax.ppermute(pay, 'clip', xor_pairs(clip_total, mask))]
    all_to_all x1, waiting for transfers between devices: 1.84 us -> 0.56 us  [per_device(): lax.all_to_all(copies, axes, split_axis=0, concat_axis=0, tiled=True)]
    all_to_all x1, starting transfers between devices: 4.03 us -> 5.29 us  [per_device(): lax.all_to_all(copies, axes, split_axis=0, concat_axis=0, tiled=True)]
    all_to_all x1, waiting for transfers between devices: 1.64 us -> 0.55 us  [per_device(): parts = lax.all_to_all(core, axes, split_axis=0, concat_axis=0, tiled=True)]
  transfers between devices with their start and end apart: 6 -> 6, of which waited for: 3 -> 4; matrix products, arithmetic and copies ran while one was open for 0% -> 0% of each run, Pallas kernels for 46% -> 42%
where the time goes in v3:
time: 63 us; the launch traced here: 62.4 us
  Pallas kernels  35.6 us (57%)
  starting transfers between devices  17 us (27%)
  waiting for transfers between devices  8.39 us (13%)
  between operations  1.36 us (2%)
    pallas_call x2, Pallas kernels, owned_rows(): pl.pallas_call(functools.partial(owned_rows_kernel, scale, clip_total, be...  13.4 us
    all_to_all x1, starting transfers between devices, per_device(): recv = lax.all_to_all(send, 'sess', split_axis=0, concat_axis=0, tiled=True)  7.28 us
    pallas_call x1, Pallas kernels, per_device(): pl.pallas_call(functools.partial(readout_kernel, scale), in_specs=[smem]...  6.73 us
    pallas_call x1, Pallas kernels, per_device(): pl.pallas_call(core_forward_kernel, out_shape=(jax.ShapeDtypeStruct((rows...  6.1 us
    all_to_all x1, waiting for transfers between devices, per_device(): recv = lax.all_to_all(send, 'sess', split_axis=0, concat_axis=0, tiled=True)  5.31 us
    all_to_all x1, starting transfers between devices, per_device(): lax.all_to_all(copies, axes, split_axis=0, concat_axis=0, tiled=True)  5.29 us
    pallas_call x1, Pallas kernels, per_device(): pl.pallas_call(functools.partial(core_backward_kernel, channels), out_sha...  4.81 us
    all_to_all x1, starting transfers between devices, per_device(): parts = lax.all_to_all(core, axes, split_axis=0, concat_axis=0, tiled=True)  2.81 us
  transfers between devices with their start and end apart: 6, of which 4 were waited for; matrix products, arithmetic and copies ran while one was open for 0% of the time, Pallas kernels for 42%

profile of v3, /device:TPU:0, one launch (start us, length us, event | category | flops | bytes accessed | tf_op | source)
XLA Modules:
  0.0 62.4 jit_solution(6912655239046318305)
XLA Ops:
  0.6 1.8 %select.1 = bf16[8,16,512]{2,1,0:T(8,128)(2,1)} custom-call(s32[1,8]{1,0:T(1,128)} %bitcast.29, bf16[8,2304]{1,0:T(8,128)(2,1)} %bitcast.28, bf16[8,4096]{1,0:T(8,128)(2,1)} %bitcast.27), custom_call_target="tpu_custom_call" | custom-call | tf_op jit(solution)/shard_map/select/pallas_call | solution.py:449
  2.5 7.3 %all-to-all-start = ((bf16[8,16,512]{2,1,0:T(8,128)(2,1)}), bf16[8,16,512]{2,1,0:T(8,128)(2,1)S(1)}, u32[]{:S(2)}, u32[]{:S(2)}) async-start(bf16[8,16,512]{2,1,0:T(8,128)(2,1)} %select.1), calls=%async_computation | async-start | bytes 262144 | tf_op jit(solution)/shard_map/all_to_all | solution.py:455
  10.4 1.4 %prep.1 = (bf16[512,448]{1,0:T(8,128)(2,1)S(1)}, bf16[256,256]{1,0:T(8,128)(2,1)S(1)}, bf16[256,256]{1,0:T(8,128)(2,1)S(1)}, f32[2,64,128]{2,1,0:T(8,128)S(1)}, ...) custom-call(bf16[64,147]{1,0:T(8,128)(2,1)} %weight.1, f32[1,64]{1,0:T(1,128)} %bitcast.30, ...), custom_call_target="tpu_custom_call" | custom-call | flops 134217728 | bytes 1048576 | tf_op jit(solution)/shard_map/prep/pallas_call | solution.py:460
  11.8 5.3 %all-to-all-done.recv = bf16[8,16,512]{2,1,0:T(8,128)(2,1)S(1)} async-done(((bf16[8,16,512]{2,1,0:T(8,128)(2,1)}), bf16[8,16,512]{2,1,0:T(8,128)(2,1)S(1)}, u32[]{:S(2)}, u32[]{:S(2)}) %all-to-all-start) | async-done | bytes 131104 | tf_op jit(solution)/shard_map/all_to_all | solution.py:455
  17.1 6.1 %core_forward.1 = (bf16[512,640]{1,0:T(8,128)(2,1)S(1)}, f32[8,4096]{1,0:T(8,128)S(1)}, bf16[512,2304]{1,0:T(8,128)(2,1)S(1)}, bf16[512,2304]{1,0:T(8,128)(2,1)S...) custom-call(bf16[8,16,512]{2,1,0:T(8,128)(2,1)S(1)} %all-to-all-done, ...), custom_call_target="tpu_custom_call" | custom-call | flops 1056964608 | bytes 9437184 | tf_op jit(solution)/shard_map/core_forward/pallas_call | solution.py:483
  23.2 1.6 %collective-permute-start = (bf16[512,640]{1,0:T(8,128)(2,1)S(1)}, bf16[512,640]{1,0:T(8,128)(2,1)S(1)}, u32[]{:S(2)}, u32[]{:S(2)}) collective-permute-start(bf16[512,640]{1,0:T(8,128)(2,1)S(1)} %get-tuple-element.50.pay.refs_0_), channel_id=1, source_target_pairs={{0,16},{8,24},{16,0},{24,8},{1,17},{9,25},{17,1},{25,9},{2,18},{10... | collective-permute-start | bytes 1966088 | tf_op jit(solution)/shard_map/ppermute | solution.py:506
  24.8 0.0 collective-permute-start.1
  24.8 6.7 %readout.1 = (bf16[512,576]{1,0:T(8,128)(2,1)S(1)}, f32[8,128]{1,0:T(8,128)S(1)}) custom-call(s32[1]{0:T(128)S(6)} %copy.25.count, f32[8,4096]{1,0:T(8,128)S(1)} %get-tuple-element.51.target, bf16[512,640]{1,0:T(8,128)(2,1)S(1)} %get-tuple-element.50.pay.refs_0_, bf16[576,4096]{1,0:T(8,128)(2,1)S(1)} %get-tuple-element.52.mask, ...), custom_call_target="tpu_custom_call" | custom-call | flops 4831838208 | bytes 4718592 | tf_op jit(solution)/shard_map/readout/pallas_call | solution.py:511
  31.5 4.8 %core_backward.1 = f32[32,4,128]{2,1,0:T(4,128)} custom-call(bf16[512,576]{1,0:T(8,128)(2,1)S(1)} %get-tuple-element.54.pooled_grad, f32[8,128]{1,0:T(8,128)S(1)} %get-tuple-element.55.loss, bf16[512,2304]{1,0:T(8,128)(2,1)S(1)} %get-tuple-element.56.act1, bf16[512,2304]{1,0:T(8,128)(2,1)S(1)} %get-tuple-element.57.slope1, ...), custom_call_target="tpu_custom_call" | custom-call | flops 4831838208 | bytes 9437184 | tf_op jit(solution)/shard_map/core_backward/pallas_call | solution.py:524
  36.3 2.0 %collective-permute-done.refs_2_ = bf16[512,640]{1,0:T(8,128)(2,1)S(1)} collective-permute-done((bf16[512,640]{1,0:T(8,128)(2,1)S(1)}, bf16[512,640]{1,0:T(8,128)(2,1)S(1)}, u32[]{:S(2)}, u32[]{:S(2)}) %collective-permute-start) | collective-permute-done | bytes 655392 | tf_op jit(solution)/shard_map/ppermute | solution.py:506
  38.3 0.0 collective-permute-start.2
  38.3 2.8 %all-to-all-start.1 = ((f32[32,4,128]{2,1,0:T(4,128)}), f32[32,4,128]{2,1,0:T(4,128)S(1)}, u32[]{:S(2)}, u32[]{:S(2)}) async-start(f32[32,4,128]{2,1,0:T(4,128)} %core_backward.1), calls=%async_computation.1 | async-start | bytes 131072 | tf_op jit(solution)/shard_map/all_to_all | solution.py:540
  41.1 0.0 collective-permute-done.1.refs_1_
  41.1 0.0 collective-permute-done.2.refs_3_
  41.2 6.7 %owned_rows.2 = (f32[576,1024]{1,0:T(8,128)}, f32[64,1024]{1,0:T(8,128)}, f32[1,1024]{1,0:T(1,128)}) custom-call(s32[1]{0:T(128)} %bitcast.9.where, s32[1]{0:T(128)S(6)} %copy.25.count, bf16[512,640]{1,0:T(8,128)(2,1)S(1)} %get-tuple-element.50.pay.refs_0_, bf16[512,640]{1,0:T(8,128)(2,1)S(1)} %collective-permute-done.1.refs_1_, ...), custom_call_target="tpu_custom_call" | custom-call | flops 2415919104 | bytes 1179648 | tf_op jit(solution)/shard_map/owned_rows/pallas_call | solution.py:543
  47.9 0.6 all-to-all-done.1.parts
  48.4 0.7 %share.1 = f32[32,4,128]{2,1,0:T(4,128)} custom-call(f32[32,4,128]{2,1,0:T(4,128)S(1)} %all-to-all-done.1.parts), custom_call_target="tpu_custom_call" | custom-call | tf_op jit(solution)/shard_map/share/pallas_call | solution.py:570
  49.1 5.3 %all-to-all-start.2 = ((f32[32,4,128]{2,1,0:T(4,128)}), f32[32,4,128]{2,1,0:T(4,128)S(1)}, u32[]{:S(2)}, u32[]{:S(2)}) async-start(f32[32,4,128]{2,1,0:T(4,128)} %share.1), calls=%async_computation.2 | async-start | bytes 131072 | tf_op jit(solution)/shard_map/all_to_all | solution.py:576
  54.4 6.7 %owned_rows.3 = (f32[576,1024]{1,0:T(8,128)}, f32[64,1024]{1,0:T(8,128)}, f32[1,1024]{1,0:T(1,128)}) custom-call(s32[1]{0:T(128)} %bitcast.9.where, s32[1]{0:T(128)S(6)} %copy.25.count, bf16[512,640]{1,0:T(8,128)(2,1)S(1)} %get-tuple-element.50.pay.refs_0_, ...), custom_call_target="tpu_custom_call", output_to_operand_aliasing={{0}: (9, {}), {1}: (10, {}), {2}: (11, {})} | custom-call | flops 2415919104 | bytes 1179648 | tf_op jit(solution)/shard_map/owned_rows/pallas_call | solution.py:543
  61.1 0.6 all-to-all-done.2.parts
  61.7 0.7 %unpack.1 = (f32[64,147]{1,0:T(8,128)}, f32[1,64]{1,0:T(1,128)}, f32[64,64]{1,0:T(8,128)}, f32[1,64]{1,0:T(1,128)}, f32[1,1]{1,0:T(1,128)}) custom-call(f32[32,4,128]{2,1,0:T(4,128)S(1)} %all-to-all-done.2.parts), custom_call_target="tpu_custom_call" | custom-call | tf_op jit(solution)/shard_map/unpack/pallas_call | solution.py:582
Async XLA Ops:
  2.5 14.6 %all-to-all-start = ((bf16[8,16,512]{2,1,0:T(8,128)(2,1)}), bf16[8,16,512]{2,1,0:T(8,128)(2,1)S(1)}, u32[]{:S(2)}, u32[]{:S(2)}) async-start(bf16[8,16,512]{2,1,0:T(8,128)(2,1)} %select.1), calls=%async_computation | async-start | bytes 262144 | tf_op jit(solution)/shard_map/all_to_all | solution.py:455
  23.2 15.1 %collective-permute-start = (bf16[512,640]{1,0:T(8,128)(2,1)S(1)}, bf16[512,640]{1,0:T(8,128)(2,1)S(1)}, u32[]{:S(2)}, u32[]{:S(2)}) collective-permute-start(bf16[512,640]{1,0:T(8,128)(2,1)S(1)} %get-tuple-element.50.pay.refs_0_), channel_id=1, source_target_pairs={{0,16},{8,24},{16,0},{24,8},{1,17},{9,25},{17,1},{25,9},{2,18},{10... | collective-permute-start | bytes 1966088 | tf_op jit(solution)/shard_map/ppermute | solution.py:506
  24.8 16.4 %collective-permute-start.1 = (bf16[512,640]{1,0:T(8,128)(2,1)S(1)}, bf16[512,640]{1,0:T(8,128)(2,1)S(1)}, u32[]{:S(2)}, u32[]{:S(2)}) collective-permute-start(bf16[512,640]{1,0:T(8,128)(2,1)S(1)} %get-tuple-element.50.pay.refs_0_), channel_id=1, source_target_pairs={{0,8},{8,0},{16,24},{24,16},{1,9},{9,1},{17,25},{25,17},{2,10},{10... | collective-permute-start | bytes 1966088 | tf_op jit(solution)/shard_map/ppermute | solution.py:506
  38.3 2.8 %collective-permute-start.2 = (bf16[512,640]{1,0:T(8,128)(2,1)S(1)}, bf16[512,640]{1,0:T(8,128)(2,1)S(1)}, u32[]{:S(2)}, u32[]{:S(2)}) collective-permute-start(bf16[512,640]{1,0:T(8,128)(2,1)S(1)} %collective-permute-done.refs_2_), channel_id=1, source_target_pairs={{0,8},{8,0},{16,24},{24,16},{1,9},{9,1},{17,25},{25,17},{2,10},{10... | collective-permute-start | bytes 1966088 | tf_op jit(solution)/shard_map/ppermute | solution.py:537
  38.3 10.1 %all-to-all-start.1 = ((f32[32,4,128]{2,1,0:T(4,128)}), f32[32,4,128]{2,1,0:T(4,128)S(1)}, u32[]{:S(2)}, u32[]{:S(2)}) async-start(f32[32,4,128]{2,1,0:T(4,128)} %core_backward.1), calls=%async_computation.1 | async-start | bytes 131072 | tf_op jit(solution)/shard_map/all_to_all | solution.py:540
  49.1 12.6 %all-to-all-start.2 = ((f32[32,4,128]{2,1,0:T(4,128)}), f32[32,4,128]{2,1,0:T(4,128)S(1)}, u32[]{:S(2)}, u32[]{:S(2)}) async-start(f32[32,4,128]{2,1,0:T(4,128)} %share.1), calls=%async_computation.2 | async-start | bytes 131072 | tf_op jit(solution)/shard_map/all_to_all | solution.py:576

commit v4 on v3

--- a/solution.py
+++ b/solution.py
@@ -118,7 +118,9 @@
     feats,
     sems,
 ):
-    copies = [pltpu.make_async_copy(mask_in, mask, sems.at[0]), pltpu.make_async_copy(wt_in, wt, sems.at[1])]
+    copies = [pltpu.make_async_copy(wt_in, wt, sems.at[0])]
+    for k, r in enumerate(range(0, mask.shape[0], SEG)):
+        copies.append(pltpu.make_async_copy(mask_in.at[r : r + SEG, :], mask.at[r : r + SEG, :], sems.at[k + 1]))
     for copy in copies:
         copy.start()
     frames, _, width = recv.shape
@@ -356,56 +358,77 @@
     loss[...] = high[0:1, rest + 2 : rest + 3]
 
 
-def owned_rows_kernel(scale, clips, begin, own, where, count, *refs):
+def owned_rows_kernel(scale, clips, own, block, held, where, count, *refs):
     pays = refs[:clips]
-    wt, rbias, mask = refs[clips : clips + 3]
-    outs = refs[-8:-5]
-    stage = refs[-5:-2]
-    mask_part, sems = refs[-2:]
-    pooled_n, block = stage[0].shape
-    channels = wt.shape[0]
-    frames = pays[0].shape[0] // channels
-    first = pl.multiple_of(where[0] * own + begin, block)
-    fetch = pltpu.make_async_copy(mask.at[:, pl.ds(first, block)], mask_part, sems.at[3])
-    fetch.start()
-    w = wt[:, pl.ds(first, block)].astype(F32)
-    add = rbias[:, pl.ds(first, block)]
-    alive = (first + iota((frames, block), 1)) < count[0]
-    total = None
-    feat = jnp.zeros((channels, block), F32)
-    bias = jnp.zeros((frames, block), F32)
+    wt, rbias, mask_in = refs[clips : clips + 3]
+    channels = refs[clips].shape[0]
+    before = refs[clips + 3 : clips + 3 + held]
+    outs = refs[clips + 3 + held : -8]
+    proj0, proj1, mixed0, mixed1, turned, mask, stage, sems = refs[-8:]
+    proj = (proj0, proj1)
+    mixed = (mixed0, mixed1)
+    pooled_n = mask.shape[0]
+    low_rows = pooled_n + channels
+    rows = pays[0].shape[0]
+    frames = rows // channels
+    steps = own // block
+    first = pl.multiple_of(where[0] * own, own)
+    fetches = []
+    for k in range(steps):
+        lanes = pl.ds(pl.multiple_of(first + k * block, block), block)
+        fetches.append(pltpu.make_async_copy(mask_in.at[:, lanes], mask.at[:, k * block : (k + 1) * block], sems.at[k]))
+        fetches[k].start()
+    for c in range(clips):
+        turned[:, c * rows : (c + 1) * rows] = pays[c][:, 0:pooled_n].T
     segs = block // SEG
-    base = pl.multiple_of(first // SEG * frames, segs * frames)
     low = iota((frames, 128), 1) < SEG
-    fetch.wait()
-    m = mask_part[...]
-    for pay in pays:
-        pooled = pay[:, 0:pooled_n]
-        held = pay[pl.ds(base, segs * frames), pooled_n - SEG : pooled_n + SEG].astype(F32)
-        tiles = []
-        for j in range(0, segs, 2):
-            even = held[j * frames : (j + 1) * frames]
-            odd = held[(j + 1) * frames : (j + 2) * frames]
-            tiles.append(jnp.where(low, pltpu.roll(even, SEG, 1), odd))
-        target = jnp.concatenate(tiles, axis=1)
-        projected = dot(pooled, m)
-        _, grad = drive_terms(projected, target, w, add, alive, scale, channels)
-        for f in range(frames):
-            feat = feat + grad[f : f + 1] * projected[f * channels : (f + 1) * channels]
-        bias = bias + grad
-        part = dot(pooled, mixed_rows(grad, w), TN)
-        total = part if total is None else total + part
-    stage[0][...] = total
-    stage[1][...] = feat
-    stage[2][...] = jnp.sum(bias, axis=0, keepdims=True)
-    copies = [
-        pltpu.make_async_copy(src, dst.at[:, begin : begin + block], sems.at[k])
-        for k, (src, dst) in enumerate(zip(stage, outs))
-    ]
-    for copy in copies:
-        copy.start()
-    for copy in copies:
-        copy.wait()
+    items = [(k, c) for k in range(steps) for c in range(clips)]
+    feats = [jnp.zeros((channels, block), F32) for _ in range(steps)]
+    biases = [jnp.zeros((frames, block), F32) for _ in range(steps)]
+    stores = []
+    for t in range(len(items) + 2):
+        if t < len(items):
+            k, c = items[t]
+            if c == 0:
+                fetches[k].wait()
+            proj[t % 2][...] = dot(pays[c][:, 0:pooled_n], mask[:, k * block : (k + 1) * block])
+        if 1 <= t <= len(items):
+            k, c = items[t - 1]
+            start = pl.multiple_of(first + k * block, block)
+            base = pl.multiple_of(start // SEG * frames, segs * frames)
+            packed = pays[c][pl.ds(base, segs * frames), pooled_n - SEG : pooled_n + SEG].astype(F32)
+            tiles = []
+            for j in range(0, segs, 2):
+                even = packed[j * frames : (j + 1) * frames]
+                odd = packed[(j + 1) * frames : (j + 2) * frames]
+                tiles.append(jnp.where(low, pltpu.roll(even, SEG, 1), odd))
+            target = jnp.concatenate(tiles, axis=1)
+            w = wt[:, pl.ds(start, block)].astype(F32)
+            alive = (start + iota((frames, block), 1)) < count[0]
+            now = proj[(t - 1) % 2]
+            _, grad = drive_terms(now, target, w, rbias[:, pl.ds(start, block)], alive, scale, channels)
+            for f in range(frames):
+                feats[k] = feats[k] + grad[f : f + 1] * now[f * channels : (f + 1) * channels, :]
+                at = c * rows + f * channels
+                mixed[k % 2][at : at + channels, :] = (grad[f : f + 1] * w).astype(BF)
+            biases[k] = biases[k] + grad
+        if t >= 2 and items[t - 2][1] == clips - 1:
+            k = items[t - 2][0]
+            at = slice(k * block, (k + 1) * block)
+            total = dot(turned[...], mixed[k % 2][...])
+            bias = jnp.sum(biases[k], axis=0, keepdims=True)
+            if held:
+                stage[:, at] = total + before[0][0:pooled_n, at]
+                outs[1][:, at] = feats[k] + before[0][pooled_n:low_rows, at]
+                outs[2][:, at] = bias + before[0][low_rows : low_rows + 1, at]
+                stores.append(pltpu.make_async_copy(stage.at[:, at], outs[0].at[:, at], sems.at[steps + k]))
+                stores[-1].start()
+            else:
+                outs[0][0:pooled_n, at] = total
+                outs[0][pooled_n:low_rows, at] = feats[k]
+                outs[0][low_rows:, at] = jnp.broadcast_to(bias, (8, block))
+    for store in stores:
+        store.wait()
 
 
 def params(limit=20):
@@ -494,7 +517,7 @@
         ),
         in_specs=[vmem] * 5 + [anywhere] * 2,
         scratch_shapes=[pltpu.VMEM((rows, CHUNK), F32)] * 4
-        + [pltpu.VMEM((rows, pix), BF), pltpu.SemaphoreType.DMA((2,))],
+        + [pltpu.VMEM((rows, pix), BF), pltpu.SemaphoreType.DMA((1 + pooled_n // SEG,))],
         compiler_params=params(),
         cost_estimate=cost(2 * rows * pix * patch_cols, 8 * rows * pix),
         name="core_forward",
@@ -530,43 +553,41 @@
         name="core_backward",
     )(pooled_grad, loss, act1, slope1, slope2, xcol, blocks_t, table, unpool)
 
-    far = [mask for mask in near if mask > 1]
-    held, core = lax.optimization_barrier(([near[mask] for mask in far], core))
-    pays = [near[0], near[1]]
-    for mask, value in zip(far, held):
-        pays += [value, lax.ppermute(value, "clip", xor_pairs(clip_total, 1))]
-
     axes = ("clip", "sess")
     parts = lax.all_to_all(core, axes, split_axis=0, concat_axis=0, tiled=True)
 
-    def owned_rows(begin, held):
+    def owned_rows(clips, held):
+        last = len(held) > 0
         return pl.pallas_call(
-            functools.partial(owned_rows_kernel, scale, clip_total, begin, own),
-            in_specs=[smem, smem] + [vmem] * (clip_total + 2) + [anywhere] * (1 + len(held)),
-            out_specs=[anywhere] * 3,
+            functools.partial(owned_rows_kernel, scale, len(clips), own, block, len(held)),
+            in_specs=[smem, smem] + [vmem] * (len(clips) + 2) + [anywhere] + [vmem] * len(held),
+            out_specs=[anywhere, vmem, vmem] if last else [vmem],
             out_shape=[
                 jax.ShapeDtypeStruct((pooled_n, own), F32),
                 jax.ShapeDtypeStruct((channels, own), F32),
                 jax.ShapeDtypeStruct((1, own), F32),
-            ],
-            input_output_aliases={5 + clip_total + k: k for k in range(len(held))},
-            scratch_shapes=[
-                pltpu.VMEM((pooled_n, block), F32),
-                pltpu.VMEM((channels, block), F32),
-                pltpu.VMEM((1, block), F32),
-                pltpu.VMEM((pooled_n, block), BF),
-                pltpu.SemaphoreType.DMA((4,)),
+            ]
+            if last
+            else [jax.ShapeDtypeStruct((pooled_n + channels + 8, own), F32)],
+            scratch_shapes=[pltpu.VMEM((rows, block), F32)] * 2
+            + [pltpu.VMEM((len(clips) * rows, block), BF)] * 2
+            + [
+                pltpu.VMEM((pooled_n, len(clips) * rows), BF),
+                pltpu.VMEM((pooled_n, own), BF),
+                pltpu.VMEM((pooled_n, own) if last else (8, 128), F32),
+                pltpu.SemaphoreType.DMA((2 * (own // block),)),
             ],
             compiler_params=params(),
-            cost_estimate=cost(2 * work * block // own, 4 * block * pooled_n),
+            cost_estimate=cost(2 * work * len(clips) // clip_total, 4 * own * pooled_n),
             name="owned_rows",
-        )(where, counts, *pays, wt_v, rbias, mask_t, *held)
-
-    readout_grads = ()
-    early = max(block, own // 2)
-    for begin in range(0, early, block):
-        readout_grads = owned_rows(begin, readout_grads)
-    parts, readout_grads = lax.optimization_barrier((parts, readout_grads))
+        )(where, counts, *clips, wt_v, rbias, mask_t, *held)
+
+    readout_grads = owned_rows([near[0], near[1]], ())
+    far = [mask for mask in near if mask > 1]
+    parts, readout_grads, reached = lax.optimization_barrier((parts, readout_grads, [near[mask] for mask in far]))
+    others = []
+    for value in reached:
+        others += [value, lax.ppermute(value, "clip", xor_pairs(clip_total, 1))]
     copies = pl.pallas_call(
         share_kernel,
         out_shape=jax.ShapeDtypeStruct(pieces, F32),
@@ -574,10 +595,8 @@
         name="share",
     )(parts)
     summed = lax.all_to_all(copies, axes, split_axis=0, concat_axis=0, tiled=True)
-    if early < own:
-        for begin in range(early, own, block):
-            readout_grads = owned_rows(begin, readout_grads)
-        summed, readout_grads = lax.optimization_barrier((summed, readout_grads))
+    readout_grads = owned_rows(others, readout_grads)
+    summed, readout_grads = lax.optimization_barrier((summed, readout_grads))
     mask_grad, feat_grad, grad_rbias = readout_grads
     grad_conv, grad_cb, grad_mix, grad_mb, loss = pl.pallas_call(
         unpack_kernel,

time: 63 us -> 63.6 us (level)
  waiting for transfers between devices: 8.39 us -> 5.32 us
  local copies, waits for them, and re-layouts: 0 us -> 1.95 us
  Pallas kernels: 35.6 us -> 36.8 us
    ppermute x2, waiting for transfers between devices: 1.97 us -> 0.01 us  [per_device(): near[mask] = lax.ppermute(pay, 'clip', xor_pairs(clip_total, mask))]
    unnamed x0 -> x4, local copies, waits for them, and re-layouts: none -> 1.95 us
    pallas_call x1, Pallas kernels: 6.1 us -> 6.86 us  [per_device(): pl.pallas_call(core_forward_kernel, out_shape=(jax.ShapeDtypeStruct((rows...]
  transfers between devices with their start and end apart: 6 -> 6, of which waited for: 4 -> 1; matrix products, arithmetic and copies ran while one was open for 0% -> 0% of each run, Pallas kernels for 42% -> 44%
where the time goes in v4:
time: 63.6 us; the launch traced here: 63 us
  Pallas kernels  36.8 us (58%)
  starting transfers between devices  17.5 us (28%)
  waiting for transfers between devices  5.32 us (8%)
  local copies, waits for them, and re-layouts  1.95 us (3%)
  between operations  1.4 us (2%)
    pallas_call x2, Pallas kernels, owned_rows(): pl.pallas_call(functools.partial(owned_rows_kernel, scale, len(clips), ow...  13.5 us
    all_to_all x1, starting transfers between devices, per_device(): recv = lax.all_to_all(send, 'sess', split_axis=0, concat_axis=0, tiled=True)  7.28 us
    pallas_call x1, Pallas kernels, per_device(): pl.pallas_call(functools.partial(readout_kernel, scale), in_specs=[smem]...  7.14 us
    pallas_call x1, Pallas kernels, per_device(): pl.pallas_call(core_forward_kernel, out_shape=(jax.ShapeDtypeStruct((rows...  6.86 us
    all_to_all x1, starting transfers between devices, per_device(): lax.all_to_all(copies, axes, split_axis=0, concat_axis=0, tiled=True)  5.84 us
    all_to_all x1, waiting for transfers between devices, per_device(): recv = lax.all_to_all(send, 'sess', split_axis=0, concat_axis=0, tiled=True)  5.31 us
    pallas_call x1, Pallas kernels, per_device(): pl.pallas_call(functools.partial(core_backward_kernel, channels), out_sha...  4.77 us
    all_to_all x1, starting transfers between devices, per_device(): parts = lax.all_to_all(core, axes, split_axis=0, concat_axis=0, tiled=True)  2.57 us
  transfers between devices with their start and end apart: 6, of which 1 were waited for; matrix products, arithmetic and copies ran while one was open for 0% of the time, Pallas kernels for 44%

profile of v4, /device:TPU:0, one launch (start us, length us, event | category | flops | bytes accessed | tf_op | source)
XLA Modules:
  0.0 63.0 jit_solution(11966392403275773010)
XLA Ops:
  0.6 1.8 %select.1 = bf16[8,16,512]{2,1,0:T(8,128)(2,1)} custom-call(s32[1,8]{1,0:T(1,128)} %bitcast.27, bf16[8,2304]{1,0:T(8,128)(2,1)} %bitcast.26, bf16[8,4096]{1,0:T(8,128)(2,1)} %bitcast.25), custom_call_target="tpu_custom_call" | custom-call | tf_op jit(solution)/shard_map/select/pallas_call | solution.py:472
  2.5 7.3 %all-to-all-start = ((bf16[8,16,512]{2,1,0:T(8,128)(2,1)}), bf16[8,16,512]{2,1,0:T(8,128)(2,1)S(1)}, u32[]{:S(2)}, u32[]{:S(2)}) async-start(bf16[8,16,512]{2,1,0:T(8,128)(2,1)} %select.1), calls=%async_computation | async-start | bytes 262144 | tf_op jit(solution)/shard_map/all_to_all | solution.py:478
  10.4 1.4 %prep.1 = (bf16[512,448]{1,0:T(8,128)(2,1)S(1)}, bf16[256,256]{1,0:T(8,128)(2,1)S(1)}, bf16[256,256]{1,0:T(8,128)(2,1)S(1)}, f32[2,64,128]{2,1,0:T(8,128)S(1)}, ...) custom-call(bf16[64,147]{1,0:T(8,128)(2,1)} %weight.1, f32[1,64]{1,0:T(1,128)} %bitcast.30, ...), custom_call_target="tpu_custom_call" | custom-call | flops 134217728 | bytes 1048576 | tf_op jit(solution)/shard_map/prep/pallas_call | solution.py:483
  11.8 5.3 %all-to-all-done.recv = bf16[8,16,512]{2,1,0:T(8,128)(2,1)S(1)} async-done(((bf16[8,16,512]{2,1,0:T(8,128)(2,1)}), bf16[8,16,512]{2,1,0:T(8,128)(2,1)S(1)}, u32[]{:S(2)}, u32[]{:S(2)}) %all-to-all-start) | async-done | bytes 131104 | tf_op jit(solution)/shard_map/all_to_all | solution.py:478
  17.1 6.9 %core_forward.1 = (bf16[512,640]{1,0:T(8,128)(2,1)}, f32[8,4096]{1,0:T(8,128)S(1)}, bf16[512,2304]{1,0:T(8,128)(2,1)S(1)}, bf16[512,2304]{1,0:T(8,128)(2,1)S(1)}...) custom-call(bf16[8,16,512]{2,1,0:T(8,128)(2,1)S(1)} %all-to-all-done, ...), custom_call_target="tpu_custom_call" | custom-call | flops 1056964608 | bytes 9437184 | tf_op jit(solution)/shard_map/core_forward/pallas_call | solution.py:506
  24.0 0.1 collective-permute-start
  24.0 1.6 %collective-permute-start.1 = (bf16[512,640]{1,0:T(8,128)(2,1)}, bf16[512,640]{1,0:T(8,128)(2,1)}, u32[]{:S(2)}, u32[]{:S(2)}) collective-permute-start(bf16[512,640]{1,0:T(8,128)(2,1)} %get-tuple-element.45.pay.refs_0_), channel_id=1, source_target_pairs={{0,16},{8,24},{16,0},{24,8},{1,17},{9,25},{17,1},{25,9},{2,18},{10... | collective-permute-start | bytes 1966088 | tf_op jit(solution)/shard_map/ppermute | solution.py:529
  25.6 7.1 %readout.1 = (bf16[512,576]{1,0:T(8,128)(2,1)S(1)}, f32[8,128]{1,0:T(8,128)S(1)}) custom-call(s32[1]{0:T(128)S(6)} %copy.19.count, f32[8,4096]{1,0:T(8,128)S(1)} %get-tuple-element.44.target, bf16[512,640]{1,0:T(8,128)(2,1)} %get-tuple-element.45.pay.refs_0_, bf16[576,4096]{1,0:T(8,128)(2,1)S(1)} %get-tuple-element.46.mask, ...), custom_call_target="tpu_custom_call" | custom-call | flops 4831838208 | bytes 4718592 | tf_op jit(solution)/shard_map/readout/pallas_call | solution.py:534
  32.8 4.8 %core_backward.1 = f32[32,4,128]{2,1,0:T(4,128)} custom-call(bf16[512,576]{1,0:T(8,128)(2,1)S(1)} %get-tuple-element.48.pooled_grad, f32[8,128]{1,0:T(8,128)S(1)} %get-tuple-element.49.loss, bf16[512,2304]{1,0:T(8,128)(2,1)S(1)} %get-tuple-element.50.act1, bf16[512,2304]{1,0:T(8,128)(2,1)S(1)} %get-tuple-element.51.slope1, ...), custom_call_target="tpu_custom_call" | custom-call | flops 4831838208 | bytes 9437184 | tf_op jit(solution)/shard_map/core_backward/pallas_call | solution.py:547
  37.5 2.6 %all-to-all-start.1 = ((f32[32,4,128]{2,1,0:T(4,128)}), f32[32,4,128]{2,1,0:T(4,128)S(1)}, u32[]{:S(2)}, u32[]{:S(2)}) async-start(f32[32,4,128]{2,1,0:T(4,128)} %core_backward.1), calls=%async_computation.1 | async-start | bytes 131072 | tf_op jit(solution)/shard_map/all_to_all | solution.py:557
  40.1 0.0 collective-permute-done.refs_1_
  40.1 0.0 copy-start
  40.1 0.9 %copy-done = bf16[512,640]{1,0:T(8,128)(2,1)} copy-done((bf16[512,640]{1,0:T(8,128)(2,1)}, bf16[512,640]{1,0:T(8,128)(2,1)S(1)}, u32[]{:S(2)}) %copy-start) | copy-done | bytes 655384
  41.0 0.0 copy-start.1
  41.0 1.1 %copy-done.1 = bf16[512,640]{1,0:T(8,128)(2,1)S(1)} copy-done((bf16[512,640]{1,0:T(8,128)(2,1)S(1)}, bf16[512,640]{1,0:T(8,128)(2,1)}, u32[]{:S(2)}) %copy-start.1) | copy-done | bytes 655384
  42.1 5.8 %owned_rows.2.refs_5_ = f32[648,1024]{1,0:T(8,128)S(1)} custom-call(s32[1]{0:T(128)} %bitcast.9.where, s32[1]{0:T(128)S(6)} %copy.19.count, bf16[512,640]{1,0:T(8,128)(2,1)} %get-tuple-element.45.pay.refs_0_, bf16[512,640]{1,0:T(8,128)(2,1)S(1)} %copy-done.1, bf16[64,4096]{1,0:T(8,128)(2,1)S(1)} %get-tuple-element.47.wt.refs_2_, f32[1,4096]{1,0:T(1,128)} %refs_3_.3, ...), custom_call_target="tpu_custom_call" | custom-call | flops 2415919104 | bytes 2359296 | tf_op jit(solution)/shard_map/owned_rows/pallas_call | solution.py:561
  47.8 0.0 all-to-all-done.1.parts
  47.9 0.0 collective-permute-done.1.refs_0_
  47.9 0.2 collective-permute-start.2
  48.1 0.7 %share.1 = f32[32,4,128]{2,1,0:T(4,128)} custom-call(f32[32,4,128]{2,1,0:T(4,128)S(1)} %all-to-all-done.1.parts), custom_call_target="tpu_custom_call" | custom-call | tf_op jit(solution)/shard_map/share/pallas_call | solution.py:591
  48.7 5.8 %all-to-all-start.2 = ((f32[32,4,128]{2,1,0:T(4,128)}), f32[32,4,128]{2,1,0:T(4,128)S(1)}, u32[]{:S(2)}, u32[]{:S(2)}) async-start(f32[32,4,128]{2,1,0:T(4,128)} %share.1), calls=%async_computation.2 | async-start | bytes 131072 | tf_op jit(solution)/shard_map/all_to_all | solution.py:597
  54.6 0.0 collective-permute-done.2.refs_1_
  54.6 7.7 %owned_rows.3 = (f32[576,1024]{1,0:T(8,128)}, f32[64,1024]{1,0:T(8,128)}, f32[1,1024]{1,0:T(1,128)}) custom-call(s32[1]{0:T(128)} %bitcast.9.where, s32[1]{0:T(128)S(6)} %copy.19.count, bf16[512,640]{1,0:T(8,128)(2,1)} %collective-permute-done.1.refs_0_, bf16[512,640]{1,0:T(8,128)(2,1)} %collective-permute-done.2.refs_1_, ...), custom_call_target="tpu_custom_call" | custom-call | flops 2415919104 | bytes 2359296 | tf_op jit(solution)/shard_map/owned_rows/pallas_call | solution.py:561
  62.3 0.0 all-to-all-done.2.parts
  62.3 0.7 %unpack.1 = (f32[64,147]{1,0:T(8,128)}, f32[1,64]{1,0:T(1,128)}, f32[64,64]{1,0:T(8,128)}, f32[1,64]{1,0:T(1,128)}, f32[1,1]{1,0:T(1,128)}) custom-call(f32[32,4,128]{2,1,0:T(4,128)S(1)} %all-to-all-done.2.parts), custom_call_target="tpu_custom_call" | custom-call | tf_op jit(solution)/shard_map/unpack/pallas_call | solution.py:601
Async XLA Ops:
  2.5 14.6 %all-to-all-start = ((bf16[8,16,512]{2,1,0:T(8,128)(2,1)}), bf16[8,16,512]{2,1,0:T(8,128)(2,1)S(1)}, u32[]{:S(2)}, u32[]{:S(2)}) async-start(bf16[8,16,512]{2,1,0:T(8,128)(2,1)} %select.1), calls=%async_computation | async-start | bytes 262144 | tf_op jit(solution)/shard_map/all_to_all | solution.py:478
  24.0 16.2 %collective-permute-start = (bf16[512,640]{1,0:T(8,128)(2,1)}, bf16[512,640]{1,0:T(8,128)(2,1)S(1)}, u32[]{:S(2)}, u32[]{:S(2)}) collective-permute-start(bf16[512,640]{1,0:T(8,128)(2,1)} %get-tuple-element.45.pay.refs_0_), channel_id=1, source_target_pairs={{0,8},{8,0},{16,24},{24,16},{1,9},{9,1},{17,25},{25,17},{2,10},{10... | collective-permute-start | bytes 1966088 | tf_op jit(solution)/shard_map/ppermute | solution.py:529
  24.0 23.8 %collective-permute-start.1 = (bf16[512,640]{1,0:T(8,128)(2,1)}, bf16[512,640]{1,0:T(8,128)(2,1)}, u32[]{:S(2)}, u32[]{:S(2)}) collective-permute-start(bf16[512,640]{1,0:T(8,128)(2,1)} %get-tuple-element.45.pay.refs_0_), channel_id=1, source_target_pairs={{0,16},{8,24},{16,0},{24,8},{1,17},{9,25},{17,1},{25,9},{2,18},{10... | collective-permute-start | bytes 1966088 | tf_op jit(solution)/shard_map/ppermute | solution.py:529
  37.5 10.3 %all-to-all-start.1 = ((f32[32,4,128]{2,1,0:T(4,128)}), f32[32,4,128]{2,1,0:T(4,128)S(1)}, u32[]{:S(2)}, u32[]{:S(2)}) async-start(f32[32,4,128]{2,1,0:T(4,128)} %core_backward.1), calls=%async_computation.1 | async-start | bytes 131072 | tf_op jit(solution)/shard_map/all_to_all | solution.py:557
  40.1 0.9 %copy-start = (bf16[512,640]{1,0:T(8,128)(2,1)}, bf16[512,640]{1,0:T(8,128)(2,1)S(1)}, u32[]{:S(2)}) copy-start(bf16[512,640]{1,0:T(8,128)(2,1)S(1)} %collective-permute-done.refs_1_) | copy-start | bytes 1966084
  41.0 1.1 %copy-start.1 = (bf16[512,640]{1,0:T(8,128)(2,1)S(1)}, bf16[512,640]{1,0:T(8,128)(2,1)}, u32[]{:S(2)}) copy-start(bf16[512,640]{1,0:T(8,128)(2,1)} %copy-done) | copy-start | bytes 1966084
  47.9 6.7 %collective-permute-start.2 = (bf16[512,640]{1,0:T(8,128)(2,1)}, bf16[512,640]{1,0:T(8,128)(2,1)}, u32[]{:S(2)}, u32[]{:S(2)}) collective-permute-start(bf16[512,640]{1,0:T(8,128)(2,1)} %collective-permute-done.1.refs_0_), channel_id=1, source_target_pairs={{0,8},{8,0},{16,24},{24,16},{1,9},{9,1},{17,25},{25,17},{2,10},{10... | collective-permute-start | bytes 1966088 | tf_op jit(solution)/shard_map/ppermute | solution.py:590
  48.7 13.6 %all-to-all-start.2 = ((f32[32,4,128]{2,1,0:T(4,128)}), f32[32,4,128]{2,1,0:T(4,128)S(1)}, u32[]{:S(2)}, u32[]{:S(2)}) async-start(f32[32,4,128]{2,1,0:T(4,128)} %share.1), calls=%async_computation.2 | async-start | bytes 131072 | tf_op jit(solution)/shard_map/all_to_all | solution.py:597

commit v5 on v4

--- a/solution.py
+++ b/solution.py
@@ -18,7 +18,6 @@
 BF = jnp.bfloat16
 F32 = jnp.float32
 NT = (((1,), (1,)), ((), ()))
-TN = (((0,), (0,)), ((), ()))
 
 
 def dot(a, b, dims=(((1,), (0,)), ((), ())), precision=None):
@@ -52,10 +51,7 @@
     out[...] = jnp.stack(rows, axis=1).astype(BF)
 
 
-def prep_kernel(frames, weight, cbias, mix, mbias, wbig, blocks, blocks_t, bias, table, pool, unpool):
-    channels, taps = weight.shape
-    patch_cols = wbig.shape[1]
-    group = blocks.shape[0] // channels
+def fill_table(table, frames):
     t = iota(table.shape, 0)
     l = iota(table.shape, 1)
     dy = l // (DX * frames)
@@ -64,14 +60,20 @@
     hit = (t == place) | (t == place + KS * KS) | (t == place + 2 * KS * KS)
     last = (t == KT * KS * KS) & (l == KS * frames)
     table[...] = jnp.where(((dx < KS) & hit & (t < KT * KS * KS)) | last, 1.0, 0.0).astype(BF)
-    r = iota(pool.shape, 0)
-    c = iota(pool.shape, 1)
-    target = (r // (2 * WW)) * (WW // 2) + (r % WW) // 2
-    pool[...] = jnp.where(target == c, 0.25, 0.0).astype(BF)
-    r = iota(unpool.shape, 1)
-    c = iota(unpool.shape, 0)
-    target = (r // (2 * WW)) * (WW // 2) + (r % WW) // 2
-    unpool[...] = jnp.where(target == c, 0.25, 0.0).astype(BF)
+
+
+def pool_weights(shape, pixel_axis):
+    pixel = iota(shape, pixel_axis)
+    target = (pixel // (2 * WW)) * (WW // 2) + (pixel % WW) // 2
+    return jnp.where(target == iota(shape, 1 - pixel_axis), 0.25, 0.0).astype(BF)
+
+
+def prep_kernel(frames, weight, cbias, mix, mbias, wbig, blocks, blocks_t, bias, pool, table):
+    channels, taps = weight.shape
+    patch_cols = wbig.shape[1]
+    group = blocks.shape[0] // channels
+    fill_table(table, frames)
+    pool[...] = pool_weights(pool.shape, 0)
     size = channels * group
     same = (iota((size, size), 0) // channels) == (iota((size, size), 1) // channels)
     square = mix[...].astype(F32)
@@ -102,15 +104,14 @@
     bias,
     pool,
     mask_in,
-    wt_in,
     pay,
+    pay_send,
     target,
     act1,
     slope1,
     slope2,
     xcol,
     mask,
-    wt,
     pre0,
     pre1,
     mid0,
@@ -118,11 +119,10 @@
     feats,
     sems,
 ):
-    copies = [pltpu.make_async_copy(wt_in, wt, sems.at[0])]
-    for k, r in enumerate(range(0, mask.shape[0], SEG)):
-        copies.append(pltpu.make_async_copy(mask_in.at[r : r + SEG, :], mask.at[r : r + SEG, :], sems.at[k + 1]))
-    for copy in copies:
-        copy.start()
+    copies = []
+    for k, at in enumerate(range(0, mask.shape[1], 512)):
+        copies.append(pltpu.make_async_copy(mask_in.at[:, at : at + 512], mask.at[:, at : at + 512], sems.at[k]))
+        copies[k].start()
     frames, _, width = recv.shape
     rows, pix = act1.shape
     channels = bias.shape[1]
@@ -166,6 +166,12 @@
     half = 2 * WW
     pre = (pre0, pre1)
     mid = (mid0, mid1)
+
+    def send(at):
+        lanes = slice(at, at + half)
+        copies.append(pltpu.make_async_copy(pay.at[:, lanes], pay_send.at[:, lanes], sems.at[len(copies)]))
+        copies[-1].start()
+
     count = pix // CHUNK
     wide = wbig[...]
 
@@ -192,6 +198,7 @@
                 first = (t - 3) * CHUNK
                 pooled = dot(feats[:, first : first + 2 * CHUNK], pool[...])
                 pay[:, first // 4 : first // 4 + half] = pooled.astype(BF)
+                send(first // 4)
     p = pix - CHUNK
     tail = dot(feats[:, p:pix], pool[0:CHUNK, :])
     pieces = []
@@ -201,6 +208,7 @@
         pieces += [pltpu.roll(tile, SEG, 1), tile]
     packed = jnp.concatenate(pieces, axis=0)
     pay[:, p // 4 : p // 4 + half] = jnp.where(iota((rows, half), 1) < SEG, tail, packed).astype(BF)
+    send(p // 4)
     for copy in copies:
         copy.wait()
 
@@ -219,26 +227,37 @@
     return rate, grad
 
 
-def mixed_rows(grad, w):
-    frames = grad.shape[0]
-    return jnp.concatenate([grad[f : f + 1] * w for f in range(frames)], axis=0).astype(BF)
-
-
 def readout_kernel(
-    scale, count, target, pay, mask, wt, rbias, pooled_grad, loss, proj0, proj1, mixed, acc
+    scale, count, target, pay, mask_near, mask_in, wt, rbias, pooled_grad, loss, mask_late, proj0, proj1, mixed, acc, sems
 ):
-    pooled_n, neurons = mask.shape
+    pooled_n, early = mask_near.shape
+    neurons = early + mask_late.shape[1]
     channels = wt.shape[0]
     frames = target.shape[0]
     proj = (proj0, proj1)
     block = proj0.shape[1]
     steps = neurons // block
+    copies = {}
+    for at in range(early, neurons, block):
+        lanes = slice(at - early, at - early + block)
+        copies[at] = pltpu.make_async_copy(
+            mask_in.at[:, at : at + block], mask_late.at[:, lanes], sems.at[(at - early) // block]
+        )
+        copies[at].start()
+
+    def mask_part(at, size):
+        if at < early:
+            return mask_near[:, at : at + size]
+        return mask_late[:, at - early : at - early + size]
+
     pooled = pay[:, 0:pooled_n]
     loss_sum = jnp.zeros((frames, block), F32)
     begun = False
     for t in range(steps + 2):
         if t < steps:
-            proj[t % 2][...] = dot(pooled, mask[:, t * block : (t + 1) * block])
+            if t * block in copies:
+                copies[t * block].wait()
+            proj[t % 2][...] = dot(pooled, mask_part(t * block, block))
         if 1 <= t <= steps:
             at = slice((t - 1) * block, t * block)
             w = wt[:, at].astype(F32)
@@ -251,7 +270,7 @@
         if t >= 2 and (t % 2 == 1 or t == steps + 1):
             low = ((t - 2) // 2) * 2 * block
             at = slice(low, (t - 1) * block)
-            part = dot(mask[:, at], mixed[:, at], NT)
+            part = dot(mask_part(low, (t - 1) * block - low), mixed[:, at], NT)
             acc[...] = acc[...] + part if begun else part
             begun = True
     pooled_grad[...] = acc[...].T.astype(BF)
@@ -259,7 +278,7 @@
 
 
 def core_backward_kernel(
-    channels, pooled_grad, loss, act1, slope1, slope2, xcol, blocks_t, table, unpool, out, up0, up1, down0, down1, g2, g1
+    channels, pooled_grad, loss, act1, slope1, slope2, xcol, blocks_t, out, up0, up1, down0, down1, g2, g1, table
 ):
     rows, pix = act1.shape
     frames = rows // channels
@@ -270,6 +289,8 @@
     down = (down0, down1)
     count = pix // CHUNK
     half = 2 * WW
+    unpool = pool_weights((half, 4 * half), 1)
+    fill_table(table, frames)
     bias_sum = jnp.zeros((channels, 128), F32)
     for t in range(count + 2):
         if t < count:
@@ -359,17 +380,17 @@
 
 
 def owned_rows_kernel(scale, clips, own, block, held, where, count, *refs):
-    pays = refs[:clips]
-    wt, rbias, mask_in = refs[clips : clips + 3]
-    channels = refs[clips].shape[0]
+    sent = refs[:clips]
+    wt_in, mask_in, rbias = refs[clips : clips + 3]
     before = refs[clips + 3 : clips + 3 + held]
-    outs = refs[clips + 3 + held : -8]
-    proj0, proj1, mixed0, mixed1, turned, mask, stage, sems = refs[-8:]
+    outs = refs[clips + 3 + held : -10]
+    pays, wt, proj0, proj1, mixed0, mixed1, turned, mask, stage, sems = refs[-10:]
     proj = (proj0, proj1)
     mixed = (mixed0, mixed1)
     pooled_n = mask.shape[0]
+    channels = wt.shape[0]
     low_rows = pooled_n + channels
-    rows = pays[0].shape[0]
+    rows = pays.shape[1]
     frames = rows // channels
     steps = own // block
     first = pl.multiple_of(where[0] * own, own)
@@ -377,9 +398,13 @@
     for k in range(steps):
         lanes = pl.ds(pl.multiple_of(first + k * block, block), block)
         fetches.append(pltpu.make_async_copy(mask_in.at[:, lanes], mask.at[:, k * block : (k + 1) * block], sems.at[k]))
-        fetches[k].start()
-    for c in range(clips):
-        turned[:, c * rows : (c + 1) * rows] = pays[c][:, 0:pooled_n].T
+    arrive = [pltpu.make_async_copy(sent[c], pays.at[c], sems.at[2 * steps + c]) for c in range(clips)]
+    weights = pltpu.make_async_copy(wt_in.at[:, pl.ds(first, own)], wt, sems.at[2 * steps + clips])
+    arrive[0].start()
+    fetches[0].start()
+    weights.start()
+    for copy in arrive[1:] + fetches[1:]:
+        copy.start()
     segs = block // SEG
     low = iota((frames, 128), 1) < SEG
     items = [(k, c) for k in range(steps) for c in range(clips)]
@@ -389,21 +414,26 @@
     for t in range(len(items) + 2):
         if t < len(items):
             k, c = items[t]
+            if k == 0:
+                arrive[c].wait()
+                turned[:, c * rows : (c + 1) * rows] = pays[c, :, 0:pooled_n].T
             if c == 0:
                 fetches[k].wait()
-            proj[t % 2][...] = dot(pays[c][:, 0:pooled_n], mask[:, k * block : (k + 1) * block])
+            if t == 0:
+                weights.wait()
+            proj[t % 2][...] = dot(pays[c, :, 0:pooled_n], mask[:, k * block : (k + 1) * block])
         if 1 <= t <= len(items):
             k, c = items[t - 1]
             start = pl.multiple_of(first + k * block, block)
             base = pl.multiple_of(start // SEG * frames, segs * frames)
-            packed = pays[c][pl.ds(base, segs * frames), pooled_n - SEG : pooled_n + SEG].astype(F32)
+            packed = pays[c, pl.ds(base, segs * frames), pooled_n - SEG : pooled_n + SEG].astype(F32)
             tiles = []
             for j in range(0, segs, 2):
                 even = packed[j * frames : (j + 1) * frames]
                 odd = packed[(j + 1) * frames : (j + 2) * frames]
                 tiles.append(jnp.where(low, pltpu.roll(even, SEG, 1), odd))
             target = jnp.concatenate(tiles, axis=1)
-            w = wt[:, pl.ds(start, block)].astype(F32)
+            w = wt[:, k * block : (k + 1) * block].astype(F32)
             alive = (start + iota((frames, block), 1)) < count[0]
             now = proj[(t - 1) % 2]
             _, grad = drive_terms(now, target, w, rbias[:, pl.ds(start, block)], alive, scale, channels)
@@ -431,8 +461,8 @@
         store.wait()
 
 
-def params(limit=20):
-    return pltpu.CompilerParams(vmem_limit_bytes=limit << 20)
+def params(rows=512):
+    return pltpu.CompilerParams(vmem_limit_bytes=min(56, 20 * max(1, rows // 512)) << 20)
 
 
 def cost(flops, moved=1 << 20):
@@ -475,22 +505,23 @@
         compiler_params=params(),
         name="select",
     )(*in_hbm(assignment[None, :], video.reshape(clip_block, pix), responses.reshape(clip_block, neurons)))
+    where = lax.axis_index("clip").astype(jnp.int32)[None]
+    send, where = lax.optimization_barrier((send, where))
     recv = lax.all_to_all(send, "sess", split_axis=0, concat_axis=0, tiled=True)
 
     patch_cols = KS * DX * frames
     span = channels * group
     half = 2 * WW
-    wbig, blocks, blocks_t, bias, table, pool, unpool = pl.pallas_call(
+    wbig, blocks, blocks_t, bias, pool = pl.pallas_call(
         functools.partial(prep_kernel, frames),
         out_shape=(
             jax.ShapeDtypeStruct((rows, patch_cols), BF),
             jax.ShapeDtypeStruct((span, span), BF),
             jax.ShapeDtypeStruct((span, span), BF),
             jax.ShapeDtypeStruct((2, channels, 128), F32),
-            jax.ShapeDtypeStruct((PACK, patch_cols), BF),
             jax.ShapeDtypeStruct((4 * half, half), BF),
-            jax.ShapeDtypeStruct((half, 4 * half), BF),
         ),
+        scratch_shapes=[pltpu.VMEM((PACK, patch_cols), BF)],
         compiler_params=params(),
         cost_estimate=cost(1 << 27),
         name="prep",
@@ -498,69 +529,79 @@
 
     wt = jnp.swapaxes(feat_w, 1, 2).reshape(channels, neurons)
     mask_t = jnp.swapaxes(masks, 1, 2).reshape(pooled_n, neurons)
-    mask_t, wt, rbias = in_hbm(mask_t, wt, readout_bias)
+    rbias = readout_bias
+    mask_far, wt_far = in_hbm(mask_t, wt)
     width = pooled_n + SEG
+    early = neurons // 2
     vmem = pl.BlockSpec(memory_space=pltpu.VMEM)
     anywhere = pl.BlockSpec(memory_space=pl.ANY)
     smem = pl.BlockSpec(memory_space=pltpu.SMEM)
-    pay, target, act1, slope1, slope2, xcol, mask_v, wt_v = pl.pallas_call(
+    pay, pay_send, target, act1, slope1, slope2, xcol, mask_near = pl.pallas_call(
         core_forward_kernel,
         out_shape=(
+            jax.ShapeDtypeStruct((rows, width), BF),
             jax.ShapeDtypeStruct((rows, width), BF),
             jax.ShapeDtypeStruct((frames, neurons), F32),
             jax.ShapeDtypeStruct((rows, pix), BF),
             jax.ShapeDtypeStruct((rows, pix), BF),
             jax.ShapeDtypeStruct((rows, pix), BF),
             jax.ShapeDtypeStruct((patch_cols, pix), BF),
-            jax.ShapeDtypeStruct((pooled_n, neurons), BF),
-            jax.ShapeDtypeStruct((channels, neurons), BF),
+            jax.ShapeDtypeStruct((pooled_n, early), BF),
         ),
-        in_specs=[vmem] * 5 + [anywhere] * 2,
+        in_specs=[vmem] * 5 + [anywhere],
+        out_specs=(vmem, anywhere) + (vmem,) * 6,
         scratch_shapes=[pltpu.VMEM((rows, CHUNK), F32)] * 4
-        + [pltpu.VMEM((rows, pix), BF), pltpu.SemaphoreType.DMA((1 + pooled_n // SEG,))],
+        + [pltpu.VMEM((rows, pix), BF), pltpu.SemaphoreType.DMA((early // 512 + width // half,))],
         compiler_params=params(),
         cost_estimate=cost(2 * rows * pix * patch_cols, 8 * rows * pix),
         name="core_forward",
-    )(recv, wbig, blocks, bias, pool, mask_t, wt)
-
-    near = {0: pay}
+    )(recv, wbig, blocks, bias, pool, mask_far)
+
+    (pay_send,) = in_hbm(pay_send)
+    near = {0: pay_send}
     for mask in range(1, clip_total):
         if mask % 2 == 0 or mask == 1:
-            near[mask] = lax.ppermute(pay, "clip", xor_pairs(clip_total, mask))
+            near[mask] = lax.ppermute(pay_send, "clip", xor_pairs(clip_total, mask))
 
     big = min(512, neurons)
     work = 2 * rows * neurons * pooled_n
-    where = lax.axis_index("clip").astype(jnp.int32)[None]
     pooled_grad, loss = pl.pallas_call(
         functools.partial(readout_kernel, scale),
-        in_specs=[smem] + [vmem] * 5,
+        in_specs=[smem] + [vmem] * 3 + [anywhere] + [vmem] * 2,
         out_shape=(jax.ShapeDtypeStruct((rows, pooled_n), BF), jax.ShapeDtypeStruct((8, 128), F32)),
-        scratch_shapes=[pltpu.VMEM((rows, big), F32)] * 2
-        + [pltpu.VMEM((rows, neurons), BF), pltpu.VMEM((pooled_n, rows), F32)],
+        scratch_shapes=[pltpu.VMEM((pooled_n, neurons - early), BF)]
+        + [pltpu.VMEM((rows, big), F32)] * 2
+        + [
+            pltpu.VMEM((rows, neurons), BF),
+            pltpu.VMEM((pooled_n, rows), F32),
+            pltpu.SemaphoreType.DMA(((neurons - early) // big,)),
+        ],
         compiler_params=params(),
         cost_estimate=cost(2 * work, 2 * neurons * pooled_n),
         name="readout",
-    )(counts, target, pay, mask_v, wt_v, rbias)
+    )(counts, target, pay, mask_near, mask_far, wt, rbias)
 
     assert 2 * channels % total == 0
     pieces = (total, 2 * channels // total, 128)
     core = pl.pallas_call(
         functools.partial(core_backward_kernel, channels),
         out_shape=jax.ShapeDtypeStruct(pieces, F32),
-        scratch_shapes=[pltpu.VMEM((rows, CHUNK), F32)] * 4 + [pltpu.VMEM((rows, pix), BF)] * 2,
+        scratch_shapes=[pltpu.VMEM((rows, CHUNK), F32)] * 4
+        + [pltpu.VMEM((rows, pix), BF)] * 2
+        + [pltpu.VMEM((PACK, patch_cols), BF)],
         compiler_params=params(),
         cost_estimate=cost(2 * work, 8 * rows * pix),
         name="core_backward",
-    )(pooled_grad, loss, act1, slope1, slope2, xcol, blocks_t, table, unpool)
+    )(pooled_grad, loss, act1, slope1, slope2, xcol, blocks_t)
 
     axes = ("clip", "sess")
     parts = lax.all_to_all(core, axes, split_axis=0, concat_axis=0, tiled=True)
 
-    def owned_rows(clips, held):
+    def owned_rows(clips, held, block):
         last = len(held) > 0
         return pl.pallas_call(
             functools.partial(owned_rows_kernel, scale, len(clips), own, block, len(held)),
-            in_specs=[smem, smem] + [vmem] * (len(clips) + 2) + [anywhere] + [vmem] * len(held),
+            in_specs=[smem, smem] + [anywhere] * (len(clips) + 2) + [vmem] * (1 + len(held)),
             out_specs=[anywhere, vmem, vmem] if last else [vmem],
             out_shape=[
                 jax.ShapeDtypeStruct((pooled_n, own), F32),
@@ -569,25 +610,25 @@
             ]
             if last
             else [jax.ShapeDtypeStruct((pooled_n + channels + 8, own), F32)],
-            scratch_shapes=[pltpu.VMEM((rows, block), F32)] * 2
+            scratch_shapes=[pltpu.VMEM((len(clips), rows, width), BF), pltpu.VMEM((channels, own), BF)]
+            + [pltpu.VMEM((rows, block), F32)] * 2
             + [pltpu.VMEM((len(clips) * rows, block), BF)] * 2
             + [
                 pltpu.VMEM((pooled_n, len(clips) * rows), BF),
                 pltpu.VMEM((pooled_n, own), BF),
                 pltpu.VMEM((pooled_n, own) if last else (8, 128), F32),
-                pltpu.SemaphoreType.DMA((2 * (own // block),)),
+                pltpu.SemaphoreType.DMA((2 * (own // block) + len(clips) + 1,)),
             ],
-            compiler_params=params(),
+            compiler_params=params(rows),
             cost_estimate=cost(2 * work * len(clips) // clip_total, 4 * own * pooled_n),
             name="owned_rows",
-        )(where, counts, *clips, wt_v, rbias, mask_t, *held)
-
-    readout_grads = owned_rows([near[0], near[1]], ())
+        )(where, counts, *in_hbm(*clips), wt_far, mask_far, rbias, *held)
+
     far = [mask for mask in near if mask > 1]
-    parts, readout_grads, reached = lax.optimization_barrier((parts, readout_grads, [near[mask] for mask in far]))
-    others = []
-    for value in reached:
-        others += [value, lax.ppermute(value, "clip", xor_pairs(clip_total, 1))]
+    reached, _ = lax.optimization_barrier(([near[mask] for mask in far], core))
+    others = [lax.ppermute(value, "clip", xor_pairs(clip_total, 1)) for value in reached]
+    (partial,) = owned_rows([near[0], near[1]] + reached, (), block)
+    parts, partial = lax.optimization_barrier((parts, partial))
     copies = pl.pallas_call(
         share_kernel,
         out_shape=jax.ShapeDtypeStruct(pieces, F32),
@@ -595,7 +636,7 @@
         name="share",
     )(parts)
     summed = lax.all_to_all(copies, axes, split_axis=0, concat_axis=0, tiled=True)
-    readout_grads = owned_rows(others, readout_grads)
+    readout_grads = owned_rows(others, (partial,), max(128, block // 2))
     summed, readout_grads = lax.optimization_barrier((summed, readout_grads))
     mask_grad, feat_grad, grad_rbias = readout_grads
     grad_conv, grad_cb, grad_mix, grad_mb, loss = pl.pallas_call(

time: 63.6 us -> 62.3 us (0.980)
  waiting for transfers between devices: 5.32 us -> 8.76 us
  Pallas kernels: 36.8 us -> 34.5 us
  local copies, waits for them, and re-layouts: 1.95 us -> 0.01 us
    unnamed x4 -> x6, local copies, waits for them, and re-layouts: 1.95 us -> 0.01 us
    pallas_call x1, Pallas kernels: 6.86 us -> 5.25 us  [per_device(): pl.pallas_call(core_forward_kernel, out_shape=(jax.ShapeDtypeStruct((rows...]
    ppermute x3, waiting for transfers between devices: 0.01 us -> 1.57 us  [the longest x2 1.56 us: per_device(): near[mask] = lax.ppermute(pay_send, 'clip', xor_pairs(clip_total, mask))]
    all_to_all x1, waiting for transfers between devices: 0.01 us -> 1.49 us  [per_device(): lax.all_to_all(copies, axes, split_axis=0, concat_axis=0, tiled=True)]
    pallas_call x2, Pallas kernels: 13.5 us -> 12.7 us  [owned_rows(): pl.pallas_call(functools.partial(owned_rows_kernel, scale, len(clips), ow...]
  transfers between devices with their start and end apart: 6 -> 6, of which waited for: 1 -> 4; matrix products, arithmetic and copies ran while one was open for 0% -> 0% of each run, Pallas kernels for 44% -> 43%
where the time goes in v5:
time: 62.3 us; the launch traced here: 61.9 us
  Pallas kernels  34.5 us (55%)
  starting transfers between devices  17.2 us (28%)
  waiting for transfers between devices  8.76 us (14%)
  between operations  1.39 us (2%)
    pallas_call x2, Pallas kernels, owned_rows(): pl.pallas_call(functools.partial(owned_rows_kernel, scale, len(clips), ow...  12.7 us
    all_to_all x1, starting transfers between devices, per_device(): recv = lax.all_to_all(send, 'sess', split_axis=0, concat_axis=0, tiled=True)  7.28 us
    pallas_call x1, Pallas kernels, per_device(): pl.pallas_call(functools.partial(readout_kernel, scale), in_specs=[smem]...  7.1 us
    all_to_all x1, starting transfers between devices, per_device(): lax.all_to_all(copies, axes, split_axis=0, concat_axis=0, tiled=True)  5.51 us
    all_to_all x1, waiting for transfers between devices, per_device(): recv = lax.all_to_all(send, 'sess', split_axis=0, concat_axis=0, tiled=True)  5.37 us
    pallas_call x1, Pallas kernels, per_device(): pl.pallas_call(core_forward_kernel, out_shape=(jax.ShapeDtypeStruct((rows...  5.25 us
    pallas_call x1, Pallas kernels, per_device(): pl.pallas_call(functools.partial(core_backward_kernel, channels), out_sha...  4.96 us
    all_to_all x1, starting transfers between devices, per_device(): parts = lax.all_to_all(core, axes, split_axis=0, concat_axis=0, tiled=True)  2.8 us
  transfers between devices with their start and end apart: 6, of which 4 were waited for; matrix products, arithmetic and copies ran while one was open for 0% of the time, Pallas kernels for 43%

profile of v5, /device:TPU:0, one launch (start us, length us, event | category | flops | bytes accessed | tf_op | source)
XLA Modules:
  0.0 61.9 jit_solution(3055448912893073709)
XLA Ops:
  0.6 1.8 %select.1 = bf16[8,16,512]{2,1,0:T(8,128)(2,1)} custom-call(s32[1,8]{1,0:T(1,128)} %bitcast.30, bf16[8,2304]{1,0:T(8,128)(2,1)} %bitcast.29, bf16[8,4096]{1,0:T(8,128)(2,1)} %bitcast.28), custom_call_target="tpu_custom_call" | custom-call | tf_op jit(solution)/shard_map/select/pallas_call | solution.py:502
  2.5 7.3 %all-to-all-start = ((bf16[8,16,512]{2,1,0:T(8,128)(2,1)}), bf16[8,16,512]{2,1,0:T(8,128)(2,1)S(1)}, u32[]{:S(2)}, u32[]{:S(2)}) async-start(bf16[8,16,512]{2,1,0:T(8,128)(2,1)} %select.1), calls=%async_computation | async-start | bytes 262144 | tf_op jit(solution)/shard_map/all_to_all | solution.py:510
  10.4 1.3 %prep.1 = (bf16[512,448]{1,0:T(8,128)(2,1)S(1)}, bf16[256,256]{1,0:T(8,128)(2,1)S(1)}, bf16[256,256]{1,0:T(8,128)(2,1)S(1)}, f32[2,64,128]{2,1,0:T(8,128)S(1)}, bf16[512,128]{1,0:T(8,128)(2,1)S(1)}) custom-call(bf16[64,147]{1,0:T(8,128)(2,1)} %weight.1, f32[1,64]{1,0:T(1,128)} %bitcast.33, bf16[64,64]{1,0:T(8,128)(2,1)} %mix.1, f32[1,64]{1,0:T(1,128)} %bitcast.34), custom_call_target="tpu_custom_call" | custom-call | flops 134217728 | bytes 1048576 | tf_op jit(solution)/shard_map/prep/pallas_call | solution.py:515
  11.7 5.4 %all-to-all-done.recv = bf16[8,16,512]{2,1,0:T(8,128)(2,1)S(1)} async-done(((bf16[8,16,512]{2,1,0:T(8,128)(2,1)}), bf16[8,16,512]{2,1,0:T(8,128)(2,1)S(1)}, u32[]{:S(2)}, u32[]{:S(2)}) %all-to-all-start) | async-done | bytes 131104 | tf_op jit(solution)/shard_map/all_to_all | solution.py:510
  17.1 0.0 copy-start
  17.1 0.0 copy-start.1
  17.1 5.3 %core_forward.1 = (bf16[512,640]{1,0:T(8,128)(2,1)S(1)}, bf16[512,640]{1,0:T(8,128)(2,1)S(1)}, f32[8,4096]{1,0:T(8,128)S(1)}, bf16[512,2304]{1,0:T(8,128)(2,1)S(...) custom-call(bf16[8,16,512]{2,1,0:T(8,128)(2,1)S(1)} %all-to-all-done, ...), custom_call_target="tpu_custom_call" | custom-call | flops 1056964608 | bytes 9437184 | tf_op jit(solution)/shard_map/core_forward/pallas_call | solution.py:539
  22.4 0.0 copy-start.2
  22.4 1.6 %collective-permute-start.1 = (bf16[512,640]{1,0:T(8,128)(2,1)S(1)}, bf16[512,640]{1,0:T(8,128)(2,1)}, u32[]{:S(2)}, u32[]{:S(2)}) collective-permute-start(bf16[512,640]{1,0:T(8,128)(2,1)S(1)} %get-tuple-element.56.refs_0_), channel_id=1, source_target_pairs={{0,16},{8,24},{16,0},{24,8},{1,17},{9,25},{17,1},{25,9},{2,18},{10... | collective-permute-start | bytes 1966088 | tf_op jit(solution)/shard_map/ppermute | solution.py:564
  24.0 0.0 collective-permute-start
  24.0 0.0 copy-done
  24.0 0.0 copy-done.1
  24.0 7.1 %readout.1 = (bf16[512,576]{1,0:T(8,128)(2,1)S(1)}, f32[8,128]{1,0:T(8,128)S(1)}) custom-call(s32[1]{0:T(128)S(6)} %copy.19.count, f32[8,4096]{1,0:T(8,128)S(1)} %get-tuple-element.45.target, bf16[512,640]{1,0:T(8,128)(2,1)S(1)} %get-tuple-element.46.pay, bf16[576,2048]{1,0:T(8,128)(2,1)S(1)} %get-tuple-element.47.mask_near, bf16[576,4096]{1,0:T(8,128)(2,1)} %bitcast.25, ...), custom_call_target="tpu_custom_call" | custom-call | flops 4831838208 | bytes 4718592 | tf_op jit(solution)/shard_map/readout/pallas_call | solution.py:568
  31.1 0.0 copy-done.2
  31.1 5.0 %core_backward.1 = f32[32,4,128]{2,1,0:T(4,128)} custom-call(bf16[512,576]{1,0:T(8,128)(2,1)S(1)} %get-tuple-element.48.pooled_grad, f32[8,128]{1,0:T(8,128)S(1)} %get-tuple-element.49.loss, bf16[512,2304]{1,0:T(8,128)(2,1)S(1)} %get-tuple-element.50.act1, bf16[512,2304]{1,0:T(8,128)(2,1)S(1)} %get-tuple-element.51.slope1, ...), custom_call_target="tpu_custom_call" | custom-call | flops 4831838208 | bytes 9437184 | tf_op jit(solution)/shard_map/core_backward/pallas_call | solution.py:586
  36.0 1.6 %collective-permute-done.1.refs_2_ = bf16[512,640]{1,0:T(8,128)(2,1)} collective-permute-done((bf16[512,640]{1,0:T(8,128)(2,1)S(1)}, bf16[512,640]{1,0:T(8,128)(2,1)}, u32[]{:S(2)}, u32[]{:S(2)}) %collective-permute-start.1) | collective-permute-done | bytes 655392 | tf_op jit(solution)/shard_map/ppermute | solution.py:564
  37.6 0.0 collective-permute-start.2
  37.6 2.8 %all-to-all-start.1 = ((f32[32,4,128]{2,1,0:T(4,128)}), f32[32,4,128]{2,1,0:T(4,128)S(1)}, u32[]{:S(2)}, u32[]{:S(2)}) async-start(f32[32,4,128]{2,1,0:T(4,128)} %core_backward.1), calls=%async_computation.1 | async-start | bytes 131072 | tf_op jit(solution)/shard_map/all_to_all | solution.py:598
  40.4 0.0 collective-permute-done.refs_1_
  40.4 6.9 %owned_rows.2.refs_4_ = f32[648,1024]{1,0:T(8,128)S(1)} custom-call(s32[1]{0:T(128)} %bitcast.3.where, s32[1]{0:T(128)S(6)} %copy.19.count, bf16[512,640]{1,0:T(8,128)(2,1)} %copy-done.2, bf16[512,640]{1,0:T(8,128)(2,1)} %collective-permute-done.refs_1_, bf16[512,640]{1,0:T(8,128)(2,1)} %collective-permute-done.1.refs_2_, bf16[64,4096]{1,0:T(8,128)(2,1)} %bitcast.21, ...), custom_call_target="tpu_custom_call" | custom-call | flops 3623878656 | bytes 2359296 | tf_op jit(solution)/shard_map/owned_rows/pallas_call | solution.py:602
  47.4 0.3 all-to-all-done.1.parts
  47.7 0.7 %share.1 = f32[32,4,128]{2,1,0:T(4,128)} custom-call(f32[32,4,128]{2,1,0:T(4,128)S(1)} %all-to-all-done.1.parts), custom_call_target="tpu_custom_call" | custom-call | tf_op jit(solution)/shard_map/share/pallas_call | solution.py:632
  48.4 5.5 %all-to-all-start.2 = ((f32[32,4,128]{2,1,0:T(4,128)}), f32[32,4,128]{2,1,0:T(4,128)S(1)}, u32[]{:S(2)}, u32[]{:S(2)}) async-start(f32[32,4,128]{2,1,0:T(4,128)} %share.1), calls=%async_computation.2 | async-start | bytes 131072 | tf_op jit(solution)/shard_map/all_to_all | solution.py:638
  53.9 0.0 collective-permute-done.2.refs_0_
  53.9 5.8 %owned_rows.3 = (f32[576,1024]{1,0:T(8,128)}, f32[64,1024]{1,0:T(8,128)}, f32[1,1024]{1,0:T(1,128)}) custom-call(s32[1]{0:T(128)} %bitcast.3.where, s32[1]{0:T(128)S(6)} %copy.19.count, bf16[512,640]{1,0:T(8,128)(2,1)} %collective-permute-done.2.refs_0_, bf16[64,4096]{1,0:T(8,128)(2,1)} %bitcast.22, bf16[576,4096]{1,0:T(8,128)(2,1)} %bitcast.27, ...), custom_call_target="tpu_custom_call" | custom-call | flops 1207959552 | bytes 2359296 | tf_op jit(solution)/shard_map/owned_rows/pallas_call | solution.py:602
  59.7 1.5 %all-to-all-done.2.parts = f32[32,4,128]{2,1,0:T(4,128)S(1)} async-done(((f32[32,4,128]{2,1,0:T(4,128)}), f32[32,4,128]{2,1,0:T(4,128)S(1)}, u32[]{:S(2)}, u32[]{:S(2)}) %all-to-all-start.2) | async-done | bytes 65568 | tf_op jit(solution)/shard_map/all_to_all | solution.py:638
  61.2 0.7 %unpack.1 = (f32[64,147]{1,0:T(8,128)}, f32[1,64]{1,0:T(1,128)}, f32[64,64]{1,0:T(8,128)}, f32[1,64]{1,0:T(1,128)}, f32[1,1]{1,0:T(1,128)}) custom-call(f32[32,4,128]{2,1,0:T(4,128)S(1)} %all-to-all-done.2.parts), custom_call_target="tpu_custom_call" | custom-call | tf_op jit(solution)/shard_map/unpack/pallas_call | solution.py:642
Async XLA Ops:
  2.5 14.6 %all-to-all-start = ((bf16[8,16,512]{2,1,0:T(8,128)(2,1)}), bf16[8,16,512]{2,1,0:T(8,128)(2,1)S(1)}, u32[]{:S(2)}, u32[]{:S(2)}) async-start(bf16[8,16,512]{2,1,0:T(8,128)(2,1)} %select.1), calls=%async_computation | async-start | bytes 262144 | tf_op jit(solution)/shard_map/all_to_all | solution.py:510
  17.1 6.9 %copy-start = (bf16[1,4096,64]{1,2,0:T(8,128)(2,1)S(1)}, bf16[1,4096,64]{1,2,0:T(8,128)(2,1)}, u32[]{:S(2)}) copy-start(bf16[1,4096,64]{1,2,0:T(8,128)(2,1)} %param.20) | copy-start | bytes 1572868
  17.1 6.9 %copy-start.1 = (f32[1,4096]{1,0:T(1,128)S(1)}, f32[1,4096]{1,0:T(1,128)}, u32[]{:S(2)}) copy-start(f32[1,4096]{1,0:T(1,128)} %refs_3_.1) | copy-start | bytes 49156
  22.4 8.7 %copy-start.2 = (bf16[512,640]{1,0:T(8,128)(2,1)}, bf16[512,640]{1,0:T(8,128)(2,1)S(1)}, u32[]{:S(2)}) copy-start(bf16[512,640]{1,0:T(8,128)(2,1)S(1)} %get-tuple-element.56.refs_0_) | copy-start | bytes 1966084
  22.4 15.2 %collective-permute-start.1 = (bf16[512,640]{1,0:T(8,128)(2,1)S(1)}, bf16[512,640]{1,0:T(8,128)(2,1)}, u32[]{:S(2)}, u32[]{:S(2)}) collective-permute-start(bf16[512,640]{1,0:T(8,128)(2,1)S(1)} %get-tuple-element.56.refs_0_), channel_id=1, source_target_pairs={{0,16},{8,24},{16,0},{24,8},{1,17},{9,25},{17,1},{25,9},{2,18},{10... | collective-permute-start | bytes 1966088 | tf_op jit(solution)/shard_map/ppermute | solution.py:564
  24.0 16.5 %collective-permute-start = (bf16[512,640]{1,0:T(8,128)(2,1)S(1)}, bf16[512,640]{1,0:T(8,128)(2,1)}, u32[]{:S(2)}, u32[]{:S(2)}) collective-permute-start(bf16[512,640]{1,0:T(8,128)(2,1)S(1)} %get-tuple-element.56.refs_0_), channel_id=1, source_target_pairs={{0,8},{8,0},{16,24},{24,16},{1,9},{9,1},{17,25},{25,17},{2,10},{10... | collective-permute-start | bytes 1966088 | tf_op jit(solution)/shard_map/ppermute | solution.py:564
  37.6 16.3 %collective-permute-start.2 = (bf16[512,640]{1,0:T(8,128)(2,1)}, bf16[512,640]{1,0:T(8,128)(2,1)}, u32[]{:S(2)}, u32[]{:S(2)}) collective-permute-start(bf16[512,640]{1,0:T(8,128)(2,1)} %collective-permute-done.1.refs_2_), channel_id=1, source_target_pairs={{0,8},{8,0},{16,24},{24,16},{1,9},{9,1},{17,25},{25,17},{2,10},{10... | collective-permute-start | bytes 1966088 | tf_op jit(solution)/shard_map/ppermute | solution.py:629
  37.6 10.1 %all-to-all-start.1 = ((f32[32,4,128]{2,1,0:T(4,128)}), f32[32,4,128]{2,1,0:T(4,128)S(1)}, u32[]{:S(2)}, u32[]{:S(2)}) async-start(f32[32,4,128]{2,1,0:T(4,128)} %core_backward.1), calls=%async_computation.1 | async-start | bytes 131072 | tf_op jit(solution)/shard_map/all_to_all | solution.py:598
  48.4 12.8 %all-to-all-start.2 = ((f32[32,4,128]{2,1,0:T(4,128)}), f32[32,4,128]{2,1,0:T(4,128)S(1)}, u32[]{:S(2)}, u32[]{:S(2)}) async-start(f32[32,4,128]{2,1,0:T(4,128)} %share.1), calls=%async_computation.2 | async-start | bytes 131072 | tf_op jit(solution)/shard_map/all_to_all | solution.py:638

commit v6 on v5

--- a/solution.py
+++ b/solution.py
@@ -105,7 +105,6 @@
     pool,
     mask_in,
     pay,
-    pay_send,
     target,
     act1,
     slope1,
@@ -120,9 +119,8 @@
     sems,
 ):
     copies = []
-    for k, at in enumerate(range(0, mask.shape[1], 512)):
-        copies.append(pltpu.make_async_copy(mask_in.at[:, at : at + 512], mask.at[:, at : at + 512], sems.at[k]))
-        copies[k].start()
+    for k, r in enumerate(range(0, mask.shape[0], SEG)):
+        copies.append(pltpu.make_async_copy(mask_in.at[r : r + SEG, :], mask.at[r : r + SEG, :], sems.at[k]))
     frames, _, width = recv.shape
     rows, pix = act1.shape
     channels = bias.shape[1]
@@ -166,12 +164,6 @@
     half = 2 * WW
     pre = (pre0, pre1)
     mid = (mid0, mid1)
-
-    def send(at):
-        lanes = slice(at, at + half)
-        copies.append(pltpu.make_async_copy(pay.at[:, lanes], pay_send.at[:, lanes], sems.at[len(copies)]))
-        copies[-1].start()
-
     count = pix // CHUNK
     wide = wbig[...]
 
@@ -184,6 +176,8 @@
             slope[r : r + channels, at] = e.astype(BF)
 
     for t in range(count + 2):
+        if t < len(copies):
+            copies[t].start()
         if t < count:
             pre[t % 2][...] = dot(wide, xcol[:, t * CHUNK : (t + 1) * CHUNK])
         if 1 <= t <= count:
@@ -198,7 +192,6 @@
                 first = (t - 3) * CHUNK
                 pooled = dot(feats[:, first : first + 2 * CHUNK], pool[...])
                 pay[:, first // 4 : first // 4 + half] = pooled.astype(BF)
-                send(first // 4)
     p = pix - CHUNK
     tail = dot(feats[:, p:pix], pool[0:CHUNK, :])
     pieces = []
@@ -208,7 +201,6 @@
         pieces += [pltpu.roll(tile, SEG, 1), tile]
     packed = jnp.concatenate(pieces, axis=0)
     pay[:, p // 4 : p // 4 + half] = jnp.where(iota((rows, half), 1) < SEG, tail, packed).astype(BF)
-    send(p // 4)
     for copy in copies:
         copy.wait()
 
@@ -228,36 +220,39 @@
 
 
 def readout_kernel(
-    scale, count, target, pay, mask_near, mask_in, wt, rbias, pooled_grad, loss, mask_late, proj0, proj1, mixed, acc, sems
+    scale,
+    where,
+    count,
+    target,
+    pay,
+    mask,
+    wt,
+    rbias,
+    pooled_grad,
+    loss,
+    mask_own,
+    wt_own,
+    proj0,
+    proj1,
+    mixed,
+    acc,
 ):
-    pooled_n, early = mask_near.shape
-    neurons = early + mask_late.shape[1]
+    pooled_n, neurons = mask.shape
+    own = mask_own.shape[1]
     channels = wt.shape[0]
     frames = target.shape[0]
     proj = (proj0, proj1)
     block = proj0.shape[1]
     steps = neurons // block
-    copies = {}
-    for at in range(early, neurons, block):
-        lanes = slice(at - early, at - early + block)
-        copies[at] = pltpu.make_async_copy(
-            mask_in.at[:, at : at + block], mask_late.at[:, lanes], sems.at[(at - early) // block]
-        )
-        copies[at].start()
-
-    def mask_part(at, size):
-        if at < early:
-            return mask_near[:, at : at + size]
-        return mask_late[:, at - early : at - early + size]
-
+    first = pl.multiple_of(where[0] * own, own)
+    mask_own[...] = mask[:, pl.ds(first, own)]
+    wt_own[...] = wt[:, pl.ds(first, own)]
     pooled = pay[:, 0:pooled_n]
     loss_sum = jnp.zeros((frames, block), F32)
     begun = False
     for t in range(steps + 2):
         if t < steps:
-            if t * block in copies:
-                copies[t * block].wait()
-            proj[t % 2][...] = dot(pooled, mask_part(t * block, block))
+            proj[t % 2][...] = dot(pooled, mask[:, t * block : (t + 1) * block])
         if 1 <= t <= steps:
             at = slice((t - 1) * block, t * block)
             w = wt[:, at].astype(F32)
@@ -267,10 +262,11 @@
             loss_sum = loss_sum + jnp.where(alive, rate - goal * jnp.log(rate), 0.0)
             for f in range(frames):
                 mixed[f * channels : (f + 1) * channels, at] = (grad[f : f + 1] * w).astype(BF)
-        if t >= 2 and (t % 2 == 1 or t == steps + 1):
-            low = ((t - 2) // 2) * 2 * block
-            at = slice(low, (t - 1) * block)
-            part = dot(mask_part(low, (t - 1) * block - low), mixed[:, at], NT)
+        last = t - 2
+        if last >= 0 and (last % 2 == 0 or last == steps - 1):
+            low = (last - 1 if last > 0 and last % 2 == 0 else last) * block
+            at = slice(low, (last + 1) * block)
+            part = dot(mask[:, at], mixed[:, at], NT)
             acc[...] = acc[...] + part if begun else part
             begun = True
     pooled_grad[...] = acc[...].T.astype(BF)
@@ -350,24 +346,24 @@
     upper = jnp.where(low == used - 128, mix_bias_grad, upper)
     upper = jnp.where((low == used - 127) & (iota((channels, 128), 0) == 0), loss[0:1, 0:1], upper)
     upper = jnp.where(low >= channels, folded, upper)
-    pieces, lines, _ = out.shape
-    both = jnp.concatenate([conv[:, 0:128], upper], axis=0)
-    for k in range(pieces):
-        out[k] = both[k * lines : (k + 1) * lines, :]
-
-
-def share_kernel(parts, out):
-    total = parts.shape[0]
-    tile = parts[0]
-    for d in range(1, total):
-        tile = tile + parts[d]
-    for d in range(total):
-        out[d] = tile
-
-
-def unpack_kernel(parts, conv, conv_bias, mix, mix_bias, loss):
+    out[0:channels, :] = conv[:, 0:128]
+    out[channels:, :] = upper
+
+
+def pair_sum(values):
+    while len(values) > 1:
+        values = [values[k] + values[k + 1] for k in range(0, len(values), 2)]
+    return values[0]
+
+
+def add_kernel(*refs):
+    refs[-1][...] = pair_sum([ref[...] for ref in refs[:-1]])
+
+
+def unpack_kernel(*refs):
+    conv, conv_bias, mix, mix_bias, loss = refs[-5:]
     channels, taps = conv.shape
-    both = jnp.concatenate([parts[k] for k in range(parts.shape[0])], axis=0)
+    both = pair_sum([ref[...] for ref in refs[:-5]])
     low = both[0:channels]
     high = both[channels:]
     rest = taps - 128
@@ -379,32 +375,21 @@
     loss[...] = high[0:1, rest + 2 : rest + 3]
 
 
-def owned_rows_kernel(scale, clips, own, block, held, where, count, *refs):
-    sent = refs[:clips]
-    wt_in, mask_in, rbias = refs[clips : clips + 3]
+def owned_rows_kernel(scale, clips, own, block, held, last, where, count, *refs):
+    pays = refs[:clips]
+    wt, rbias, mask = refs[clips : clips + 3]
     before = refs[clips + 3 : clips + 3 + held]
-    outs = refs[clips + 3 + held : -10]
-    pays, wt, proj0, proj1, mixed0, mixed1, turned, mask, stage, sems = refs[-10:]
+    outs = refs[clips + 3 + held : -7]
+    proj0, proj1, mixed0, mixed1, turned, stage, sems = refs[-7:]
     proj = (proj0, proj1)
     mixed = (mixed0, mixed1)
     pooled_n = mask.shape[0]
     channels = wt.shape[0]
     low_rows = pooled_n + channels
-    rows = pays.shape[1]
+    rows = pays[0].shape[0]
     frames = rows // channels
     steps = own // block
     first = pl.multiple_of(where[0] * own, own)
-    fetches = []
-    for k in range(steps):
-        lanes = pl.ds(pl.multiple_of(first + k * block, block), block)
-        fetches.append(pltpu.make_async_copy(mask_in.at[:, lanes], mask.at[:, k * block : (k + 1) * block], sems.at[k]))
-    arrive = [pltpu.make_async_copy(sent[c], pays.at[c], sems.at[2 * steps + c]) for c in range(clips)]
-    weights = pltpu.make_async_copy(wt_in.at[:, pl.ds(first, own)], wt, sems.at[2 * steps + clips])
-    arrive[0].start()
-    fetches[0].start()
-    weights.start()
-    for copy in arrive[1:] + fetches[1:]:
-        copy.start()
     segs = block // SEG
     low = iota((frames, 128), 1) < SEG
     items = [(k, c) for k in range(steps) for c in range(clips)]
@@ -415,18 +400,13 @@
         if t < len(items):
             k, c = items[t]
             if k == 0:
-                arrive[c].wait()
-                turned[:, c * rows : (c + 1) * rows] = pays[c, :, 0:pooled_n].T
-            if c == 0:
-                fetches[k].wait()
-            if t == 0:
-                weights.wait()
-            proj[t % 2][...] = dot(pays[c, :, 0:pooled_n], mask[:, k * block : (k + 1) * block])
+                turned[:, c * rows : (c + 1) * rows] = pays[c][:, 0:pooled_n].T
+            proj[t % 2][...] = dot(pays[c][:, 0:pooled_n], mask[:, k * block : (k + 1) * block])
         if 1 <= t <= len(items):
             k, c = items[t - 1]
             start = pl.multiple_of(first + k * block, block)
             base = pl.multiple_of(start // SEG * frames, segs * frames)
-            packed = pays[c, pl.ds(base, segs * frames), pooled_n - SEG : pooled_n + SEG].astype(F32)
+            packed = pays[c][pl.ds(base, segs * frames), pooled_n - SEG : pooled_n + SEG].astype(F32)
             tiles = []
             for j in range(0, segs, 2):
                 even = packed[j * frames : (j + 1) * frames]
@@ -446,16 +426,21 @@
             k = items[t - 2][0]
             at = slice(k * block, (k + 1) * block)
             total = dot(turned[...], mixed[k % 2][...])
+            feat = feats[k]
             bias = jnp.sum(biases[k], axis=0, keepdims=True)
             if held:
-                stage[:, at] = total + before[0][0:pooled_n, at]
-                outs[1][:, at] = feats[k] + before[0][pooled_n:low_rows, at]
-                outs[2][:, at] = bias + before[0][low_rows : low_rows + 1, at]
-                stores.append(pltpu.make_async_copy(stage.at[:, at], outs[0].at[:, at], sems.at[steps + k]))
+                total = total + before[0][0:pooled_n, at]
+                feat = feat + before[0][pooled_n:low_rows, at]
+                bias = bias + before[0][low_rows : low_rows + 1, at]
+            if last:
+                stage[:, at] = total
+                outs[1][:, at] = feat
+                outs[2][:, at] = bias
+                stores.append(pltpu.make_async_copy(stage.at[:, at], outs[0].at[:, at], sems.at[k]))
                 stores[-1].start()
             else:
                 outs[0][0:pooled_n, at] = total
-                outs[0][pooled_n:low_rows, at] = feats[k]
+                outs[0][pooled_n:low_rows, at] = feat
                 outs[0][low_rows:, at] = jnp.broadcast_to(bias, (8, block))
     for store in stores:
         store.wait()
@@ -471,6 +456,15 @@
 
 def in_hbm(*arrays):
     return [pltpu.with_memory_space_constraint(a, pltpu.HBM) for a in arrays]
+
+
+def rounds_of(size):
+    assert size & (size - 1) == 0
+    bits = [1 << k for k in range(size.bit_length() - 1)]
+    groups = [bits[:1]] if len(bits) % 2 else []
+    bits = bits[len(bits) % 2 :]
+    groups += [[low, low * 2, low * 3] for low in bits[::2]]
+    return groups
 
 
 def xor_pairs(size, mask):
@@ -482,7 +476,6 @@
 ):
     sess_total = lax.axis_size("sess")
     clip_total = lax.axis_size("clip")
-    total = sess_total * clip_total
     clip_block, frame_block, pix = video.shape
     neurons = responses.shape[2]
     pooled_n = masks.shape[2]
@@ -530,62 +523,56 @@
     wt = jnp.swapaxes(feat_w, 1, 2).reshape(channels, neurons)
     mask_t = jnp.swapaxes(masks, 1, 2).reshape(pooled_n, neurons)
     rbias = readout_bias
-    mask_far, wt_far = in_hbm(mask_t, wt)
+    (mask_far,) = in_hbm(mask_t)
     width = pooled_n + SEG
-    early = neurons // 2
     vmem = pl.BlockSpec(memory_space=pltpu.VMEM)
     anywhere = pl.BlockSpec(memory_space=pl.ANY)
     smem = pl.BlockSpec(memory_space=pltpu.SMEM)
-    pay, pay_send, target, act1, slope1, slope2, xcol, mask_near = pl.pallas_call(
+    pay, target, act1, slope1, slope2, xcol, mask_near = pl.pallas_call(
         core_forward_kernel,
         out_shape=(
-            jax.ShapeDtypeStruct((rows, width), BF),
             jax.ShapeDtypeStruct((rows, width), BF),
             jax.ShapeDtypeStruct((frames, neurons), F32),
             jax.ShapeDtypeStruct((rows, pix), BF),
             jax.ShapeDtypeStruct((rows, pix), BF),
             jax.ShapeDtypeStruct((rows, pix), BF),
             jax.ShapeDtypeStruct((patch_cols, pix), BF),
-            jax.ShapeDtypeStruct((pooled_n, early), BF),
+            jax.ShapeDtypeStruct((pooled_n, neurons), BF),
         ),
         in_specs=[vmem] * 5 + [anywhere],
-        out_specs=(vmem, anywhere) + (vmem,) * 6,
         scratch_shapes=[pltpu.VMEM((rows, CHUNK), F32)] * 4
-        + [pltpu.VMEM((rows, pix), BF), pltpu.SemaphoreType.DMA((early // 512 + width // half,))],
+        + [pltpu.VMEM((rows, pix), BF), pltpu.SemaphoreType.DMA((pooled_n // SEG,))],
         compiler_params=params(),
         cost_estimate=cost(2 * rows * pix * patch_cols, 8 * rows * pix),
         name="core_forward",
     )(recv, wbig, blocks, bias, pool, mask_far)
 
-    (pay_send,) = in_hbm(pay_send)
-    near = {0: pay_send}
+    near = {0: pay}
     for mask in range(1, clip_total):
         if mask % 2 == 0 or mask == 1:
-            near[mask] = lax.ppermute(pay_send, "clip", xor_pairs(clip_total, mask))
+            near[mask] = lax.ppermute(pay, "clip", xor_pairs(clip_total, mask))
 
     big = min(512, neurons)
     work = 2 * rows * neurons * pooled_n
-    pooled_grad, loss = pl.pallas_call(
+    pooled_grad, loss, mask_own, wt_own = pl.pallas_call(
         functools.partial(readout_kernel, scale),
-        in_specs=[smem] + [vmem] * 3 + [anywhere] + [vmem] * 2,
-        out_shape=(jax.ShapeDtypeStruct((rows, pooled_n), BF), jax.ShapeDtypeStruct((8, 128), F32)),
-        scratch_shapes=[pltpu.VMEM((pooled_n, neurons - early), BF)]
-        + [pltpu.VMEM((rows, big), F32)] * 2
-        + [
-            pltpu.VMEM((rows, neurons), BF),
-            pltpu.VMEM((pooled_n, rows), F32),
-            pltpu.SemaphoreType.DMA(((neurons - early) // big,)),
-        ],
+        in_specs=[smem, smem] + [vmem] * 5,
+        out_shape=(
+            jax.ShapeDtypeStruct((rows, pooled_n), BF),
+            jax.ShapeDtypeStruct((8, 128), F32),
+            jax.ShapeDtypeStruct((pooled_n, own), BF),
+            jax.ShapeDtypeStruct((channels, own), BF),
+        ),
+        scratch_shapes=[pltpu.VMEM((rows, big), F32)] * 2
+        + [pltpu.VMEM((rows, neurons), BF), pltpu.VMEM((pooled_n, rows), F32)],
         compiler_params=params(),
         cost_estimate=cost(2 * work, 2 * neurons * pooled_n),
         name="readout",
-    )(counts, target, pay, mask_near, mask_far, wt, rbias)
-
-    assert 2 * channels % total == 0
-    pieces = (total, 2 * channels // total, 128)
+    )(where, counts, target, pay, mask_near, wt, rbias)
+
     core = pl.pallas_call(
         functools.partial(core_backward_kernel, channels),
-        out_shape=jax.ShapeDtypeStruct(pieces, F32),
+        out_shape=jax.ShapeDtypeStruct((2 * channels, 128), F32),
         scratch_shapes=[pltpu.VMEM((rows, CHUNK), F32)] * 4
         + [pltpu.VMEM((rows, pix), BF)] * 2
         + [pltpu.VMEM((PACK, patch_cols), BF)],
@@ -594,14 +581,10 @@
         name="core_backward",
     )(pooled_grad, loss, act1, slope1, slope2, xcol, blocks_t)
 
-    axes = ("clip", "sess")
-    parts = lax.all_to_all(core, axes, split_axis=0, concat_axis=0, tiled=True)
-
-    def owned_rows(clips, held, block):
-        last = len(held) > 0
+    def owned_rows(clips, held, last):
         return pl.pallas_call(
-            functools.partial(owned_rows_kernel, scale, len(clips), own, block, len(held)),
-            in_specs=[smem, smem] + [anywhere] * (len(clips) + 2) + [vmem] * (1 + len(held)),
+            functools.partial(owned_rows_kernel, scale, len(clips), own, block, len(held), last),
+            in_specs=[smem, smem] + [vmem] * (len(clips) + 3 + len(held)),
             out_specs=[anywhere, vmem, vmem] if last else [vmem],
             out_shape=[
                 jax.ShapeDtypeStruct((pooled_n, own), F32),
@@ -610,35 +593,38 @@
             ]
             if last
             else [jax.ShapeDtypeStruct((pooled_n + channels + 8, own), F32)],
-            scratch_shapes=[pltpu.VMEM((len(clips), rows, width), BF), pltpu.VMEM((channels, own), BF)]
-            + [pltpu.VMEM((rows, block), F32)] * 2
+            scratch_shapes=[pltpu.VMEM((rows, block), F32)] * 2
             + [pltpu.VMEM((len(clips) * rows, block), BF)] * 2
             + [
                 pltpu.VMEM((pooled_n, len(clips) * rows), BF),
-                pltpu.VMEM((pooled_n, own), BF),
                 pltpu.VMEM((pooled_n, own) if last else (8, 128), F32),
-                pltpu.SemaphoreType.DMA((2 * (own // block) + len(clips) + 1,)),
+                pltpu.SemaphoreType.DMA((own // block,)),
             ],
             compiler_params=params(rows),
             cost_estimate=cost(2 * work * len(clips) // clip_total, 4 * own * pooled_n),
             name="owned_rows",
-        )(where, counts, *in_hbm(*clips), wt_far, mask_far, rbias, *held)
+        )(where, counts, *clips, wt_own, rbias, mask_own, *held)
 
     far = [mask for mask in near if mask > 1]
     reached, _ = lax.optimization_barrier(([near[mask] for mask in far], core))
     others = [lax.ppermute(value, "clip", xor_pairs(clip_total, 1)) for value in reached]
-    (partial,) = owned_rows([near[0], near[1]] + reached, (), block)
-    parts, partial = lax.optimization_barrier((parts, partial))
-    copies = pl.pallas_call(
-        share_kernel,
-        out_shape=jax.ShapeDtypeStruct(pieces, F32),
-        compiler_params=params(),
-        name="share",
-    )(parts)
-    summed = lax.all_to_all(copies, axes, split_axis=0, concat_axis=0, tiled=True)
-    readout_grads = owned_rows(others, (partial,), max(128, block // 2))
-    summed, readout_grads = lax.optimization_barrier((summed, readout_grads))
-    mask_grad, feat_grad, grad_rbias = readout_grads
+    work_of = [[near[0], near[1]], reached, others]
+    rounds = [("clip", masks) for masks in rounds_of(clip_total)] + [("sess", masks) for masks in rounds_of(sess_total)]
+    held = ()
+    for step, (axis, masks) in enumerate(rounds):
+        got = [core] + [lax.ppermute(core, axis, xor_pairs(lax.axis_size(axis), mask)) for mask in masks]
+        if step < len(work_of):
+            held = owned_rows(work_of[step], held, step == len(work_of) - 1)
+            got, held = lax.optimization_barrier((got, held))
+        if step < len(rounds) - 1:
+            core = pl.pallas_call(
+                add_kernel,
+                out_shape=jax.ShapeDtypeStruct(core.shape, F32),
+                compiler_params=params(),
+                name="add",
+            )(*got)
+            core, held = lax.optimization_barrier((core, held))
+    mask_grad, feat_grad, grad_rbias = held
     grad_conv, grad_cb, grad_mix, grad_mb, loss = pl.pallas_call(
         unpack_kernel,
         out_shape=(
@@ -650,7 +636,7 @@
         ),
         compiler_params=params(),
         name="unpack",
-    )(summed)
+    )(*got)
     return (
         loss.reshape(()),
         grad_conv,

time: 62.3 us -> 57.7 us (0.926)
  Pallas kernels: 34.5 us -> 29.2 us
  waiting for transfers between devices: 8.76 us -> 11 us
  starting transfers between devices: 17.2 us -> 15.7 us
    all_to_all x2 -> x0, starting transfers between devices: 8.31 us -> none  [the longest x1 5.51 us: per_device(): lax.all_to_all(copies, axes, split_axis=0, concat_axis=0, tiled=True)]
    ppermute x2 -> x9, starting transfers between devices: 1.59 us -> 8.46 us  [the longest x7 6.88 us: per_device(): lax.ppermute(core, axis, xor_pairs(lax.axis_size(axis), mask))]
    ppermute x2 -> x9, waiting for transfers between devices: 1.56 us -> 5.64 us  [the longest x2 3.01 us: per_device(): near[mask] = lax.ppermute(pay, 'clip', xor_pairs(clip_total, mask))]
    pallas_call x2 -> x3, Pallas kernels: 12.7 us -> 8.86 us  [owned_rows(): pl.pallas_call(functools.partial(owned_rows_kernel, scale, len(clips), ow...]
    all_to_all x2 -> x0, waiting for transfers between devices: 1.82 us -> none  [the longest x1 1.49 us: per_device(): lax.all_to_all(copies, axes, split_axis=0, concat_axis=0, tiled=True)]
    pallas_call x2 -> x3, Pallas kernels: 7.77 us -> 6.17 us  [the longest x1 6.14 us: per_device(): pl.pallas_call(functools.partial(readout_kernel, scale), in_specs=[smem,...]
    pallas_call x1, Pallas kernels: 5.25 us -> 5.97 us  [per_device(): pl.pallas_call(core_forward_kernel, out_shape=(jax.ShapeDtypeStruct((rows...]
  transfers between devices with their start and end apart: 6 -> 11, of which waited for: 4 -> 4; matrix products, arithmetic and copies ran while one was open for 0% -> 0% of each run, Pallas kernels for 43% -> 36%
where the time goes in v6:
time: 57.7 us; the launch traced here: 57.4 us
  Pallas kernels  29.2 us (51%)
  starting transfers between devices  15.7 us (27%)
  waiting for transfers between devices  11 us (19%)
  between operations  1.4 us (2%)
    pallas_call x3, Pallas kernels, owned_rows(): pl.pallas_call(functools.partial(owned_rows_kernel, scale, len(clips), ow...  8.86 us
    all_to_all x1, starting transfers between devices, per_device(): recv = lax.all_to_all(send, 'sess', split_axis=0, concat_axis=0, tiled=True)  7.28 us
    ppermute x7, starting transfers between devices, per_device(): lax.ppermute(core, axis, xor_pairs(lax.axis_size(axis), mask))  6.88 us
    pallas_call x1, Pallas kernels, per_device(): pl.pallas_call(functools.partial(readout_kernel, scale), in_specs=[smem,...  6.14 us
    pallas_call x1, Pallas kernels, per_device(): pl.pallas_call(core_forward_kernel, out_shape=(jax.ShapeDtypeStruct((rows...  5.97 us
    all_to_all x1, waiting for transfers between devices, per_device(): recv = lax.all_to_all(send, 'sess', split_axis=0, concat_axis=0, tiled=True)  5.37 us
    pallas_call x1, Pallas kernels, per_device(): pl.pallas_call(functools.partial(core_backward_kernel, channels), out_sha...  4.34 us
    ppermute x2, waiting for transfers between devices, per_device(): near[mask] = lax.ppermute(pay, 'clip', xor_pairs(clip_total, mask))  3.01 us
  transfers between devices with their start and end apart: 11, of which 4 were waited for; matrix products, arithmetic and copies ran while one was open for 0% of the time, Pallas kernels for 36%

profile of v6, /device:TPU:0, one launch (start us, length us, event | category | flops | bytes accessed | tf_op | source)
XLA Modules:
  0.0 57.4 jit_solution(3282464572109732704)
XLA Ops:
  0.6 1.8 %select.1 = bf16[8,16,512]{2,1,0:T(8,128)(2,1)} custom-call(s32[1,8]{1,0:T(1,128)} %bitcast.25, bf16[8,2304]{1,0:T(8,128)(2,1)} %bitcast.24, bf16[8,4096]{1,0:T(8,128)(2,1)} %bitcast.23), custom_call_target="tpu_custom_call" | custom-call | tf_op jit(solution)/shard_map/select/pallas_call | solution.py:495
  2.5 7.3 %all-to-all-start = ((bf16[8,16,512]{2,1,0:T(8,128)(2,1)}), bf16[8,16,512]{2,1,0:T(8,128)(2,1)S(1)}, u32[]{:S(2)}, u32[]{:S(2)}) async-start(bf16[8,16,512]{2,1,0:T(8,128)(2,1)} %select.1), calls=%async_computation | async-start | bytes 262144 | tf_op jit(solution)/shard_map/all_to_all | solution.py:503
  10.4 1.3 %prep.1 = (bf16[512,448]{1,0:T(8,128)(2,1)S(1)}, bf16[256,256]{1,0:T(8,128)(2,1)S(1)}, bf16[256,256]{1,0:T(8,128)(2,1)S(1)}, f32[2,64,128]{2,1,0:T(8,128)S(1)}, bf16[512,128]{1,0:T(8,128)(2,1)S(1)}) custom-call(bf16[64,147]{1,0:T(8,128)(2,1)} %weight.1, f32[1,64]{1,0:T(1,128)} %bitcast.28, bf16[64,64]{1,0:T(8,128)(2,1)} %mix.1, f32[1,64]{1,0:T(1,128)} %bitcast.29), custom_call_target="tpu_custom_call" | custom-call | flops 134217728 | bytes 1048576 | tf_op jit(solution)/shard_map/prep/pallas_call | solution.py:508
  11.7 5.4 %all-to-all-done.recv = bf16[8,16,512]{2,1,0:T(8,128)(2,1)S(1)} async-done(((bf16[8,16,512]{2,1,0:T(8,128)(2,1)}), bf16[8,16,512]{2,1,0:T(8,128)(2,1)S(1)}, u32[]{:S(2)}, u32[]{:S(2)}) %all-to-all-start) | async-done | bytes 131104 | tf_op jit(solution)/shard_map/all_to_all | solution.py:503
  17.1 0.0 copy-start
  17.1 0.0 copy-start.1
  17.1 6.0 %core_forward.1 = (bf16[512,640]{1,0:T(8,128)(2,1)S(1)}, f32[8,4096]{1,0:T(8,128)S(1)}, bf16[512,2304]{1,0:T(8,128)(2,1)S(1)}, bf16[512,2304]{1,0:T(8,128)(2,1)S...) custom-call(bf16[8,16,512]{2,1,0:T(8,128)(2,1)S(1)} %all-to-all-done.recv, ...), custom_call_target="tpu_custom_call" | custom-call | flops 1056964608 | bytes 9437184 | tf_op jit(solution)/shard_map/core_forward/pallas_call | solution.py:531
  23.1 1.6 %collective-permute-start.5 = (bf16[512,640]{1,0:T(8,128)(2,1)S(1)}, bf16[512,640]{1,0:T(8,128)(2,1)S(1)}, u32[]{:S(2)}, u32[]{:S(2)}) collective-permute-start(bf16[512,640]{1,0:T(8,128)(2,1)S(1)} %get-tuple-element.61.pay.refs_0_), channel_id=1, source_target_pairs={{0,16},{8,24},{16,0},{24,8},{1,17},{9,25},{17,1},{25,9},{2,18},{10... | collective-permute-start | bytes 1966088 | tf_op jit(solution)/shard_map/ppermute | solution.py:553
  24.7 0.0 collective-permute-start.3
  24.7 0.0 copy-done
  24.7 0.0 copy-done.1
  24.7 6.1 %readout.1 = (bf16[512,576]{1,0:T(8,128)(2,1)S(1)}, f32[8,128]{1,0:T(8,128)S(1)}, bf16[576,1024]{1,0:T(8,128)(2,1)S(1)}, bf16[64,1024]{1,0:T(8,128)(2,1)S(1)}) custom-call(s32[1]{0:T(128)} %bitcast.3.where, s32[1]{0:T(128)S(6)} %copy.19.count, f32[8,4096]{1,0:T(8,128)S(1)} %get-tuple-element.60.target, bf16[512,640]{1,0:T(8,128)(2,1)S(1)} %get-tuple-element.61.pay.refs_0_, ...), custom_call_target="tpu_custom_call" | custom-call | flops 4831838208 | bytes 4718592 | tf_op jit(solution)/shard_map/readout/pallas_call | solution.py:557
  30.8 4.3 %core_backward.1.refs_0_ = f32[128,128]{1,0:T(8,128)S(1)} custom-call(bf16[512,576]{1,0:T(8,128)(2,1)S(1)} %get-tuple-element.63.pooled_grad, f32[8,128]{1,0:T(8,128)S(1)} %get-tuple-element.64.loss, bf16[512,2304]{1,0:T(8,128)(2,1)S(1)} %get-tuple-element.65.act1, bf16[512,2304]{1,0:T(8,128)(2,1)S(1)} %get-tuple-element.66.slope1, ...), custom_call_target="tpu_custom_call" | custom-call | flops 4831838208 | bytes 9437184 | tf_op jit(solution)/shard_map/core_backward/pallas_call | solution.py:573
  35.2 3.0 %collective-permute-done.5.refs_0_ = bf16[512,640]{1,0:T(8,128)(2,1)S(1)} collective-permute-done((bf16[512,640]{1,0:T(8,128)(2,1)S(1)}, bf16[512,640]{1,0:T(8,128)(2,1)S(1)}, u32[]{:S(2)}, u32[]{:S(2)}) %collective-permute-start.5) | collective-permute-done | bytes 655392 | tf_op jit(solution)/shard_map/ppermute | solution.py:553
  38.2 0.0 collective-permute-start.9
  38.2 1.6 %collective-permute-start.2 = (f32[128,128]{1,0:T(8,128)S(1)}, f32[128,128]{1,0:T(8,128)S(1)}, u32[]{:S(2)}, u32[]{:S(2)}) collective-permute-start(f32[128,128]{1,0:T(8,128)S(1)} %core_backward.1.refs_0_), channel_id=1, source_target_pairs={{0,24},{8,16},{16,8},{24,0},{1,25},{9,17},{17,9},{25,1},{2,26},{10... | collective-permute-start | bytes 196616 | tf_op jit(solution)/shard_map/ppermute | solution.py:615
  39.8 0.5 collective-permute-start.1
  40.3 0.0 collective-permute-start
  40.3 0.0 collective-permute-done.3.refs_1_
  40.3 3.3 %owned_rows.3.refs_4_ = f32[648,1024]{1,0:T(8,128)S(1)} custom-call(s32[1]{0:T(128)} %bitcast.3.where, s32[1]{0:T(128)S(6)} %copy.19.count, bf16[512,640]{1,0:T(8,128)(2,1)S(1)} %get-tuple-element.61.pay.refs_0_, bf16[512,640]{1,0:T(8,128)(2,1)S(1)} %collective-permute-done.3.refs_1_, bf16[64,1024]{1,0:T(8,128)(2,1)S(1)} %get-tuple-element.70.refs_2_.refs_1_, ...), custom_call_target="tpu_custom_call" | custom-call | flops 2415919104 | bytes 2359296 | tf_op jit(solution)/shard_map/owned_rows/pallas_call | solution.py:585
  43.6 0.0 collective-permute-done.2.refs_3_
  43.6 0.5 collective-permute-done.1.refs_2_
  44.1 0.0 collective-permute-done.refs_1_
  44.1 0.3 collective-permute-start.4
  44.4 1.9 %owned_rows.4.refs_4_ = f32[648,1024]{1,0:T(8,128)S(1)} custom-call(s32[1]{0:T(128)} %bitcast.3.where, s32[1]{0:T(128)S(6)} %copy.19.count, bf16[512,640]{1,0:T(8,128)(2,1)S(1)} %collective-permute-done.5.refs_0_, bf16[64,1024]{1,0:T(8,128)(2,1)S(1)} %get-tuple-element.70.refs_2_.refs_1_, f32[1,4096]{1,0:T(1,128)S(1)} %copy-done, ...), custom_call_target="tpu_custom_call" | custom-call | flops 1207959552 | bytes 2359296 | tf_op jit(solution)/shard_map/owned_rows/pallas_call | solution.py:585
  46.3 2.2 %collective-permute-done.4.refs_1_ = f32[128,128]{1,0:T(8,128)S(1)} collective-permute-done((f32[128,128]{1,0:T(8,128)S(1)}, f32[128,128]{1,0:T(8,128)S(1)}, u32[]{:S(2)}, u32[]{:S(2)}) %collective-permute-start.4) | collective-permute-done | bytes 65568 | tf_op jit(solution)/shard_map/ppermute | solution.py:615
  48.5 0.9 %collective-permute-start.8 = (f32[128,128]{1,0:T(8,128)S(1)}, f32[128,128]{1,0:T(8,128)S(1)}, u32[]{:S(2)}, u32[]{:S(2)}) collective-permute-start(f32[128,128]{1,0:T(8,128)S(1)} %add.3.refs_0_), channel_id=1, source_target_pairs={{0,6},{1,7},{2,4},{3,5},{4,2},{5,3},{6,0},{7,1},{8,14},{9,15},{10,... | collective-permute-start | bytes 196616 | tf_op jit(solution)/shard_map/ppermute | solution.py:615
  49.4 0.5 collective-permute-start.7
  49.9 3.0 %collective-permute-start.6 = (f32[128,128]{1,0:T(8,128)S(1)}, f32[128,128]{1,0:T(8,128)S(1)}, u32[]{:S(2)}, u32[]{:S(2)}) collective-permute-start(f32[128,128]{1,0:T(8,128)S(1)} %add.3.refs_0_), channel_id=1, source_target_pairs={{0,2},{1,3},{2,0},{3,1},{4,6},{5,7},{6,4},{7,5},{8,10},{9,11},{10,... | collective-permute-start | bytes 196616 | tf_op jit(solution)/shard_map/ppermute | solution.py:615
  52.9 0.0 collective-permute-done.9.refs_0_
  52.9 3.7 %owned_rows.5 = (f32[576,1024]{1,0:T(8,128)}, f32[64,1024]{1,0:T(8,128)}, f32[1,1024]{1,0:T(1,128)}) custom-call(s32[1]{0:T(128)} %bitcast.3.where, s32[1]{0:T(128)S(6)} %copy.19.count, bf16[512,640]{1,0:T(8,128)(2,1)S(1)} %collective-permute-done.9.refs_0_, bf16[64,1024]{1,0:T(8,128)(2,1)S(1)} %get-tuple-element.70.refs_2_.refs_1_, f32[1,4096]{1,0:T(1,128)S(1)} %copy-done, ...), custom_call_target="tpu_custom_call" | custom-call | flops 1207959552 | bytes 2359296 | tf_op jit(solution)/shard_map/owned_rows/pallas_call | solution.py:585
  56.6 0.0 collective-permute-done.8.refs_3_
  56.6 0.0 collective-permute-done.7.refs_2_
  56.6 0.0 collective-permute-done.6.refs_1_
  56.7 0.7 %unpack.1 = (f32[64,147]{1,0:T(8,128)}, f32[1,64]{1,0:T(1,128)}, f32[64,64]{1,0:T(8,128)}, f32[1,64]{1,0:T(1,128)}, f32[1,1]{1,0:T(1,128)}) custom-call(f32[128,128]{1,0:T(8,128)S(1)} %add.3.refs_0_, f32[128,128]{1,0:T(8,128)S(1)} %collective-permute-done.6.refs_1_, f32[128,128]{1,0:T(8,128)S(1)} %collective-permute-done.7.refs_2_, ...), custom_call_target="tpu_custom_call" | custom-call | tf_op jit(solution)/shard_map/unpack/pallas_call | solution.py:628
  (2 shorter events, 0.0 us)
Async XLA Ops:
  2.5 14.6 %all-to-all-start = ((bf16[8,16,512]{2,1,0:T(8,128)(2,1)}), bf16[8,16,512]{2,1,0:T(8,128)(2,1)S(1)}, u32[]{:S(2)}, u32[]{:S(2)}) async-start(bf16[8,16,512]{2,1,0:T(8,128)(2,1)} %select.1), calls=%async_computation | async-start | bytes 262144 | tf_op jit(solution)/shard_map/all_to_all | solution.py:503
  17.1 7.6 %copy-start = (f32[1,4096]{1,0:T(1,128)S(1)}, f32[1,4096]{1,0:T(1,128)}, u32[]{:S(2)}) copy-start(f32[1,4096]{1,0:T(1,128)} %refs_2_.3) | copy-start | bytes 49156
  17.1 7.6 %copy-start.1 = (bf16[1,4096,64]{1,2,0:T(8,128)(2,1)S(1)}, bf16[1,4096,64]{1,2,0:T(8,128)(2,1)}, u32[]{:S(2)}) copy-start(bf16[1,4096,64]{1,2,0:T(8,128)(2,1)} %param.20) | copy-start | bytes 1572868
  23.1 15.1 %collective-permute-start.5 = (bf16[512,640]{1,0:T(8,128)(2,1)S(1)}, bf16[512,640]{1,0:T(8,128)(2,1)S(1)}, u32[]{:S(2)}, u32[]{:S(2)}) collective-permute-start(bf16[512,640]{1,0:T(8,128)(2,1)S(1)} %get-tuple-element.61.pay.refs_0_), channel_id=1, source_target_pairs={{0,16},{8,24},{16,0},{24,8},{1,17},{9,25},{17,1},{25,9},{2,18},{10... | collective-permute-start | bytes 1966088 | tf_op jit(solution)/shard_map/ppermute | solution.py:553
  24.7 15.7 %collective-permute-start.3 = (bf16[512,640]{1,0:T(8,128)(2,1)S(1)}, bf16[512,640]{1,0:T(8,128)(2,1)S(1)}, u32[]{:S(2)}, u32[]{:S(2)}) collective-permute-start(bf16[512,640]{1,0:T(8,128)(2,1)S(1)} %get-tuple-element.61.pay.refs_0_), channel_id=1, source_target_pairs={{0,8},{8,0},{16,24},{24,16},{1,9},{9,1},{17,25},{25,17},{2,10},{10... | collective-permute-start | bytes 1966088 | tf_op jit(solution)/shard_map/ppermute | solution.py:553
  38.2 14.7 %collective-permute-start.9 = (bf16[512,640]{1,0:T(8,128)(2,1)S(1)}, bf16[512,640]{1,0:T(8,128)(2,1)S(1)}, u32[]{:S(2)}, u32[]{:S(2)}) collective-permute-start(bf16[512,640]{1,0:T(8,128)(2,1)S(1)} %collective-permute-done.5.refs_0_), channel_id=1, source_target_pairs={{0,8},{8,0},{16,24},{24,16},{1,9},{9,1},{17,25},{25,17},{2,10},{10... | collective-permute-start | bytes 1966088 | tf_op jit(solution)/shard_map/ppermute | solution.py:610
  38.2 5.4 %collective-permute-start.2 = (f32[128,128]{1,0:T(8,128)S(1)}, f32[128,128]{1,0:T(8,128)S(1)}, u32[]{:S(2)}, u32[]{:S(2)}) collective-permute-start(f32[128,128]{1,0:T(8,128)S(1)} %core_backward.1.refs_0_), channel_id=1, source_target_pairs={{0,24},{8,16},{16,8},{24,0},{1,25},{9,17},{17,9},{25,1},{2,26},{10... | collective-permute-start | bytes 196616 | tf_op jit(solution)/shard_map/ppermute | solution.py:615
  39.8 4.3 %collective-permute-start.1 = (f32[128,128]{1,0:T(8,128)S(1)}, f32[128,128]{1,0:T(8,128)S(1)}, u32[]{:S(2)}, u32[]{:S(2)}) collective-permute-start(f32[128,128]{1,0:T(8,128)S(1)} %core_backward.1.refs_0_), channel_id=1, source_target_pairs={{0,16},{8,24},{16,0},{24,8},{1,17},{9,25},{17,1},{25,9},{2,18},{10... | collective-permute-start | bytes 196616 | tf_op jit(solution)/shard_map/ppermute | solution.py:615
  40.3 3.8 %collective-permute-start = (f32[128,128]{1,0:T(8,128)S(1)}, f32[128,128]{1,0:T(8,128)S(1)}, u32[]{:S(2)}, u32[]{:S(2)}) collective-permute-start(f32[128,128]{1,0:T(8,128)S(1)} %core_backward.1.refs_0_), channel_id=1, source_target_pairs={{0,8},{8,0},{16,24},{24,16},{1,9},{9,1},{17,25},{25,17},{2,10},{10... | collective-permute-start | bytes 196616 | tf_op jit(solution)/shard_map/ppermute | solution.py:615
  44.1 4.3 %collective-permute-start.4 = (f32[128,128]{1,0:T(8,128)S(1)}, f32[128,128]{1,0:T(8,128)S(1)}, u32[]{:S(2)}, u32[]{:S(2)}) collective-permute-start(f32[128,128]{1,0:T(8,128)S(1)} %add.2.refs_0_), channel_id=1, source_target_pairs={{0,1},{1,0},{2,3},{3,2},{4,5},{5,4},{6,7},{7,6},{8,9},{9,8},{10,11... | collective-permute-start | bytes 196616 | tf_op jit(solution)/shard_map/ppermute | solution.py:615
  48.5 8.2 %collective-permute-start.8 = (f32[128,128]{1,0:T(8,128)S(1)}, f32[128,128]{1,0:T(8,128)S(1)}, u32[]{:S(2)}, u32[]{:S(2)}) collective-permute-start(f32[128,128]{1,0:T(8,128)S(1)} %add.3.refs_0_), channel_id=1, source_target_pairs={{0,6},{1,7},{2,4},{3,5},{4,2},{5,3},{6,0},{7,1},{8,14},{9,15},{10,... | collective-permute-start | bytes 196616 | tf_op jit(solution)/shard_map/ppermute | solution.py:615
  49.4 7.2 %collective-permute-start.7 = (f32[128,128]{1,0:T(8,128)S(1)}, f32[128,128]{1,0:T(8,128)S(1)}, u32[]{:S(2)}, u32[]{:S(2)}) collective-permute-start(f32[128,128]{1,0:T(8,128)S(1)} %add.3.refs_0_), channel_id=1, source_target_pairs={{0,4},{1,5},{2,6},{3,7},{4,0},{5,1},{6,2},{7,3},{8,12},{9,13},{10,... | collective-permute-start | bytes 196616 | tf_op jit(solution)/shard_map/ppermute | solution.py:615
  49.9 6.7 %collective-permute-start.6 = (f32[128,128]{1,0:T(8,128)S(1)}, f32[128,128]{1,0:T(8,128)S(1)}, u32[]{:S(2)}, u32[]{:S(2)}) collective-permute-start(f32[128,128]{1,0:T(8,128)S(1)} %add.3.refs_0_), channel_id=1, source_target_pairs={{0,2},{1,3},{2,0},{3,1},{4,6},{5,7},{6,4},{7,5},{8,10},{9,11},{10,... | collective-permute-start | bytes 196616 | tf_op jit(solution)/shard_map/ppermute | solution.py:615

commit v7 on v6

--- a/solution.py
+++ b/solution.py
@@ -68,7 +68,17 @@
     return jnp.where(target == iota(shape, 1 - pixel_axis), 0.25, 0.0).astype(BF)
 
 
-def prep_kernel(frames, weight, cbias, mix, mbias, wbig, blocks, blocks_t, bias, pool, table):
+def fetch_rows(source, first, target, sems):
+    copies = []
+    for k, r in enumerate(range(0, target.shape[0], SEG)):
+        part = source.at[r : r + SEG, first : first + target.shape[1]]
+        copies.append(pltpu.make_async_copy(part, target.at[r : r + SEG, :], sems.at[k]))
+        copies[k].start()
+    return copies
+
+
+def prep_kernel(frames, weight, cbias, mix, mbias, mask_in, wbig, blocks, blocks_t, bias, pool, mask, table, sems):
+    copies = fetch_rows(mask_in, 0, mask, sems)
     channels, taps = weight.shape
     patch_cols = wbig.shape[1]
     group = blocks.shape[0] // channels
@@ -95,6 +105,8 @@
         for dt in range(KT):
             total = total + jnp.where(source == f + dt - 1, spread[dt * channels : (dt + 1) * channels], 0.0)
         wbig[f * channels : (f + 1) * channels, :] = total.astype(BF)
+    for copy in copies:
+        copy.wait()
 
 
 def core_forward_kernel(
@@ -118,9 +130,7 @@
     feats,
     sems,
 ):
-    copies = []
-    for k, r in enumerate(range(0, mask.shape[0], SEG)):
-        copies.append(pltpu.make_async_copy(mask_in.at[r : r + SEG, :], mask.at[r : r + SEG, :], sems.at[k]))
+    copies = fetch_rows(mask_in, mask_in.shape[1] - mask.shape[1], mask, sems)
     frames, _, width = recv.shape
     rows, pix = act1.shape
     channels = bias.shape[1]
@@ -176,8 +186,6 @@
             slope[r : r + channels, at] = e.astype(BF)
 
     for t in range(count + 2):
-        if t < len(copies):
-            copies[t].start()
         if t < count:
             pre[t % 2][...] = dot(wide, xcol[:, t * CHUNK : (t + 1) * CHUNK])
         if 1 <= t <= count:
@@ -225,7 +233,8 @@
     count,
     target,
     pay,
-    mask,
+    mask_near,
+    mask_late,
     wt,
     rbias,
     pooled_grad,
@@ -237,7 +246,8 @@
     mixed,
     acc,
 ):
-    pooled_n, neurons = mask.shape
+    pooled_n, early = mask_near.shape
+    neurons = target.shape[1]
     own = mask_own.shape[1]
     channels = wt.shape[0]
     frames = target.shape[0]
@@ -245,14 +255,25 @@
     block = proj0.shape[1]
     steps = neurons // block
     first = pl.multiple_of(where[0] * own, own)
-    mask_own[...] = mask[:, pl.ds(first, own)]
+
+    @pl.when(first < early)
+    def _():
+        mask_own[...] = mask_near[:, pl.ds(pl.multiple_of(jnp.minimum(first, early - own), own), own)]
+
+    @pl.when(first >= early)
+    def _():
+        mask_own[...] = mask_late[:, pl.ds(pl.multiple_of(jnp.maximum(first - early, 0), own), own)]
+
+    def mask_part(low, high):
+        return mask_near[:, low:high] if high <= early else mask_late[:, low - early : high - early]
+
     wt_own[...] = wt[:, pl.ds(first, own)]
     pooled = pay[:, 0:pooled_n]
     loss_sum = jnp.zeros((frames, block), F32)
     begun = False
     for t in range(steps + 2):
         if t < steps:
-            proj[t % 2][...] = dot(pooled, mask[:, t * block : (t + 1) * block])
+            proj[t % 2][...] = dot(pooled, mask_part(t * block, (t + 1) * block))
         if 1 <= t <= steps:
             at = slice((t - 1) * block, t * block)
             w = wt[:, at].astype(F32)
@@ -263,10 +284,10 @@
             for f in range(frames):
                 mixed[f * channels : (f + 1) * channels, at] = (grad[f : f + 1] * w).astype(BF)
         last = t - 2
-        if last >= 0 and (last % 2 == 0 or last == steps - 1):
-            low = (last - 1 if last > 0 and last % 2 == 0 else last) * block
+        if last >= 0 and last % 2 == 1:
+            low = (last - 1) * block
             at = slice(low, (last + 1) * block)
-            part = dot(mask[:, at], mixed[:, at], NT)
+            part = dot(mask_part(low, at.stop), mixed[:, at], NT)
             acc[...] = acc[...] + part if begun else part
             begun = True
     pooled_grad[...] = acc[...].T.astype(BF)
@@ -502,24 +523,6 @@
     send, where = lax.optimization_barrier((send, where))
     recv = lax.all_to_all(send, "sess", split_axis=0, concat_axis=0, tiled=True)
 
-    patch_cols = KS * DX * frames
-    span = channels * group
-    half = 2 * WW
-    wbig, blocks, blocks_t, bias, pool = pl.pallas_call(
-        functools.partial(prep_kernel, frames),
-        out_shape=(
-            jax.ShapeDtypeStruct((rows, patch_cols), BF),
-            jax.ShapeDtypeStruct((span, span), BF),
-            jax.ShapeDtypeStruct((span, span), BF),
-            jax.ShapeDtypeStruct((2, channels, 128), F32),
-            jax.ShapeDtypeStruct((4 * half, half), BF),
-        ),
-        scratch_shapes=[pltpu.VMEM((PACK, patch_cols), BF)],
-        compiler_params=params(),
-        cost_estimate=cost(1 << 27),
-        name="prep",
-    )(*in_hbm(conv_weight, conv_bias[None, :], mix_weight, mix_bias[None, :]))
-
     wt = jnp.swapaxes(feat_w, 1, 2).reshape(channels, neurons)
     mask_t = jnp.swapaxes(masks, 1, 2).reshape(pooled_n, neurons)
     rbias = readout_bias
@@ -528,7 +531,28 @@
     vmem = pl.BlockSpec(memory_space=pltpu.VMEM)
     anywhere = pl.BlockSpec(memory_space=pl.ANY)
     smem = pl.BlockSpec(memory_space=pltpu.SMEM)
-    pay, target, act1, slope1, slope2, xcol, mask_near = pl.pallas_call(
+    early = neurons // 2
+    patch_cols = KS * DX * frames
+    span = channels * group
+    half = 2 * WW
+    wbig, blocks, blocks_t, bias, pool, mask_near = pl.pallas_call(
+        functools.partial(prep_kernel, frames),
+        out_shape=(
+            jax.ShapeDtypeStruct((rows, patch_cols), BF),
+            jax.ShapeDtypeStruct((span, span), BF),
+            jax.ShapeDtypeStruct((span, span), BF),
+            jax.ShapeDtypeStruct((2, channels, 128), F32),
+            jax.ShapeDtypeStruct((4 * half, half), BF),
+            jax.ShapeDtypeStruct((pooled_n, early), BF),
+        ),
+        in_specs=[vmem] * 4 + [anywhere],
+        scratch_shapes=[pltpu.VMEM((PACK, patch_cols), BF), pltpu.SemaphoreType.DMA((pooled_n // SEG,))],
+        compiler_params=params(),
+        cost_estimate=cost(1 << 27),
+        name="prep",
+    )(*in_hbm(conv_weight, conv_bias[None, :], mix_weight, mix_bias[None, :]), mask_far)
+
+    pay, target, act1, slope1, slope2, xcol, mask_late = pl.pallas_call(
         core_forward_kernel,
         out_shape=(
             jax.ShapeDtypeStruct((rows, width), BF),
@@ -537,7 +561,7 @@
             jax.ShapeDtypeStruct((rows, pix), BF),
             jax.ShapeDtypeStruct((rows, pix), BF),
             jax.ShapeDtypeStruct((patch_cols, pix), BF),
-            jax.ShapeDtypeStruct((pooled_n, neurons), BF),
+            jax.ShapeDtypeStruct((pooled_n, neurons - early), BF),
         ),
         in_specs=[vmem] * 5 + [anywhere],
         scratch_shapes=[pltpu.VMEM((rows, CHUNK), F32)] * 4
@@ -556,7 +580,7 @@
     work = 2 * rows * neurons * pooled_n
     pooled_grad, loss, mask_own, wt_own = pl.pallas_call(
         functools.partial(readout_kernel, scale),
-        in_specs=[smem, smem] + [vmem] * 5,
+        in_specs=[smem, smem] + [vmem] * 6,
         out_shape=(
             jax.ShapeDtypeStruct((rows, pooled_n), BF),
             jax.ShapeDtypeStruct((8, 128), F32),
@@ -568,7 +592,7 @@
         compiler_params=params(),
         cost_estimate=cost(2 * work, 2 * neurons * pooled_n),
         name="readout",
-    )(where, counts, target, pay, mask_near, wt, rbias)
+    )(where, counts, target, pay, mask_near, mask_late, wt, rbias)
 
     core = pl.pallas_call(
         functools.partial(core_backward_kernel, channels),

time: 57.7 us -> 57 us (0.988)
  waiting for transfers between devices: 11 us -> 9.63 us
  Pallas kernels: 29.2 us -> 29.8 us
    all_to_all x1, waiting for transfers between devices: 5.37 us -> 3.92 us  [per_device(): recv = lax.all_to_all(send, 'sess', split_axis=0, concat_axis=0, tiled=True)]
    pallas_call x1, Pallas kernels: 1.31 us -> 2.77 us  [per_device(): pl.pallas_call(functools.partial(prep_kernel, frames), out_shape=(jax.Sha...]
    pallas_call x1, Pallas kernels: 5.97 us -> 5.15 us  [per_device(): pl.pallas_call(core_forward_kernel, out_shape=(jax.ShapeDtypeStruct((rows...]
  transfers between devices with their start and end apart: 11 -> 11, of which waited for: 4 -> 4; matrix products, arithmetic and copies ran while one was open for 0% -> 0% of each run, Pallas kernels for 36% -> 39%
where the time goes in v7:
time: 57 us; the launch traced here: 56.6 us
  Pallas kernels  29.8 us (52%)
  starting transfers between devices  15.7 us (28%)
  waiting for transfers between devices  9.63 us (17%)
  between operations  1.4 us (2%)
    pallas_call x3, Pallas kernels, owned_rows(): pl.pallas_call(functools.partial(owned_rows_kernel, scale, len(clips), ow...  8.83 us
    all_to_all x1, starting transfers between devices, per_device(): recv = lax.all_to_all(send, 'sess', split_axis=0, concat_axis=0, tiled=True)  7.28 us
    ppermute x7, starting transfers between devices, per_device(): lax.ppermute(core, axis, xor_pairs(lax.axis_size(axis), mask))  6.88 us
    pallas_call x1, Pallas kernels, per_device(): pl.pallas_call(functools.partial(readout_kernel, scale), in_specs=[smem,...  6.35 us
    pallas_call x1, Pallas kernels, per_device(): pl.pallas_call(core_forward_kernel, out_shape=(jax.ShapeDtypeStruct((rows...  5.15 us
    pallas_call x1, Pallas kernels, per_device(): pl.pallas_call(functools.partial(core_backward_kernel, channels), out_sha...  4.1 us
    all_to_all x1, waiting for transfers between devices, per_device(): recv = lax.all_to_all(send, 'sess', split_axis=0, concat_axis=0, tiled=True)  3.92 us
    ppermute x2, waiting for transfers between devices, per_device(): near[mask] = lax.ppermute(pay, 'clip', xor_pairs(clip_total, mask))  3.05 us
  transfers between devices with their start and end apart: 11, of which 4 were waited for; matrix products, arithmetic and copies ran while one was open for 0% of the time, Pallas kernels for 39%

profile of v7, /device:TPU:0, one launch (start us, length us, event | category | flops | bytes accessed | tf_op | source)
XLA Modules:
  0.0 56.6 jit_solution(8336689352502338418)
XLA Ops:
  0.6 1.8 %select.1 = bf16[8,16,512]{2,1,0:T(8,128)(2,1)} custom-call(s32[1,8]{1,0:T(1,128)} %bitcast.26, bf16[8,2304]{1,0:T(8,128)(2,1)} %bitcast.25, bf16[8,4096]{1,0:T(8,128)(2,1)} %bitcast.24), custom_call_target="tpu_custom_call" | custom-call | tf_op jit(solution)/shard_map/select/pallas_call | solution.py:516
  2.5 7.3 %all-to-all-start = ((bf16[8,16,512]{2,1,0:T(8,128)(2,1)}), bf16[8,16,512]{2,1,0:T(8,128)(2,1)S(1)}, u32[]{:S(2)}, u32[]{:S(2)}) async-start(bf16[8,16,512]{2,1,0:T(8,128)(2,1)} %select.1), calls=%async_computation | async-start | bytes 262144 | tf_op jit(solution)/shard_map/all_to_all | solution.py:524
  10.4 2.8 %prep.1 = (bf16[512,448]{1,0:T(8,128)(2,1)S(1)}, bf16[256,256]{1,0:T(8,128)(2,1)S(1)}, bf16[256,256]{1,0:T(8,128)(2,1)S(1)}, f32[2,64,128]{2,1,0:T(8,128)S(1)}, ...) custom-call(bf16[64,147]{1,0:T(8,128)(2,1)} %weight.1, f32[1,64]{1,0:T(1,128)} %bitcast.27, ...), custom_call_target="tpu_custom_call" | custom-call | flops 134217728 | bytes 1048576 | tf_op jit(solution)/shard_map/prep/pallas_call | solution.py:538
  13.2 3.9 %all-to-all-done.recv = bf16[8,16,512]{2,1,0:T(8,128)(2,1)S(1)} async-done(((bf16[8,16,512]{2,1,0:T(8,128)(2,1)}), bf16[8,16,512]{2,1,0:T(8,128)(2,1)S(1)}, u32[]{:S(2)}, u32[]{:S(2)}) %all-to-all-start) | async-done | bytes 131104 | tf_op jit(solution)/shard_map/all_to_all | solution.py:524
  17.1 0.0 copy-start
  17.1 0.0 copy-start.1
  17.1 5.2 %core_forward.1 = (bf16[512,640]{1,0:T(8,128)(2,1)S(1)}, f32[8,4096]{1,0:T(8,128)S(1)}, bf16[512,2304]{1,0:T(8,128)(2,1)S(1)}, bf16[512,2304]{1,0:T(8,128)(2,1)S...) custom-call(bf16[8,16,512]{2,1,0:T(8,128)(2,1)S(1)} %all-to-all-done.recv, ...), custom_call_target="tpu_custom_call" | custom-call | flops 1056964608 | bytes 9437184 | tf_op jit(solution)/shard_map/core_forward/pallas_call | solution.py:555
  22.3 1.6 %collective-permute-start.5 = (bf16[512,640]{1,0:T(8,128)(2,1)S(1)}, bf16[512,640]{1,0:T(8,128)(2,1)S(1)}, u32[]{:S(2)}, u32[]{:S(2)}) collective-permute-start(bf16[512,640]{1,0:T(8,128)(2,1)S(1)} %get-tuple-element.62.pay.refs_0_), channel_id=1, source_target_pairs={{0,16},{8,24},{16,0},{24,8},{1,17},{9,25},{17,1},{25,9},{2,18},{10... | collective-permute-start | bytes 1966088 | tf_op jit(solution)/shard_map/ppermute | solution.py:577
  23.8 0.0 collective-permute-start.3
  23.9 0.0 copy-done
  23.9 0.0 copy-done.1
  23.9 6.3 %readout.1 = (bf16[512,576]{1,0:T(8,128)(2,1)S(1)}, f32[8,128]{1,0:T(8,128)S(1)}, bf16[576,1024]{1,0:T(8,128)(2,1)S(1)}, bf16[64,1024]{1,0:T(8,128)(2,1)S(1)}) custom-call(s32[1]{0:T(128)} %bitcast.3.where, s32[1]{0:T(128)S(6)} %copy.19.count, f32[8,4096]{1,0:T(8,128)S(1)} %get-tuple-element.61.target, bf16[512,640]{1,0:T(8,128)(2,1)S(1)} %get-tuple-element.62.pay.refs_0_, ...), custom_call_target="tpu_custom_call" | custom-call | flops 4831838208 | bytes 4718592 | tf_op jit(solution)/shard_map/readout/pallas_call | solution.py:581
  30.2 4.1 %core_backward.1.refs_0_ = f32[128,128]{1,0:T(8,128)S(1)} custom-call(bf16[512,576]{1,0:T(8,128)(2,1)S(1)} %get-tuple-element.65.pooled_grad, f32[8,128]{1,0:T(8,128)S(1)} %get-tuple-element.66.loss, bf16[512,2304]{1,0:T(8,128)(2,1)S(1)} %get-tuple-element.67.act1, bf16[512,2304]{1,0:T(8,128)(2,1)S(1)} %get-tuple-element.68.slope1, ...), custom_call_target="tpu_custom_call" | custom-call | flops 4831838208 | bytes 9437184 | tf_op jit(solution)/shard_map/core_backward/pallas_call | solution.py:597
  34.3 3.1 %collective-permute-done.5.refs_0_ = bf16[512,640]{1,0:T(8,128)(2,1)S(1)} collective-permute-done((bf16[512,640]{1,0:T(8,128)(2,1)S(1)}, bf16[512,640]{1,0:T(8,128)(2,1)S(1)}, u32[]{:S(2)}, u32[]{:S(2)}) %collective-permute-start.5) | collective-permute-done | bytes 655392 | tf_op jit(solution)/shard_map/ppermute | solution.py:577
  37.4 0.0 collective-permute-start.9
  37.4 1.6 %collective-permute-start.2 = (f32[128,128]{1,0:T(8,128)S(1)}, f32[128,128]{1,0:T(8,128)S(1)}, u32[]{:S(2)}, u32[]{:S(2)}) collective-permute-start(f32[128,128]{1,0:T(8,128)S(1)} %core_backward.1.refs_0_), channel_id=1, source_target_pairs={{0,24},{8,16},{16,8},{24,0},{1,25},{9,17},{17,9},{25,1},{2,26},{10... | collective-permute-start | bytes 196616 | tf_op jit(solution)/shard_map/ppermute | solution.py:639
  39.0 0.5 collective-permute-start.1
  39.5 0.0 collective-permute-start
  39.5 0.0 collective-permute-done.3.refs_1_
  39.5 3.3 %owned_rows.3.refs_4_ = f32[648,1024]{1,0:T(8,128)S(1)} custom-call(s32[1]{0:T(128)} %bitcast.3.where, s32[1]{0:T(128)S(6)} %copy.19.count, bf16[512,640]{1,0:T(8,128)(2,1)S(1)} %get-tuple-element.62.pay.refs_0_, bf16[512,640]{1,0:T(8,128)(2,1)S(1)} %collective-permute-done.3.refs_1_, bf16[64,1024]{1,0:T(8,128)(2,1)S(1)} %get-tuple-element.72.refs_2_.refs_1_, ...), custom_call_target="tpu_custom_call" | custom-call | flops 2415919104 | bytes 2359296 | tf_op jit(solution)/shard_map/owned_rows/pallas_call | solution.py:609
  42.8 0.0 collective-permute-done.2.refs_3_
  42.8 0.5 collective-permute-done.1.refs_2_
  43.3 0.0 collective-permute-done.refs_1_
  43.3 0.3 collective-permute-start.4
  43.6 1.9 %owned_rows.4.refs_4_ = f32[648,1024]{1,0:T(8,128)S(1)} custom-call(s32[1]{0:T(128)} %bitcast.3.where, s32[1]{0:T(128)S(6)} %copy.19.count, bf16[512,640]{1,0:T(8,128)(2,1)S(1)} %collective-permute-done.5.refs_0_, bf16[64,1024]{1,0:T(8,128)(2,1)S(1)} %get-tuple-element.72.refs_2_.refs_1_, f32[1,4096]{1,0:T(1,128)S(1)} %copy-done, ...), custom_call_target="tpu_custom_call" | custom-call | flops 1207959552 | bytes 2359296 | tf_op jit(solution)/shard_map/owned_rows/pallas_call | solution.py:609
  45.4 2.2 %collective-permute-done.4.refs_1_ = f32[128,128]{1,0:T(8,128)S(1)} collective-permute-done((f32[128,128]{1,0:T(8,128)S(1)}, f32[128,128]{1,0:T(8,128)S(1)}, u32[]{:S(2)}, u32[]{:S(2)}) %collective-permute-start.4) | collective-permute-done | bytes 65568 | tf_op jit(solution)/shard_map/ppermute | solution.py:639
  47.6 0.9 %collective-permute-start.8 = (f32[128,128]{1,0:T(8,128)S(1)}, f32[128,128]{1,0:T(8,128)S(1)}, u32[]{:S(2)}, u32[]{:S(2)}) collective-permute-start(f32[128,128]{1,0:T(8,128)S(1)} %add.3.refs_0_), channel_id=1, source_target_pairs={{0,6},{1,7},{2,4},{3,5},{4,2},{5,3},{6,0},{7,1},{8,14},{9,15},{10,... | collective-permute-start | bytes 196616 | tf_op jit(solution)/shard_map/ppermute | solution.py:639
  48.6 0.5 collective-permute-start.7
  49.1 3.0 %collective-permute-start.6 = (f32[128,128]{1,0:T(8,128)S(1)}, f32[128,128]{1,0:T(8,128)S(1)}, u32[]{:S(2)}, u32[]{:S(2)}) collective-permute-start(f32[128,128]{1,0:T(8,128)S(1)} %add.3.refs_0_), channel_id=1, source_target_pairs={{0,2},{1,3},{2,0},{3,1},{4,6},{5,7},{6,4},{7,5},{8,10},{9,11},{10,... | collective-permute-start | bytes 196616 | tf_op jit(solution)/shard_map/ppermute | solution.py:639
  52.1 0.0 collective-permute-done.9.refs_0_
  52.1 3.7 %owned_rows.5 = (f32[576,1024]{1,0:T(8,128)}, f32[64,1024]{1,0:T(8,128)}, f32[1,1024]{1,0:T(1,128)}) custom-call(s32[1]{0:T(128)} %bitcast.3.where, s32[1]{0:T(128)S(6)} %copy.19.count, bf16[512,640]{1,0:T(8,128)(2,1)S(1)} %collective-permute-done.9.refs_0_, bf16[64,1024]{1,0:T(8,128)(2,1)S(1)} %get-tuple-element.72.refs_2_.refs_1_, f32[1,4096]{1,0:T(1,128)S(1)} %copy-done, ...), custom_call_target="tpu_custom_call" | custom-call | flops 1207959552 | bytes 2359296 | tf_op jit(solution)/shard_map/owned_rows/pallas_call | solution.py:609
  55.8 0.0 collective-permute-done.8.refs_3_
  55.8 0.0 collective-permute-done.7.refs_2_
  55.8 0.0 collective-permute-done.6.refs_1_
  55.8 0.7 %unpack.1 = (f32[64,147]{1,0:T(8,128)}, f32[1,64]{1,0:T(1,128)}, f32[64,64]{1,0:T(8,128)}, f32[1,64]{1,0:T(1,128)}, f32[1,1]{1,0:T(1,128)}) custom-call(f32[128,128]{1,0:T(8,128)S(1)} %add.3.refs_0_, f32[128,128]{1,0:T(8,128)S(1)} %collective-permute-done.6.refs_1_, f32[128,128]{1,0:T(8,128)S(1)} %collective-permute-done.7.refs_2_, ...), custom_call_target="tpu_custom_call" | custom-call | tf_op jit(solution)/shard_map/unpack/pallas_call | solution.py:652
  (2 shorter events, 0.0 us)
Async XLA Ops:
  2.5 14.6 %all-to-all-start = ((bf16[8,16,512]{2,1,0:T(8,128)(2,1)}), bf16[8,16,512]{2,1,0:T(8,128)(2,1)S(1)}, u32[]{:S(2)}, u32[]{:S(2)}) async-start(bf16[8,16,512]{2,1,0:T(8,128)(2,1)} %select.1), calls=%async_computation | async-start | bytes 262144 | tf_op jit(solution)/shard_map/all_to_all | solution.py:524
  17.1 6.8 %copy-start = (f32[1,4096]{1,0:T(1,128)S(1)}, f32[1,4096]{1,0:T(1,128)}, u32[]{:S(2)}) copy-start(f32[1,4096]{1,0:T(1,128)} %refs_2_.3) | copy-start | bytes 49156
  17.1 6.8 %copy-start.1 = (bf16[1,4096,64]{1,2,0:T(8,128)(2,1)S(1)}, bf16[1,4096,64]{1,2,0:T(8,128)(2,1)}, u32[]{:S(2)}) copy-start(bf16[1,4096,64]{1,2,0:T(8,128)(2,1)} %param.20) | copy-start | bytes 1572868
  22.3 15.1 %collective-permute-start.5 = (bf16[512,640]{1,0:T(8,128)(2,1)S(1)}, bf16[512,640]{1,0:T(8,128)(2,1)S(1)}, u32[]{:S(2)}, u32[]{:S(2)}) collective-permute-start(bf16[512,640]{1,0:T(8,128)(2,1)S(1)} %get-tuple-element.62.pay.refs_0_), channel_id=1, source_target_pairs={{0,16},{8,24},{16,0},{24,8},{1,17},{9,25},{17,1},{25,9},{2,18},{10... | collective-permute-start | bytes 1966088 | tf_op jit(solution)/shard_map/ppermute | solution.py:577
  23.8 15.7 %collective-permute-start.3 = (bf16[512,640]{1,0:T(8,128)(2,1)S(1)}, bf16[512,640]{1,0:T(8,128)(2,1)S(1)}, u32[]{:S(2)}, u32[]{:S(2)}) collective-permute-start(bf16[512,640]{1,0:T(8,128)(2,1)S(1)} %get-tuple-element.62.pay.refs_0_), channel_id=1, source_target_pairs={{0,8},{8,0},{16,24},{24,16},{1,9},{9,1},{17,25},{25,17},{2,10},{10... | collective-permute-start | bytes 1966088 | tf_op jit(solution)/shard_map/ppermute | solution.py:577
  37.4 14.7 %collective-permute-start.9 = (bf16[512,640]{1,0:T(8,128)(2,1)S(1)}, bf16[512,640]{1,0:T(8,128)(2,1)S(1)}, u32[]{:S(2)}, u32[]{:S(2)}) collective-permute-start(bf16[512,640]{1,0:T(8,128)(2,1)S(1)} %collective-permute-done.5.refs_0_), channel_id=1, source_target_pairs={{0,8},{8,0},{16,24},{24,16},{1,9},{9,1},{17,25},{25,17},{2,10},{10... | collective-permute-start | bytes 1966088 | tf_op jit(solution)/shard_map/ppermute | solution.py:634
  37.4 5.4 %collective-permute-start.2 = (f32[128,128]{1,0:T(8,128)S(1)}, f32[128,128]{1,0:T(8,128)S(1)}, u32[]{:S(2)}, u32[]{:S(2)}) collective-permute-start(f32[128,128]{1,0:T(8,128)S(1)} %core_backward.1.refs_0_), channel_id=1, source_target_pairs={{0,24},{8,16},{16,8},{24,0},{1,25},{9,17},{17,9},{25,1},{2,26},{10... | collective-permute-start | bytes 196616 | tf_op jit(solution)/shard_map/ppermute | solution.py:639
  39.0 4.3 %collective-permute-start.1 = (f32[128,128]{1,0:T(8,128)S(1)}, f32[128,128]{1,0:T(8,128)S(1)}, u32[]{:S(2)}, u32[]{:S(2)}) collective-permute-start(f32[128,128]{1,0:T(8,128)S(1)} %core_backward.1.refs_0_), channel_id=1, source_target_pairs={{0,16},{8,24},{16,0},{24,8},{1,17},{9,25},{17,1},{25,9},{2,18},{10... | collective-permute-start | bytes 196616 | tf_op jit(solution)/shard_map/ppermute | solution.py:639
  39.5 3.8 %collective-permute-start = (f32[128,128]{1,0:T(8,128)S(1)}, f32[128,128]{1,0:T(8,128)S(1)}, u32[]{:S(2)}, u32[]{:S(2)}) collective-permute-start(f32[128,128]{1,0:T(8,128)S(1)} %core_backward.1.refs_0_), channel_id=1, source_target_pairs={{0,8},{8,0},{16,24},{24,16},{1,9},{9,1},{17,25},{25,17},{2,10},{10... | collective-permute-start | bytes 196616 | tf_op jit(solution)/shard_map/ppermute | solution.py:639
  43.3 4.3 %collective-permute-start.4 = (f32[128,128]{1,0:T(8,128)S(1)}, f32[128,128]{1,0:T(8,128)S(1)}, u32[]{:S(2)}, u32[]{:S(2)}) collective-permute-start(f32[128,128]{1,0:T(8,128)S(1)} %add.2.refs_0_), channel_id=1, source_target_pairs={{0,1},{1,0},{2,3},{3,2},{4,5},{5,4},{6,7},{7,6},{8,9},{9,8},{10,11... | collective-permute-start | bytes 196616 | tf_op jit(solution)/shard_map/ppermute | solution.py:639
  47.6 8.2 %collective-permute-start.8 = (f32[128,128]{1,0:T(8,128)S(1)}, f32[128,128]{1,0:T(8,128)S(1)}, u32[]{:S(2)}, u32[]{:S(2)}) collective-permute-start(f32[128,128]{1,0:T(8,128)S(1)} %add.3.refs_0_), channel_id=1, source_target_pairs={{0,6},{1,7},{2,4},{3,5},{4,2},{5,3},{6,0},{7,1},{8,14},{9,15},{10,... | collective-permute-start | bytes 196616 | tf_op jit(solution)/shard_map/ppermute | solution.py:639
  48.6 7.2 %collective-permute-start.7 = (f32[128,128]{1,0:T(8,128)S(1)}, f32[128,128]{1,0:T(8,128)S(1)}, u32[]{:S(2)}, u32[]{:S(2)}) collective-permute-start(f32[128,128]{1,0:T(8,128)S(1)} %add.3.refs_0_), channel_id=1, source_target_pairs={{0,4},{1,5},{2,6},{3,7},{4,0},{5,1},{6,2},{7,3},{8,12},{9,13},{10,... | collective-permute-start | bytes 196616 | tf_op jit(solution)/shard_map/ppermute | solution.py:639
  49.1 6.7 %collective-permute-start.6 = (f32[128,128]{1,0:T(8,128)S(1)}, f32[128,128]{1,0:T(8,128)S(1)}, u32[]{:S(2)}, u32[]{:S(2)}) collective-permute-start(f32[128,128]{1,0:T(8,128)S(1)} %add.3.refs_0_), channel_id=1, source_target_pairs={{0,2},{1,3},{2,0},{3,1},{4,6},{5,7},{6,4},{7,5},{8,10},{9,11},{10,... | collective-permute-start | bytes 196616 | tf_op jit(solution)/shard_map/ppermute | solution.py:639

commit v8 on v6

--- a/solution.py
+++ b/solution.py
@@ -118,9 +118,16 @@
     feats,
     sems,
 ):
-    copies = []
-    for k, r in enumerate(range(0, mask.shape[0], SEG)):
-        copies.append(pltpu.make_async_copy(mask_in.at[r : r + SEG, :], mask.at[r : r + SEG, :], sems.at[k]))
+    copy_count = mask.shape[0] // SEG
+
+    def mask_copy(k):
+        rows_at = pl.ds(pl.multiple_of(k * SEG, SEG), SEG)
+        return pltpu.make_async_copy(mask_in.at[rows_at, :], mask.at[rows_at, :], sems.at[k])
+
+    @pl.loop(0, copy_count)
+    def _(k):
+        mask_copy(k).start()
+
     frames, _, width = recv.shape
     rows, pix = act1.shape
     channels = bias.shape[1]
@@ -176,8 +183,6 @@
             slope[r : r + channels, at] = e.astype(BF)
 
     for t in range(count + 2):
-        if t < len(copies):
-            copies[t].start()
         if t < count:
             pre[t % 2][...] = dot(wide, xcol[:, t * CHUNK : (t + 1) * CHUNK])
         if 1 <= t <= count:
@@ -201,8 +206,10 @@
         pieces += [pltpu.roll(tile, SEG, 1), tile]
     packed = jnp.concatenate(pieces, axis=0)
     pay[:, p // 4 : p // 4 + half] = jnp.where(iota((rows, half), 1) < SEG, tail, packed).astype(BF)
-    for copy in copies:
-        copy.wait()
+
+    @pl.loop(0, copy_count)
+    def _(k):
+        mask_copy(k).wait()
 
 
 def drive_terms(projected, target, w, rbias, alive, scale, channels):
@@ -375,7 +382,7 @@
     loss[...] = high[0:1, rest + 2 : rest + 3]
 
 
-def owned_rows_kernel(scale, clips, own, block, held, last, where, count, *refs):
+def owned_rows_kernel(scale, clips, each, own, block, held, last, where, count, *refs):
     pays = refs[:clips]
     wt, rbias, mask = refs[clips : clips + 3]
     before = refs[clips + 3 : clips + 3 + held]
@@ -392,14 +399,32 @@
     first = pl.multiple_of(where[0] * own, own)
     segs = block // SEG
     low = iota((frames, 128), 1) < SEG
-    items = [(k, c) for k in range(steps) for c in range(clips)]
+    items = [(k, c) for k in range(steps) for c in range(each[k])]
+    opening = items[0][0]
+    passed = [k for k in range(steps) if each[k] == 0]
+    span = pooled_n // 2
+
+    def finished(k, part):
+        at = slice(k * block, (k + 1) * block)
+        rows_at = pl.ds(pl.multiple_of(part * span, 8), span)
+        return pltpu.make_async_copy(before[0].at[rows_at, at], outs[0].at[rows_at, at], sems.at[steps + 2 * k + part])
+
+    for k in passed:
+        at = slice(k * block, (k + 1) * block)
+        outs[1][:, at] = before[0][pooled_n:low_rows, at]
+        outs[2][:, at] = before[0][low_rows : low_rows + 1, at]
+
+        @pl.loop(0, 2)
+        def _(part, k=k):
+            finished(k, part).start()
+
     feats = [jnp.zeros((channels, block), F32) for _ in range(steps)]
     biases = [jnp.zeros((frames, block), F32) for _ in range(steps)]
     stores = []
     for t in range(len(items) + 2):
         if t < len(items):
             k, c = items[t]
-            if k == 0:
+            if k == opening:
                 turned[:, c * rows : (c + 1) * rows] = pays[c][:, 0:pooled_n].T
             proj[t % 2][...] = dot(pays[c][:, 0:pooled_n], mask[:, k * block : (k + 1) * block])
         if 1 <= t <= len(items):
@@ -422,10 +447,11 @@
                 at = c * rows + f * channels
                 mixed[k % 2][at : at + channels, :] = (grad[f : f + 1] * w).astype(BF)
             biases[k] = biases[k] + grad
-        if t >= 2 and items[t - 2][1] == clips - 1:
+        if t >= 2 and items[t - 2][1] == each[items[t - 2][0]] - 1:
             k = items[t - 2][0]
             at = slice(k * block, (k + 1) * block)
-            total = dot(turned[...], mixed[k % 2][...])
+            used = each[k] * rows
+            total = dot(turned[:, 0:used], mixed[k % 2][0:used, :])
             feat = feats[k]
             bias = jnp.sum(biases[k], axis=0, keepdims=True)
             if held:
@@ -444,6 +470,11 @@
                 outs[0][low_rows:, at] = jnp.broadcast_to(bias, (8, block))
     for store in stores:
         store.wait()
+    for k in passed:
+
+        @pl.loop(0, 2)
+        def _(part, k=k):
+            finished(k, part).wait()
 
 
 def params(rows=512):
@@ -581,9 +612,9 @@
         name="core_backward",
     )(pooled_grad, loss, act1, slope1, slope2, xcol, blocks_t)
 
-    def owned_rows(clips, held, last):
+    def owned_rows(clips, each, held, last):
         return pl.pallas_call(
-            functools.partial(owned_rows_kernel, scale, len(clips), own, block, len(held), last),
+            functools.partial(owned_rows_kernel, scale, len(clips), each, own, block, len(held), last),
             in_specs=[smem, smem] + [vmem] * (len(clips) + 3 + len(held)),
             out_specs=[anywhere, vmem, vmem] if last else [vmem],
             out_shape=[
@@ -598,7 +629,7 @@
             + [
                 pltpu.VMEM((pooled_n, len(clips) * rows), BF),
                 pltpu.VMEM((pooled_n, own) if last else (8, 128), F32),
-                pltpu.SemaphoreType.DMA((own // block,)),
+                pltpu.SemaphoreType.DMA((3 * (own // block),)),
             ],
             compiler_params=params(rows),
             cost_estimate=cost(2 * work * len(clips) // clip_total, 4 * own * pooled_n),
@@ -608,13 +639,20 @@
     far = [mask for mask in near if mask > 1]
     reached, _ = lax.optimization_barrier(([near[mask] for mask in far], core))
     others = [lax.ppermute(value, "clip", xor_pairs(clip_total, 1)) for value in reached]
-    work_of = [[near[0], near[1]], reached, others]
-    rounds = [("clip", masks) for masks in rounds_of(clip_total)] + [("sess", masks) for masks in rounds_of(sess_total)]
+    steps = own // block
+    early_steps = (steps + 1) // 2 if steps > 1 else 0
+    middle = reached + others if early_steps else reached
+    work_of = [
+        ([near[0], near[1]], (2,) * steps),
+        (middle, (len(middle),) * early_steps + (len(reached),) * (steps - early_steps)),
+        (others, (0,) * early_steps + (len(others),) * (steps - early_steps)),
+    ]
+    rounds = [("sess", masks) for masks in rounds_of(sess_total)] + [("clip", masks) for masks in rounds_of(clip_total)]
     held = ()
     for step, (axis, masks) in enumerate(rounds):
         got = [core] + [lax.ppermute(core, axis, xor_pairs(lax.axis_size(axis), mask)) for mask in masks]
         if step < len(work_of):
-            held = owned_rows(work_of[step], held, step == len(work_of) - 1)
+            held = owned_rows(*work_of[step], held, step == len(work_of) - 1)
             got, held = lax.optimization_barrier((got, held))
         if step < len(rounds) - 1:
             core = pl.pallas_call(

time: 57.7 us -> 56.2 us (0.974)
  Pallas kernels: 29.2 us -> 27.5 us
  waiting for transfers between devices: 11 us -> 11.6 us
    pallas_call x1, Pallas kernels: 5.97 us -> 4.1 us  [per_device(): pl.pallas_call(core_forward_kernel, out_shape=(jax.ShapeDtypeStruct((rows...]
  transfers between devices with their start and end apart: 11 -> 11, of which waited for: 4 -> 5; matrix products, arithmetic and copies ran while one was open for 0% -> 0% of each run, Pallas kernels for 36% -> 37%
where the time goes in v8:
time: 56.2 us; the launch traced here: 55.9 us
  Pallas kernels  27.5 us (49%)
  starting transfers between devices  15.5 us (28%)
  waiting for transfers between devices  11.6 us (21%)
  between operations  1.38 us (2%)
    pallas_call x3, Pallas kernels, owned_rows(): pl.pallas_call(functools.partial(owned_rows_kernel, scale, len(clips), ea...  9.2 us
    all_to_all x1, starting transfers between devices, per_device(): recv = lax.all_to_all(send, 'sess', split_axis=0, concat_axis=0, tiled=True)  7.28 us
    ppermute x7, starting transfers between devices, per_device(): lax.ppermute(core, axis, xor_pairs(lax.axis_size(axis), mask))  6.59 us
    pallas_call x1, Pallas kernels, per_device(): pl.pallas_call(functools.partial(readout_kernel, scale), in_specs=[smem,...  6.1 us
    all_to_all x1, waiting for transfers between devices, per_device(): recv = lax.all_to_all(send, 'sess', split_axis=0, concat_axis=0, tiled=True)  5.37 us
    pallas_call x1, Pallas kernels, per_device(): pl.pallas_call(functools.partial(core_backward_kernel, channels), out_sha...  4.17 us
    pallas_call x1, Pallas kernels, per_device(): pl.pallas_call(core_forward_kernel, out_shape=(jax.ShapeDtypeStruct((rows...  4.1 us
    ppermute x2, waiting for transfers between devices, per_device(): near[mask] = lax.ppermute(pay, 'clip', xor_pairs(clip_total, mask))  3.24 us
  transfers between devices with their start and end apart: 11, of which 5 were waited for; matrix products, arithmetic and copies ran while one was open for 0% of the time, Pallas kernels for 37%

profile of v8, /device:TPU:0, one launch (start us, length us, event | category | flops | bytes accessed | tf_op | source)
XLA Modules:
  0.0 55.9 jit_solution(4650271289439545927)
XLA Ops:
  0.6 1.8 %select.1 = bf16[8,16,512]{2,1,0:T(8,128)(2,1)} custom-call(s32[1,8]{1,0:T(1,128)} %bitcast.25, bf16[8,2304]{1,0:T(8,128)(2,1)} %bitcast.24, bf16[8,4096]{1,0:T(8,128)(2,1)} %bitcast.23), custom_call_target="tpu_custom_call" | custom-call | tf_op jit(solution)/shard_map/select/pallas_call | solution.py:526
  2.5 7.3 %all-to-all-start = ((bf16[8,16,512]{2,1,0:T(8,128)(2,1)}), bf16[8,16,512]{2,1,0:T(8,128)(2,1)S(1)}, u32[]{:S(2)}, u32[]{:S(2)}) async-start(bf16[8,16,512]{2,1,0:T(8,128)(2,1)} %select.1), calls=%async_computation | async-start | bytes 262144 | tf_op jit(solution)/shard_map/all_to_all | solution.py:534
  10.4 1.3 %prep.1 = (bf16[512,448]{1,0:T(8,128)(2,1)S(1)}, bf16[256,256]{1,0:T(8,128)(2,1)S(1)}, bf16[256,256]{1,0:T(8,128)(2,1)S(1)}, f32[2,64,128]{2,1,0:T(8,128)S(1)}, bf16[512,128]{1,0:T(8,128)(2,1)S(1)}) custom-call(bf16[64,147]{1,0:T(8,128)(2,1)} %weight.1, f32[1,64]{1,0:T(1,128)} %bitcast.28, bf16[64,64]{1,0:T(8,128)(2,1)} %mix.1, f32[1,64]{1,0:T(1,128)} %bitcast.29), custom_call_target="tpu_custom_call" | custom-call | flops 134217728 | bytes 1048576 | tf_op jit(solution)/shard_map/prep/pallas_call | solution.py:539
  11.7 5.4 %all-to-all-done.recv = bf16[8,16,512]{2,1,0:T(8,128)(2,1)S(1)} async-done(((bf16[8,16,512]{2,1,0:T(8,128)(2,1)}), bf16[8,16,512]{2,1,0:T(8,128)(2,1)S(1)}, u32[]{:S(2)}, u32[]{:S(2)}) %all-to-all-start) | async-done | bytes 131104 | tf_op jit(solution)/shard_map/all_to_all | solution.py:534
  17.1 0.0 copy-start
  17.1 0.0 copy-start.1
  17.1 4.1 %core_forward.1 = (bf16[512,640]{1,0:T(8,128)(2,1)S(1)}, f32[8,4096]{1,0:T(8,128)S(1)}, bf16[512,2304]{1,0:T(8,128)(2,1)S(1)}, bf16[512,2304]{1,0:T(8,128)(2,1)S...) custom-call(bf16[8,16,512]{2,1,0:T(8,128)(2,1)S(1)} %all-to-all-done.recv, ...), custom_call_target="tpu_custom_call" | custom-call | flops 1056964608 | bytes 9437184 | tf_op jit(solution)/shard_map/core_forward/pallas_call | solution.py:562
  21.2 1.6 %collective-permute-start.5 = (bf16[512,640]{1,0:T(8,128)(2,1)S(1)}, bf16[512,640]{1,0:T(8,128)(2,1)S(1)}, u32[]{:S(2)}, u32[]{:S(2)}) collective-permute-start(bf16[512,640]{1,0:T(8,128)(2,1)S(1)} %get-tuple-element.61.pay.refs_0_), channel_id=1, source_target_pairs={{0,16},{8,24},{16,0},{24,8},{1,17},{9,25},{17,1},{25,9},{2,18},{10... | collective-permute-start | bytes 1966088 | tf_op jit(solution)/shard_map/ppermute | solution.py:584
  22.8 0.0 collective-permute-start.1
  22.8 0.0 copy-done
  22.8 0.0 copy-done.1
  22.8 6.1 %readout.1 = (bf16[512,576]{1,0:T(8,128)(2,1)S(1)}, f32[8,128]{1,0:T(8,128)S(1)}, bf16[576,1024]{1,0:T(8,128)(2,1)S(1)}, bf16[64,1024]{1,0:T(8,128)(2,1)S(1)}) custom-call(s32[1]{0:T(128)} %bitcast.3.where, s32[1]{0:T(128)S(6)} %copy.19.count, f32[8,4096]{1,0:T(8,128)S(1)} %get-tuple-element.60.target, bf16[512,640]{1,0:T(8,128)(2,1)S(1)} %get-tuple-element.61.pay.refs_0_, ...), custom_call_target="tpu_custom_call" | custom-call | flops 4831838208 | bytes 4718592 | tf_op jit(solution)/shard_map/readout/pallas_call | solution.py:588
  28.9 4.2 %core_backward.1.refs_0_ = f32[128,128]{1,0:T(8,128)S(1)} custom-call(bf16[512,576]{1,0:T(8,128)(2,1)S(1)} %get-tuple-element.63.pooled_grad, f32[8,128]{1,0:T(8,128)S(1)} %get-tuple-element.64.loss, bf16[512,2304]{1,0:T(8,128)(2,1)S(1)} %get-tuple-element.65.act1, bf16[512,2304]{1,0:T(8,128)(2,1)S(1)} %get-tuple-element.66.slope1, ...), custom_call_target="tpu_custom_call" | custom-call | flops 4831838208 | bytes 9437184 | tf_op jit(solution)/shard_map/core_backward/pallas_call | solution.py:604
  33.1 3.2 %collective-permute-done.5.refs_0_ = bf16[512,640]{1,0:T(8,128)(2,1)S(1)} collective-permute-done((bf16[512,640]{1,0:T(8,128)(2,1)S(1)}, bf16[512,640]{1,0:T(8,128)(2,1)S(1)}, u32[]{:S(2)}, u32[]{:S(2)}) %collective-permute-start.5) | collective-permute-done | bytes 655392 | tf_op jit(solution)/shard_map/ppermute | solution.py:584
  36.3 0.0 collective-permute-start.6
  36.3 0.2 collective-permute-start
  36.5 0.0 collective-permute-done.1.refs_1_
  36.5 3.3 %owned_rows.3.refs_5_ = f32[648,1024]{1,0:T(8,128)S(1)} custom-call(s32[1]{0:T(128)} %bitcast.3.where, s32[1]{0:T(128)S(6)} %copy.19.count, bf16[512,640]{1,0:T(8,128)(2,1)S(1)} %get-tuple-element.61.pay.refs_0_, bf16[512,640]{1,0:T(8,128)(2,1)S(1)} %collective-permute-done.1.refs_1_, bf16[64,1024]{1,0:T(8,128)(2,1)S(1)} %get-tuple-element.70.refs_2_.refs_1_, ...), custom_call_target="tpu_custom_call" | custom-call | flops 2415919104 | bytes 2359296 | tf_op jit(solution)/shard_map/owned_rows/pallas_call | solution.py:616
  39.9 1.0 %collective-permute-done.refs_1_ = f32[128,128]{1,0:T(8,128)S(1)} collective-permute-done((f32[128,128]{1,0:T(8,128)S(1)}, f32[128,128]{1,0:T(8,128)S(1)}, u32[]{:S(2)}, u32[]{:S(2)}) %collective-permute-start) | collective-permute-done | bytes 65568 | tf_op jit(solution)/shard_map/ppermute | solution.py:653
  40.8 0.9 %collective-permute-start.4 = (f32[128,128]{1,0:T(8,128)S(1)}, f32[128,128]{1,0:T(8,128)S(1)}, u32[]{:S(2)}, u32[]{:S(2)}) collective-permute-start(f32[128,128]{1,0:T(8,128)S(1)} %add.2.refs_0_), channel_id=1, source_target_pairs={{0,6},{1,7},{2,4},{3,5},{4,2},{5,3},{6,0},{7,1},{8,14},{9,15},{10,... | collective-permute-start | bytes 196616 | tf_op jit(solution)/shard_map/ppermute | solution.py:653
  41.8 1.0 %collective-permute-start.3 = (f32[128,128]{1,0:T(8,128)S(1)}, f32[128,128]{1,0:T(8,128)S(1)}, u32[]{:S(2)}, u32[]{:S(2)}) collective-permute-start(f32[128,128]{1,0:T(8,128)S(1)} %add.2.refs_0_), channel_id=1, source_target_pairs={{0,4},{1,5},{2,6},{3,7},{4,0},{5,1},{6,2},{7,3},{8,12},{9,13},{10,... | collective-permute-start | bytes 196616 | tf_op jit(solution)/shard_map/ppermute | solution.py:653
  42.8 2.5 %collective-permute-start.2 = (f32[128,128]{1,0:T(8,128)S(1)}, f32[128,128]{1,0:T(8,128)S(1)}, u32[]{:S(2)}, u32[]{:S(2)}) collective-permute-start(f32[128,128]{1,0:T(8,128)S(1)} %add.2.refs_0_), channel_id=1, source_target_pairs={{0,2},{1,3},{2,0},{3,1},{4,6},{5,7},{6,4},{7,5},{8,10},{9,11},{10,... | collective-permute-start | bytes 196616 | tf_op jit(solution)/shard_map/ppermute | solution.py:653
  45.3 0.0 collective-permute-done.6.refs_1_.refs_0_
  45.3 2.9 %owned_rows.4.refs_4_ = f32[648,1024]{1,0:T(8,128)S(1)} custom-call(s32[1]{0:T(128)} %bitcast.3.where, s32[1]{0:T(128)S(6)} %copy.19.count, bf16[512,640]{1,0:T(8,128)(2,1)S(1)} %collective-permute-done.5.refs_0_, bf16[512,640]{1,0:T(8,128)(2,1)S(1)} %collective-permute-done.6.refs_1_.refs_0_, bf16[64,1024]{1,0:T(8,128)(2,1)S(1)} %get-tuple-element.70.refs_2_.refs_1_, ...), custom_call_target="tpu_custom_call" | custom-call | flops 2415919104 | bytes 2359296 | tf_op jit(solution)/shard_map/owned_rows/pallas_call | solution.py:616
  48.2 0.0 collective-permute-done.4.refs_3_
  48.2 1.0 %collective-permute-done.3.refs_2_ = f32[128,128]{1,0:T(8,128)S(1)} collective-permute-done((f32[128,128]{1,0:T(8,128)S(1)}, f32[128,128]{1,0:T(8,128)S(1)}, u32[]{:S(2)}, u32[]{:S(2)}) %collective-permute-start.3) | collective-permute-done | bytes 65568 | tf_op jit(solution)/shard_map/ppermute | solution.py:653
  49.3 0.0 collective-permute-done.2.refs_1_
  49.3 1.3 %collective-permute-start.9 = (f32[128,128]{1,0:T(8,128)S(1)}, f32[128,128]{1,0:T(8,128)S(1)}, u32[]{:S(2)}, u32[]{:S(2)}) collective-permute-start(f32[128,128]{1,0:T(8,128)S(1)} %add.3.refs_0_), channel_id=1, source_target_pairs={{0,24},{8,16},{16,8},{24,0},{1,25},{9,17},{17,9},{25,1},{2,26},{10... | collective-permute-start | bytes 196616 | tf_op jit(solution)/shard_map/ppermute | solution.py:653
  50.6 0.5 collective-permute-start.8
  51.1 0.1 collective-permute-start.7
  51.2 3.0 %owned_rows.5 = (f32[576,1024]{1,0:T(8,128)}, f32[64,1024]{1,0:T(8,128)}, f32[1,1024]{1,0:T(1,128)}) custom-call(s32[1]{0:T(128)} %bitcast.3.where, s32[1]{0:T(128)S(6)} %copy.19.count, bf16[512,640]{1,0:T(8,128)(2,1)S(1)} %collective-permute-done.6.refs_1_.refs_0_, bf16[64,1024]{1,0:T(8,128)(2,1)S(1)} %get-tuple-element.70.refs_2_.refs_1_, ...), custom_call_target="tpu_custom_call" | custom-call | flops 1207959552 | bytes 2359296 | tf_op jit(solution)/shard_map/owned_rows/pallas_call | solution.py:616
  54.2 0.0 collective-permute-done.9.refs_3_
  54.2 0.9 %collective-permute-done.8.refs_2_ = f32[128,128]{1,0:T(8,128)S(1)} collective-permute-done((f32[128,128]{1,0:T(8,128)S(1)}, f32[128,128]{1,0:T(8,128)S(1)}, u32[]{:S(2)}, u32[]{:S(2)}) %collective-permute-start.8) | collective-permute-done | bytes 65568 | tf_op jit(solution)/shard_map/ppermute | solution.py:653
  55.2 0.0 collective-permute-done.7.refs_1_
  55.2 0.7 %unpack.1 = (f32[64,147]{1,0:T(8,128)}, f32[1,64]{1,0:T(1,128)}, f32[64,64]{1,0:T(8,128)}, f32[1,64]{1,0:T(1,128)}, f32[1,1]{1,0:T(1,128)}) custom-call(f32[128,128]{1,0:T(8,128)S(1)} %add.3.refs_0_, f32[128,128]{1,0:T(8,128)S(1)} %collective-permute-done.7.refs_1_, f32[128,128]{1,0:T(8,128)S(1)} %collective-permute-done.8.refs_2_, ...), custom_call_target="tpu_custom_call" | custom-call | tf_op jit(solution)/shard_map/unpack/pallas_call | solution.py:666
  (2 shorter events, 0.0 us)
Async XLA Ops:
  2.5 14.6 %all-to-all-start = ((bf16[8,16,512]{2,1,0:T(8,128)(2,1)}), bf16[8,16,512]{2,1,0:T(8,128)(2,1)S(1)}, u32[]{:S(2)}, u32[]{:S(2)}) async-start(bf16[8,16,512]{2,1,0:T(8,128)(2,1)} %select.1), calls=%async_computation | async-start | bytes 262144 | tf_op jit(solution)/shard_map/all_to_all | solution.py:534
  17.1 5.7 %copy-start = (f32[1,4096]{1,0:T(1,128)S(1)}, f32[1,4096]{1,0:T(1,128)}, u32[]{:S(2)}) copy-start(f32[1,4096]{1,0:T(1,128)} %refs_2_.1) | copy-start | bytes 49156
  17.1 5.7 %copy-start.1 = (bf16[1,4096,64]{1,2,0:T(8,128)(2,1)S(1)}, bf16[1,4096,64]{1,2,0:T(8,128)(2,1)}, u32[]{:S(2)}) copy-start(bf16[1,4096,64]{1,2,0:T(8,128)(2,1)} %param.20) | copy-start | bytes 1572868
  21.2 15.1 %collective-permute-start.5 = (bf16[512,640]{1,0:T(8,128)(2,1)S(1)}, bf16[512,640]{1,0:T(8,128)(2,1)S(1)}, u32[]{:S(2)}, u32[]{:S(2)}) collective-permute-start(bf16[512,640]{1,0:T(8,128)(2,1)S(1)} %get-tuple-element.61.pay.refs_0_), channel_id=1, source_target_pairs={{0,16},{8,24},{16,0},{24,8},{1,17},{9,25},{17,1},{25,9},{2,18},{10... | collective-permute-start | bytes 1966088 | tf_op jit(solution)/shard_map/ppermute | solution.py:584
  22.8 13.8 %collective-permute-start.1 = (bf16[512,640]{1,0:T(8,128)(2,1)S(1)}, bf16[512,640]{1,0:T(8,128)(2,1)S(1)}, u32[]{:S(2)}, u32[]{:S(2)}) collective-permute-start(bf16[512,640]{1,0:T(8,128)(2,1)S(1)} %get-tuple-element.61.pay.refs_0_), channel_id=1, source_target_pairs={{0,8},{8,0},{16,24},{24,16},{1,9},{9,1},{17,25},{25,17},{2,10},{10... | collective-permute-start | bytes 1966088 | tf_op jit(solution)/shard_map/ppermute | solution.py:584
  36.3 9.0 %collective-permute-start.6 = (bf16[512,640]{1,0:T(8,128)(2,1)S(1)}, bf16[512,640]{1,0:T(8,128)(2,1)S(1)}, u32[]{:S(2)}, u32[]{:S(2)}) collective-permute-start(bf16[512,640]{1,0:T(8,128)(2,1)S(1)} %collective-permute-done.5.refs_0_), channel_id=1, source_target_pairs={{0,8},{8,0},{16,24},{24,16},{1,9},{9,1},{17,25},{25,17},{2,10},{10... | collective-permute-start | bytes 1966088 | tf_op jit(solution)/shard_map/ppermute | solution.py:641
  36.3 4.5 %collective-permute-start = (f32[128,128]{1,0:T(8,128)S(1)}, f32[128,128]{1,0:T(8,128)S(1)}, u32[]{:S(2)}, u32[]{:S(2)}) collective-permute-start(f32[128,128]{1,0:T(8,128)S(1)} %core_backward.1.refs_0_), channel_id=1, source_target_pairs={{0,1},{1,0},{2,3},{3,2},{4,5},{5,4},{6,7},{7,6},{8,9},{9,8},{10,11... | collective-permute-start | bytes 196616 | tf_op jit(solution)/shard_map/ppermute | solution.py:653
  40.8 7.4 %collective-permute-start.4 = (f32[128,128]{1,0:T(8,128)S(1)}, f32[128,128]{1,0:T(8,128)S(1)}, u32[]{:S(2)}, u32[]{:S(2)}) collective-permute-start(f32[128,128]{1,0:T(8,128)S(1)} %add.2.refs_0_), channel_id=1, source_target_pairs={{0,6},{1,7},{2,4},{3,5},{4,2},{5,3},{6,0},{7,1},{8,14},{9,15},{10,... | collective-permute-start | bytes 196616 | tf_op jit(solution)/shard_map/ppermute | solution.py:653
  41.8 7.5 %collective-permute-start.3 = (f32[128,128]{1,0:T(8,128)S(1)}, f32[128,128]{1,0:T(8,128)S(1)}, u32[]{:S(2)}, u32[]{:S(2)}) collective-permute-start(f32[128,128]{1,0:T(8,128)S(1)} %add.2.refs_0_), channel_id=1, source_target_pairs={{0,4},{1,5},{2,6},{3,7},{4,0},{5,1},{6,2},{7,3},{8,12},{9,13},{10,... | collective-permute-start | bytes 196616 | tf_op jit(solution)/shard_map/ppermute | solution.py:653
  42.8 6.5 %collective-permute-start.2 = (f32[128,128]{1,0:T(8,128)S(1)}, f32[128,128]{1,0:T(8,128)S(1)}, u32[]{:S(2)}, u32[]{:S(2)}) collective-permute-start(f32[128,128]{1,0:T(8,128)S(1)} %add.2.refs_0_), channel_id=1, source_target_pairs={{0,2},{1,3},{2,0},{3,1},{4,6},{5,7},{6,4},{7,5},{8,10},{9,11},{10,... | collective-permute-start | bytes 196616 | tf_op jit(solution)/shard_map/ppermute | solution.py:653
  49.3 4.9 %collective-permute-start.9 = (f32[128,128]{1,0:T(8,128)S(1)}, f32[128,128]{1,0:T(8,128)S(1)}, u32[]{:S(2)}, u32[]{:S(2)}) collective-permute-start(f32[128,128]{1,0:T(8,128)S(1)} %add.3.refs_0_), channel_id=1, source_target_pairs={{0,24},{8,16},{16,8},{24,0},{1,25},{9,17},{17,9},{25,1},{2,26},{10... | collective-permute-start | bytes 196616 | tf_op jit(solution)/shard_map/ppermute | solution.py:653
  50.6 4.6 %collective-permute-start.8 = (f32[128,128]{1,0:T(8,128)S(1)}, f32[128,128]{1,0:T(8,128)S(1)}, u32[]{:S(2)}, u32[]{:S(2)}) collective-permute-start(f32[128,128]{1,0:T(8,128)S(1)} %add.3.refs_0_), channel_id=1, source_target_pairs={{0,16},{8,24},{16,0},{24,8},{1,17},{9,25},{17,1},{25,9},{2,18},{10... | collective-permute-start | bytes 196616 | tf_op jit(solution)/shard_map/ppermute | solution.py:653
  51.1 4.1 %collective-permute-start.7 = (f32[128,128]{1,0:T(8,128)S(1)}, f32[128,128]{1,0:T(8,128)S(1)}, u32[]{:S(2)}, u32[]{:S(2)}) collective-permute-start(f32[128,128]{1,0:T(8,128)S(1)} %add.3.refs_0_), channel_id=1, source_target_pairs={{0,8},{8,0},{16,24},{24,16},{1,9},{9,1},{17,25},{25,17},{2,10},{10... | collective-permute-start | bytes 196616 | tf_op jit(solution)/shard_map/ppermute | solution.py:653

commit v9 on v6

--- a/solution.py
+++ b/solution.py
@@ -118,9 +118,16 @@
     feats,
     sems,
 ):
-    copies = []
-    for k, r in enumerate(range(0, mask.shape[0], SEG)):
-        copies.append(pltpu.make_async_copy(mask_in.at[r : r + SEG, :], mask.at[r : r + SEG, :], sems.at[k]))
+    copy_count = mask.shape[0] // SEG
+
+    def mask_copy(k):
+        rows_at = pl.ds(pl.multiple_of(k * SEG, SEG), SEG)
+        return pltpu.make_async_copy(mask_in.at[rows_at, :], mask.at[rows_at, :], sems.at[k])
+
+    @pl.loop(0, copy_count)
+    def _(k):
+        mask_copy(k).start()
+
     frames, _, width = recv.shape
     rows, pix = act1.shape
     channels = bias.shape[1]
@@ -176,8 +183,6 @@
             slope[r : r + channels, at] = e.astype(BF)
 
     for t in range(count + 2):
-        if t < len(copies):
-            copies[t].start()
         if t < count:
             pre[t % 2][...] = dot(wide, xcol[:, t * CHUNK : (t + 1) * CHUNK])
         if 1 <= t <= count:
@@ -201,8 +206,10 @@
         pieces += [pltpu.roll(tile, SEG, 1), tile]
     packed = jnp.concatenate(pieces, axis=0)
     pay[:, p // 4 : p // 4 + half] = jnp.where(iota((rows, half), 1) < SEG, tail, packed).astype(BF)
-    for copy in copies:
-        copy.wait()
+
+    @pl.loop(0, copy_count)
+    def _(k):
+        mask_copy(k).wait()
 
 
 def drive_terms(projected, target, w, rbias, alive, scale, channels):
@@ -263,8 +270,8 @@
             for f in range(frames):
                 mixed[f * channels : (f + 1) * channels, at] = (grad[f : f + 1] * w).astype(BF)
         last = t - 2
-        if last >= 0 and (last % 2 == 0 or last == steps - 1):
-            low = (last - 1 if last > 0 and last % 2 == 0 else last) * block
+        if last >= 0 and (last % 4 == 3 or last == steps - 1):
+            low = last // 4 * 4 * block
             at = slice(low, (last + 1) * block)
             part = dot(mask[:, at], mixed[:, at], NT)
             acc[...] = acc[...] + part if begun else part

time: 57.7 us -> 55.9 us (0.969)
  Pallas kernels: 29.2 us -> 27.4 us
    pallas_call x1, Pallas kernels: 5.97 us -> 4.1 us  [per_device(): pl.pallas_call(core_forward_kernel, out_shape=(jax.ShapeDtypeStruct((rows...]
  transfers between devices with their start and end apart: 11 -> 11, of which waited for: 4 -> 4; matrix products, arithmetic and copies ran while one was open for 0% -> 0% of each run, Pallas kernels for 36% -> 37%
where the time goes in v9:
time: 55.9 us; the launch traced here: 55.5 us
  Pallas kernels  27.4 us (49%)
  starting transfers between devices  15.7 us (28%)
  waiting for transfers between devices  11 us (20%)
  between operations  1.4 us (3%)
    pallas_call x3, Pallas kernels, owned_rows(): pl.pallas_call(functools.partial(owned_rows_kernel, scale, len(clips), ow...  9.06 us
    all_to_all x1, starting transfers between devices, per_device(): recv = lax.all_to_all(send, 'sess', split_axis=0, concat_axis=0, tiled=True)  7.28 us
    ppermute x7, starting transfers between devices, per_device(): lax.ppermute(core, axis, xor_pairs(lax.axis_size(axis), mask))  6.87 us
    pallas_call x1, Pallas kernels, per_device(): pl.pallas_call(functools.partial(readout_kernel, scale), in_specs=[smem,...  6.14 us
    all_to_all x1, waiting for transfers between devices, per_device(): recv = lax.all_to_all(send, 'sess', split_axis=0, concat_axis=0, tiled=True)  5.37 us
    pallas_call x1, Pallas kernels, per_device(): pl.pallas_call(functools.partial(core_backward_kernel, channels), out_sha...  4.17 us
    pallas_call x1, Pallas kernels, per_device(): pl.pallas_call(core_forward_kernel, out_shape=(jax.ShapeDtypeStruct((rows...  4.1 us
    ppermute x2, waiting for transfers between devices, per_device(): near[mask] = lax.ppermute(pay, 'clip', xor_pairs(clip_total, mask))  3.2 us
  transfers between devices with their start and end apart: 11, of which 4 were waited for; matrix products, arithmetic and copies ran while one was open for 0% of the time, Pallas kernels for 37%

profile of v9, /device:TPU:0, one launch (start us, length us, event | category | flops | bytes accessed | tf_op | source)
XLA Modules:
  0.0 55.5 jit_solution(16897098751417897601)
XLA Ops:
  0.6 1.8 %select.1 = bf16[8,16,512]{2,1,0:T(8,128)(2,1)} custom-call(s32[1,8]{1,0:T(1,128)} %bitcast.25, bf16[8,2304]{1,0:T(8,128)(2,1)} %bitcast.24, bf16[8,4096]{1,0:T(8,128)(2,1)} %bitcast.23), custom_call_target="tpu_custom_call" | custom-call | tf_op jit(solution)/shard_map/select/pallas_call | solution.py:502
  2.5 7.3 %all-to-all-start = ((bf16[8,16,512]{2,1,0:T(8,128)(2,1)}), bf16[8,16,512]{2,1,0:T(8,128)(2,1)S(1)}, u32[]{:S(2)}, u32[]{:S(2)}) async-start(bf16[8,16,512]{2,1,0:T(8,128)(2,1)} %select.1), calls=%async_computation | async-start | bytes 262144 | tf_op jit(solution)/shard_map/all_to_all | solution.py:510
  10.4 1.3 %prep.1 = (bf16[512,448]{1,0:T(8,128)(2,1)S(1)}, bf16[256,256]{1,0:T(8,128)(2,1)S(1)}, bf16[256,256]{1,0:T(8,128)(2,1)S(1)}, f32[2,64,128]{2,1,0:T(8,128)S(1)}, bf16[512,128]{1,0:T(8,128)(2,1)S(1)}) custom-call(bf16[64,147]{1,0:T(8,128)(2,1)} %weight.1, f32[1,64]{1,0:T(1,128)} %bitcast.28, bf16[64,64]{1,0:T(8,128)(2,1)} %mix.1, f32[1,64]{1,0:T(1,128)} %bitcast.29), custom_call_target="tpu_custom_call" | custom-call | flops 134217728 | bytes 1048576 | tf_op jit(solution)/shard_map/prep/pallas_call | solution.py:515
  11.7 5.4 %all-to-all-done.recv = bf16[8,16,512]{2,1,0:T(8,128)(2,1)S(1)} async-done(((bf16[8,16,512]{2,1,0:T(8,128)(2,1)}), bf16[8,16,512]{2,1,0:T(8,128)(2,1)S(1)}, u32[]{:S(2)}, u32[]{:S(2)}) %all-to-all-start) | async-done | bytes 131104 | tf_op jit(solution)/shard_map/all_to_all | solution.py:510
  17.1 0.0 copy-start
  17.1 0.0 copy-start.1
  17.1 4.1 %core_forward.1 = (bf16[512,640]{1,0:T(8,128)(2,1)S(1)}, f32[8,4096]{1,0:T(8,128)S(1)}, bf16[512,2304]{1,0:T(8,128)(2,1)S(1)}, bf16[512,2304]{1,0:T(8,128)(2,1)S...) custom-call(bf16[8,16,512]{2,1,0:T(8,128)(2,1)S(1)} %all-to-all-done.recv, ...), custom_call_target="tpu_custom_call" | custom-call | flops 1056964608 | bytes 9437184 | tf_op jit(solution)/shard_map/core_forward/pallas_call | solution.py:538
  21.2 1.6 %collective-permute-start.5 = (bf16[512,640]{1,0:T(8,128)(2,1)S(1)}, bf16[512,640]{1,0:T(8,128)(2,1)S(1)}, u32[]{:S(2)}, u32[]{:S(2)}) collective-permute-start(bf16[512,640]{1,0:T(8,128)(2,1)S(1)} %get-tuple-element.61.pay.refs_0_), channel_id=1, source_target_pairs={{0,16},{8,24},{16,0},{24,8},{1,17},{9,25},{17,1},{25,9},{2,18},{10... | collective-permute-start | bytes 1966088 | tf_op jit(solution)/shard_map/ppermute | solution.py:560
  22.8 0.0 collective-permute-start.3
  22.8 0.0 copy-done
  22.8 0.0 copy-done.1
  22.8 6.1 %readout.1 = (bf16[512,576]{1,0:T(8,128)(2,1)S(1)}, f32[8,128]{1,0:T(8,128)S(1)}, bf16[576,1024]{1,0:T(8,128)(2,1)S(1)}, bf16[64,1024]{1,0:T(8,128)(2,1)S(1)}) custom-call(s32[1]{0:T(128)} %bitcast.3.where, s32[1]{0:T(128)S(6)} %copy.19.count, f32[8,4096]{1,0:T(8,128)S(1)} %get-tuple-element.60.target, bf16[512,640]{1,0:T(8,128)(2,1)S(1)} %get-tuple-element.61.pay.refs_0_, ...), custom_call_target="tpu_custom_call" | custom-call | flops 4831838208 | bytes 4718592 | tf_op jit(solution)/shard_map/readout/pallas_call | solution.py:564
  29.0 4.2 %core_backward.1.refs_0_ = f32[128,128]{1,0:T(8,128)S(1)} custom-call(bf16[512,576]{1,0:T(8,128)(2,1)S(1)} %get-tuple-element.63.pooled_grad, f32[8,128]{1,0:T(8,128)S(1)} %get-tuple-element.64.loss, bf16[512,2304]{1,0:T(8,128)(2,1)S(1)} %get-tuple-element.65.act1, bf16[512,2304]{1,0:T(8,128)(2,1)S(1)} %get-tuple-element.66.slope1, ...), custom_call_target="tpu_custom_call" | custom-call | flops 4831838208 | bytes 9437184 | tf_op jit(solution)/shard_map/core_backward/pallas_call | solution.py:580
  33.1 3.2 %collective-permute-done.5.refs_0_ = bf16[512,640]{1,0:T(8,128)(2,1)S(1)} collective-permute-done((bf16[512,640]{1,0:T(8,128)(2,1)S(1)}, bf16[512,640]{1,0:T(8,128)(2,1)S(1)}, u32[]{:S(2)}, u32[]{:S(2)}) %collective-permute-start.5) | collective-permute-done | bytes 655392 | tf_op jit(solution)/shard_map/ppermute | solution.py:560
  36.3 0.0 collective-permute-start.9
  36.3 1.6 %collective-permute-start.2 = (f32[128,128]{1,0:T(8,128)S(1)}, f32[128,128]{1,0:T(8,128)S(1)}, u32[]{:S(2)}, u32[]{:S(2)}) collective-permute-start(f32[128,128]{1,0:T(8,128)S(1)} %core_backward.1.refs_0_), channel_id=1, source_target_pairs={{0,24},{8,16},{16,8},{24,0},{1,25},{9,17},{17,9},{25,1},{2,26},{10... | collective-permute-start | bytes 196616 | tf_op jit(solution)/shard_map/ppermute | solution.py:622
  38.0 0.5 collective-permute-start.1
  38.5 0.0 collective-permute-start
  38.5 0.0 collective-permute-done.3.refs_1_
  38.5 3.3 %owned_rows.3.refs_4_ = f32[648,1024]{1,0:T(8,128)S(1)} custom-call(s32[1]{0:T(128)} %bitcast.3.where, s32[1]{0:T(128)S(6)} %copy.19.count, bf16[512,640]{1,0:T(8,128)(2,1)S(1)} %get-tuple-element.61.pay.refs_0_, bf16[512,640]{1,0:T(8,128)(2,1)S(1)} %collective-permute-done.3.refs_1_, bf16[64,1024]{1,0:T(8,128)(2,1)S(1)} %get-tuple-element.70.refs_2_.refs_1_, ...), custom_call_target="tpu_custom_call" | custom-call | flops 2415919104 | bytes 2359296 | tf_op jit(solution)/shard_map/owned_rows/pallas_call | solution.py:592
  41.8 0.0 collective-permute-done.2.refs_3_
  41.8 0.5 collective-permute-done.1.refs_2_
  42.2 0.0 collective-permute-done.refs_1_
  42.3 0.3 collective-permute-start.4
  42.5 2.1 %owned_rows.4.refs_4_ = f32[648,1024]{1,0:T(8,128)S(1)} custom-call(s32[1]{0:T(128)} %bitcast.3.where, s32[1]{0:T(128)S(6)} %copy.19.count, bf16[512,640]{1,0:T(8,128)(2,1)S(1)} %collective-permute-done.5.refs_0_, bf16[64,1024]{1,0:T(8,128)(2,1)S(1)} %get-tuple-element.70.refs_2_.refs_1_, f32[1,4096]{1,0:T(1,128)S(1)} %copy-done, ...), custom_call_target="tpu_custom_call" | custom-call | flops 1207959552 | bytes 2359296 | tf_op jit(solution)/shard_map/owned_rows/pallas_call | solution.py:592
  44.6 2.0 %collective-permute-done.4.refs_1_ = f32[128,128]{1,0:T(8,128)S(1)} collective-permute-done((f32[128,128]{1,0:T(8,128)S(1)}, f32[128,128]{1,0:T(8,128)S(1)}, u32[]{:S(2)}, u32[]{:S(2)}) %collective-permute-start.4) | collective-permute-done | bytes 65568 | tf_op jit(solution)/shard_map/ppermute | solution.py:622
  46.6 0.9 %collective-permute-start.8 = (f32[128,128]{1,0:T(8,128)S(1)}, f32[128,128]{1,0:T(8,128)S(1)}, u32[]{:S(2)}, u32[]{:S(2)}) collective-permute-start(f32[128,128]{1,0:T(8,128)S(1)} %add.3.refs_0_), channel_id=1, source_target_pairs={{0,6},{1,7},{2,4},{3,5},{4,2},{5,3},{6,0},{7,1},{8,14},{9,15},{10,... | collective-permute-start | bytes 196616 | tf_op jit(solution)/shard_map/ppermute | solution.py:622
  47.5 0.5 collective-permute-start.7
  48.1 3.0 %collective-permute-start.6 = (f32[128,128]{1,0:T(8,128)S(1)}, f32[128,128]{1,0:T(8,128)S(1)}, u32[]{:S(2)}, u32[]{:S(2)}) collective-permute-start(f32[128,128]{1,0:T(8,128)S(1)} %add.3.refs_0_), channel_id=1, source_target_pairs={{0,2},{1,3},{2,0},{3,1},{4,6},{5,7},{6,4},{7,5},{8,10},{9,11},{10,... | collective-permute-start | bytes 196616 | tf_op jit(solution)/shard_map/ppermute | solution.py:622
  51.1 0.0 collective-permute-done.9.refs_0_
  51.1 3.7 %owned_rows.5 = (f32[576,1024]{1,0:T(8,128)}, f32[64,1024]{1,0:T(8,128)}, f32[1,1024]{1,0:T(1,128)}) custom-call(s32[1]{0:T(128)} %bitcast.3.where, s32[1]{0:T(128)S(6)} %copy.19.count, bf16[512,640]{1,0:T(8,128)(2,1)S(1)} %collective-permute-done.9.refs_0_, bf16[64,1024]{1,0:T(8,128)(2,1)S(1)} %get-tuple-element.70.refs_2_.refs_1_, f32[1,4096]{1,0:T(1,128)S(1)} %copy-done, ...), custom_call_target="tpu_custom_call" | custom-call | flops 1207959552 | bytes 2359296 | tf_op jit(solution)/shard_map/owned_rows/pallas_call | solution.py:592
  54.8 0.0 collective-permute-done.8.refs_3_
  54.8 0.0 collective-permute-done.7.refs_2_
  54.8 0.0 collective-permute-done.6.refs_1_
  54.8 0.7 %unpack.1 = (f32[64,147]{1,0:T(8,128)}, f32[1,64]{1,0:T(1,128)}, f32[64,64]{1,0:T(8,128)}, f32[1,64]{1,0:T(1,128)}, f32[1,1]{1,0:T(1,128)}) custom-call(f32[128,128]{1,0:T(8,128)S(1)} %add.3.refs_0_, f32[128,128]{1,0:T(8,128)S(1)} %collective-permute-done.6.refs_1_, f32[128,128]{1,0:T(8,128)S(1)} %collective-permute-done.7.refs_2_, ...), custom_call_target="tpu_custom_call" | custom-call | tf_op jit(solution)/shard_map/unpack/pallas_call | solution.py:635
  (2 shorter events, 0.0 us)
Async XLA Ops:
  2.5 14.6 %all-to-all-start = ((bf16[8,16,512]{2,1,0:T(8,128)(2,1)}), bf16[8,16,512]{2,1,0:T(8,128)(2,1)S(1)}, u32[]{:S(2)}, u32[]{:S(2)}) async-start(bf16[8,16,512]{2,1,0:T(8,128)(2,1)} %select.1), calls=%async_computation | async-start | bytes 262144 | tf_op jit(solution)/shard_map/all_to_all | solution.py:510
  17.1 5.7 %copy-start = (f32[1,4096]{1,0:T(1,128)S(1)}, f32[1,4096]{1,0:T(1,128)}, u32[]{:S(2)}) copy-start(f32[1,4096]{1,0:T(1,128)} %refs_2_.3) | copy-start | bytes 49156
  17.1 5.7 %copy-start.1 = (bf16[1,4096,64]{1,2,0:T(8,128)(2,1)S(1)}, bf16[1,4096,64]{1,2,0:T(8,128)(2,1)}, u32[]{:S(2)}) copy-start(bf16[1,4096,64]{1,2,0:T(8,128)(2,1)} %param.20) | copy-start | bytes 1572868
  21.2 15.1 %collective-permute-start.5 = (bf16[512,640]{1,0:T(8,128)(2,1)S(1)}, bf16[512,640]{1,0:T(8,128)(2,1)S(1)}, u32[]{:S(2)}, u32[]{:S(2)}) collective-permute-start(bf16[512,640]{1,0:T(8,128)(2,1)S(1)} %get-tuple-element.61.pay.refs_0_), channel_id=1, source_target_pairs={{0,16},{8,24},{16,0},{24,8},{1,17},{9,25},{17,1},{25,9},{2,18},{10... | collective-permute-start | bytes 1966088 | tf_op jit(solution)/shard_map/ppermute | solution.py:560
  22.8 15.7 %collective-permute-start.3 = (bf16[512,640]{1,0:T(8,128)(2,1)S(1)}, bf16[512,640]{1,0:T(8,128)(2,1)S(1)}, u32[]{:S(2)}, u32[]{:S(2)}) collective-permute-start(bf16[512,640]{1,0:T(8,128)(2,1)S(1)} %get-tuple-element.61.pay.refs_0_), channel_id=1, source_target_pairs={{0,8},{8,0},{16,24},{24,16},{1,9},{9,1},{17,25},{25,17},{2,10},{10... | collective-permute-start | bytes 1966088 | tf_op jit(solution)/shard_map/ppermute | solution.py:560
  36.3 14.7 %collective-permute-start.9 = (bf16[512,640]{1,0:T(8,128)(2,1)S(1)}, bf16[512,640]{1,0:T(8,128)(2,1)S(1)}, u32[]{:S(2)}, u32[]{:S(2)}) collective-permute-start(bf16[512,640]{1,0:T(8,128)(2,1)S(1)} %collective-permute-done.5.refs_0_), channel_id=1, source_target_pairs={{0,8},{8,0},{16,24},{24,16},{1,9},{9,1},{17,25},{25,17},{2,10},{10... | collective-permute-start | bytes 1966088 | tf_op jit(solution)/shard_map/ppermute | solution.py:617
  36.3 5.4 %collective-permute-start.2 = (f32[128,128]{1,0:T(8,128)S(1)}, f32[128,128]{1,0:T(8,128)S(1)}, u32[]{:S(2)}, u32[]{:S(2)}) collective-permute-start(f32[128,128]{1,0:T(8,128)S(1)} %core_backward.1.refs_0_), channel_id=1, source_target_pairs={{0,24},{8,16},{16,8},{24,0},{1,25},{9,17},{17,9},{25,1},{2,26},{10... | collective-permute-start | bytes 196616 | tf_op jit(solution)/shard_map/ppermute | solution.py:622
  38.0 4.3 %collective-permute-start.1 = (f32[128,128]{1,0:T(8,128)S(1)}, f32[128,128]{1,0:T(8,128)S(1)}, u32[]{:S(2)}, u32[]{:S(2)}) collective-permute-start(f32[128,128]{1,0:T(8,128)S(1)} %core_backward.1.refs_0_), channel_id=1, source_target_pairs={{0,16},{8,24},{16,0},{24,8},{1,17},{9,25},{17,1},{25,9},{2,18},{10... | collective-permute-start | bytes 196616 | tf_op jit(solution)/shard_map/ppermute | solution.py:622
  38.5 3.8 %collective-permute-start = (f32[128,128]{1,0:T(8,128)S(1)}, f32[128,128]{1,0:T(8,128)S(1)}, u32[]{:S(2)}, u32[]{:S(2)}) collective-permute-start(f32[128,128]{1,0:T(8,128)S(1)} %core_backward.1.refs_0_), channel_id=1, source_target_pairs={{0,8},{8,0},{16,24},{24,16},{1,9},{9,1},{17,25},{25,17},{2,10},{10... | collective-permute-start | bytes 196616 | tf_op jit(solution)/shard_map/ppermute | solution.py:622
  42.3 4.3 %collective-permute-start.4 = (f32[128,128]{1,0:T(8,128)S(1)}, f32[128,128]{1,0:T(8,128)S(1)}, u32[]{:S(2)}, u32[]{:S(2)}) collective-permute-start(f32[128,128]{1,0:T(8,128)S(1)} %add.2.refs_0_), channel_id=1, source_target_pairs={{0,1},{1,0},{2,3},{3,2},{4,5},{5,4},{6,7},{7,6},{8,9},{9,8},{10,11... | collective-permute-start | bytes 196616 | tf_op jit(solution)/shard_map/ppermute | solution.py:622
  46.6 8.2 %collective-permute-start.8 = (f32[128,128]{1,0:T(8,128)S(1)}, f32[128,128]{1,0:T(8,128)S(1)}, u32[]{:S(2)}, u32[]{:S(2)}) collective-permute-start(f32[128,128]{1,0:T(8,128)S(1)} %add.3.refs_0_), channel_id=1, source_target_pairs={{0,6},{1,7},{2,4},{3,5},{4,2},{5,3},{6,0},{7,1},{8,14},{9,15},{10,... | collective-permute-start | bytes 196616 | tf_op jit(solution)/shard_map/ppermute | solution.py:622
  47.5 7.2 %collective-permute-start.7 = (f32[128,128]{1,0:T(8,128)S(1)}, f32[128,128]{1,0:T(8,128)S(1)}, u32[]{:S(2)}, u32[]{:S(2)}) collective-permute-start(f32[128,128]{1,0:T(8,128)S(1)} %add.3.refs_0_), channel_id=1, source_target_pairs={{0,4},{1,5},{2,6},{3,7},{4,0},{5,1},{6,2},{7,3},{8,12},{9,13},{10,... | collective-permute-start | bytes 196616 | tf_op jit(solution)/shard_map/ppermute | solution.py:622
  48.1 6.7 %collective-permute-start.6 = (f32[128,128]{1,0:T(8,128)S(1)}, f32[128,128]{1,0:T(8,128)S(1)}, u32[]{:S(2)}, u32[]{:S(2)}) collective-permute-start(f32[128,128]{1,0:T(8,128)S(1)} %add.3.refs_0_), channel_id=1, source_target_pairs={{0,2},{1,3},{2,0},{3,1},{4,6},{5,7},{6,4},{7,5},{8,10},{9,11},{10,... | collective-permute-start | bytes 196616 | tf_op jit(solution)/shard_map/ppermute | solution.py:622
